TPU v7x, 32 devices: a whole 2x2x4 slice. The times are simulated.
32 devices in a mesh: groups: 2 (over y), grow: 4 (over z), cross: 2 (over x), side: 2 (over core).
Axes of the slice: x: 2, y: 2, z: 4, core: 2. Of those that a mesh axis runs over, the one named last changes fastest.
Arguments:
- phase_field: float32 [32, 64, 1024], P(('groups', 'grow'), 'cross', 'side'), parts along dimension 0, may hold values from -1.1 to 1.1
- solute_field: float32 [32, 64, 1024], P(('groups', 'grow'), 'cross', 'side'), parts along dimension 0, may hold values from -1 to 0.2
- shift_step: int32 [2], P('groups'), parts along dimension 0, may hold values from 0 to 1
- inflow_seed: int32 [128, 1024], P(('groups', 'cross'), 'side'), parts along dimension 0, may hold values from 0 to 1023
Outputs:
- phase_out: float32 [32, 64, 1024], P(('groups', 'grow'), 'cross', 'side'), parts along dimension 0
- solute_out: float32 [32, 64, 1024], P(('groups', 'grow'), 'cross', 'side'), parts along dimension 0
There are 2 independent parts, one for each index of `groups`. A program takes and returns all parts, laid end to end along the dimension named above; each array names one. Nothing has to cross between parts.
Inputs may be any that keep to these rules, and one draw needn't show every extreme that they name: `shift_step`: the frame moves once, between two of the 3 steps.
All inputs are finite; a program needn't handle non-finite values.
Results may differ from a plain program's by a relative error of at most 0.00002.
Values sent between devices are 32-bit elements; how exact they have to be, the bound alone decides.
No kernel may reach another device: no remote copies, remote signals or barrier semaphores. Data moves between devices by JAX's collectives and lax.ppermute only.
A program may use at most 64 MiB of HBM per device.

v0:
```python
import jax
import jax.numpy as jnp
from jax import lax
from jax.sharding import PartitionSpec as P

ITERS = 3


partition = 0.15
coupling = 2.0
diffusion = 2.0
spacing_sq = 0.64
time_step = 0.025
gradient_scale = 1.2
drift_rate = 0.01
seed_levels = 1024.0


def extended(shard, sides, width, wrap):
    for axis, dim in sides:
        size, length = (lax.axis_size(axis), shard.shape[dim])
        up = [(i, (i + 1) % size) for i in range(size if wrap else size - 1)]
        down = [(j, i) for i, j in up]
        last = lax.slice_in_dim(shard, length - width, length, axis=dim)
        first = lax.slice_in_dim(shard, 0, width, axis=dim)
        before = lax.ppermute(last, axis, up)
        after = lax.ppermute(first, axis, down)
        shard = jnp.concatenate([before, shard, after], axis=dim)
    return shard


def passed_along(shard, axis, by):
    size = lax.axis_size(axis)
    pairs = [(i, i + by) for i in range(size) if 0 <= i + by < size]
    return lax.ppermute(shard, axis, pairs)


def neighbours(side_pad, growth_pad):
    return [
        growth_pad[:, :-2],
        growth_pad[:, 2:],
        side_pad[:, :, :-2, 1:-1],
        side_pad[:, :, 2:, 1:-1],
        side_pad[:, :, 1:-1, :-2],
        side_pad[:, :, 1:-1, 2:],
    ]


def advance(center, nearby, temper):
    phases = center[0]
    solutes = center[1]
    laplace = -6.0 * phases
    for entry in nearby:
        laplace = laplace + entry[0]
    laplace = laplace / spacing_sq
    slowing = 1.0 - (1.0 - partition) * temper
    driving = (
        laplace
        + phases
        - phases * phases * phases
        - coupling * (1.0 - phases * phases) ** 2 * (solutes + temper)
    )
    growth_rate = driving / slowing
    clipped = jnp.clip(phases, -1.0, 1.0)
    mobile = 0.5 * (1.0 - clipped)
    current = jnp.zeros_like(phases)
    for entry in nearby:
        near_mobile = 0.5 * (1.0 - jnp.clip(entry[0], -1.0, 1.0))
        current = current + 0.5 * (mobile + near_mobile) * (entry[1] - solutes)
    current = current * (diffusion / spacing_sq)
    weight = 0.5 * (1.0 + partition - (1.0 - partition) * clipped)
    solute_rate = (current + 0.5 * (1.0 + (1.0 - partition) * solutes) * growth_rate) / weight
    return jnp.stack([phases + time_step * growth_rate, solutes + time_step * solute_rate])


def mirror_ends(padded, at_bottom, at_top):
    lower_row = jnp.where(at_bottom, padded[:, 1:2], padded[:, 0:1])
    upper_row = jnp.where(at_top, padded[:, -2:-1], padded[:, -1:])
    return jnp.concatenate([lower_row, padded[:, 1:-1], upper_row], 1)


def cross_pad(fields):
    return extended(fields, (("cross", 2), ("side", 3)), 1, True)


def shards(phase_field, solute_field, shift_step, inflow_seed):
    grow_index = lax.axis_index("grow")
    grow_last = lax.axis_size("grow") - 1
    at_bottom = grow_index == 0
    at_top = grow_index == grow_last
    planes = phase_field.shape[0]
    grid_rows = planes * lax.axis_size("grow")
    frame_step = shift_step[0]
    inflow = inflow_seed.astype(jnp.float32) / seed_levels - 1.0
    top_pair = jnp.stack([jnp.full_like(inflow, -1.0), inflow])[:, None]
    fields = jnp.stack([phase_field, solute_field])
    heights = (grow_index * planes + jnp.arange(planes)).astype(jnp.float32)[:, None, None]
    for step_index in range(ITERS):
        window = extended(fields, (("grow", 1),), 1, False)
        window = mirror_ends(window, at_bottom, at_top)
        side_pad = cross_pad(fields)
        nearby = neighbours(side_pad, window)
        shifts = (frame_step < step_index).astype(jnp.float32)
        temper = (
            gradient_scale * ((heights + shifts + 0.5) / grid_rows - 0.5) - drift_rate * step_index
        )
        fields = advance(side_pad[:, :, 1:-1, 1:-1], nearby, temper)
        if step_index < ITERS - 1:
            handed = passed_along(fields[:, :1], "grow", -1)
            handed = jnp.where(at_top, top_pair, handed)
            shifted = jnp.concatenate([fields[:, 1:], handed], 1)
            fields = jnp.where(frame_step == step_index, shifted, fields)
    return (fields[0], fields[1])


def solution(mesh):
    return jax.shard_map(
        shards,
        mesh=mesh,
        in_specs=(
            P(("groups", "grow"), "cross", "side"),
            P(("groups", "grow"), "cross", "side"),
            P("groups"),
            P(("groups", "cross"), "side"),
        ),
        out_specs=(P(("groups", "grow"), "cross", "side"), P(("groups", "grow"), "cross", "side")),
        check_vma=False,
    )
```

profile of v0, /device:TPU:0, one launch (start us, length us, event | category | flops | bytes accessed | tf_op | source)
XLA Modules:
  0.0 62.9 jit_solution(1464265654475939014)
XLA Ops:
  0.6 0.9 %fusion.95 = f32[2,1,32,512]{3,2,1,0:T(8,128)S(1)} fusion(f32[1,4,32,512]{3,2,1,0:T(8,128)} %bitcast.254, f32[1,4,32,512]{3,2,1,0:T(8,128)} %bitcast.248), kind=kLoop, calls=%fused_computation.192 | loop fusion | flops 32768 | bytes 655360 | tf_op jit(solution)/shard_map/stack | solution.py:96
  1.6 5.0 %collective-permute-start = (f32[2,1,32,512]{3,2,1,0:T(8,128)S(1)}, f32[2,1,32,512]{3,2,1,0:T(8,128)S(1)}, u32[]{:S(2)}, u32[]{:S(2)}) collective-permute-start(f32[2,1,32,512]{3,2,1,0:T(8,128)S(1)} %fusion.95), channel_id=1, source_target_pairs={{0,4},{4,8},{8,12},{1,5},{5,9},{9,13},{2,6},{6,10},{10,14},{3,7},{... | collective-permute-start | bytes 393224 | tf_op jit(solution)/shard_map/ppermute | solution.py:26
  6.6 1.6 %collective-permute-start.2 = (f32[2,4,1,512]{3,2,1,0:T(1,128)S(1)}, f32[2,4,1,512]{3,2,1,0:T(1,128)S(1)}, u32[]{:S(2)}, u32[]{:S(2)}) collective-permute-start(f32[2,4,1,512]{3,2,1,0:T(1,128)S(1)} %get-tuple-element.26), channel_id=1, source_target_pairs={{0,2},{2,0},{1,3},{3,1},{4,6},{6,4},{5,7},{7,5},{8,10},{10,8},{9,1... | collective-permute-start | bytes 49160 | tf_op jit(solution)/shard_map/ppermute | solution.py:26
  8.2 0.5 collective-permute-start.3
  9.4 1.3 %collective-permute-start.1 = (f32[2,1,32,512]{3,2,1,0:T(8,128)S(1)}, f32[2,1,32,512]{3,2,1,0:T(8,128)S(1)}, u32[]{:S(2)}, u32[]{:S(2)}) collective-permute-start(f32[2,1,32,512]{3,2,1,0:T(8,128)S(1)} %get-tuple-element.7), channel_id=1, source_target_pairs={{4,0},{8,4},{12,8},{5,1},{9,5},{13,9},{6,2},{10,6},{14,10},{7,3},{... | collective-permute-start | bytes 393224 | tf_op jit(solution)/shard_map/ppermute | solution.py:27
  10.7 0.0 collective-permute-done.2
  10.7 1.2 %collective-permute-done.3 = f32[2,4,1,512]{3,2,1,0:T(1,128)S(1)} collective-permute-done((f32[2,4,1,512]{3,2,1,0:T(1,128)S(1)}, f32[2,4,1,512]{3,2,1,0:T(1,128)S(1)}, u32[]{:S(2)}, u32[]{:S(2)}) %collective-permute-start.3) | collective-permute-done | bytes 16416 | tf_op jit(solution)/shard_map/ppermute | solution.py:27
  11.9 0.1 pad_maximum_fusion.53
  12.0 0.1 collective-permute-start.4
  12.1 0.5 collective-permute-start.5
  12.6 4.0 %collective-permute-done.1 = f32[2,1,32,512]{3,2,1,0:T(8,128)S(1)} collective-permute-done((f32[2,1,32,512]{3,2,1,0:T(8,128)S(1)}, f32[2,1,32,512]{3,2,1,0:T(8,128)S(1)}, u32[]{:S(2)}, u32[]{:S(2)}) %collective-permute-start.1) | collective-permute-done | bytes 131104 | tf_op jit(solution)/shard_map/ppermute | solution.py:27
  16.7 0.0 collective-permute-done.4
  16.7 0.3 add_bitcast_fusion.1
  17.0 1.0 %add_bitcast_fusion = f32[1,4,32,512]{3,2,1,0:T(8,128)S(1)} fusion(f32[4,32,512]{2,1,0:T(8,128)S(1)} %copy-done, f32[2,4,34,1]{3,2,1,0:T(8,128)S(1)} %collective-permute-done.5, f32[2,4,1,512]{3,2,1,0:T(1,128)S(1)} %collective-permute-done.3, f32[1,4,32,512]{3,2,1,0:T(8,128)S(1)} %bitcast.253, f32[1,4,32,512]{3,2,1,0:T(8,128)S(1)} %bitcast.259, ...), kind=kLoop, calls=%fused_computation.178 | loop fusion | flops 7405568 | bytes 1607840 | tf_op jit(solution)/shard_map/stack | solution.py:73
  18.0 0.0 copy-start.2
  18.0 1.3 %collective-permute-start.6 = (f32[2,1,32,512]{3,2,1,0:T(8,128)S(1)}, f32[2,1,32,512]{3,2,1,0:T(8,128)S(1)}, u32[]{:S(2)}, u32[]{:S(2)}) collective-permute-start(f32[2,1,32,512]{3,2,1,0:T(8,128)S(1)} %fusion.97), channel_id=1, source_target_pairs={{4,0},{8,4},{12,8},{5,1},{9,5},{13,9},{6,2},{10,6},{14,10},{7,3},{... | collective-permute-start | bytes 393224 | tf_op jit(solution)/shard_map/ppermute | solution.py:35
  19.4 5.5 %collective-permute-done.6 = f32[2,1,32,512]{3,2,1,0:T(8,128)S(1)} collective-permute-done((f32[2,1,32,512]{3,2,1,0:T(8,128)S(1)}, f32[2,1,32,512]{3,2,1,0:T(8,128)S(1)}, u32[]{:S(2)}, u32[]{:S(2)}) %collective-permute-start.6) | collective-permute-done | bytes 131104 | tf_op jit(solution)/shard_map/ppermute | solution.py:35
  24.9 0.1 fusion.1
  25.1 3.9 %collective-permute-start.7 = (f32[2,1,32,512]{3,2,1,0:T(8,128)S(1)}, f32[2,1,32,512]{3,2,1,0:T(8,128)S(1)}, u32[]{:S(2)}, u32[]{:S(2)}) collective-permute-start(f32[2,1,32,512]{3,2,1,0:T(8,128)S(1)} %get-tuple-element.22), channel_id=1, source_target_pairs={{0,4},{4,8},{8,12},{1,5},{5,9},{9,13},{2,6},{6,10},{10,14},{3,7},{... | collective-permute-start | bytes 393224 | tf_op jit(solution)/shard_map/ppermute | solution.py:26
  29.0 1.3 %collective-permute-start.8 = (f32[2,1,32,512]{3,2,1,0:T(8,128)S(1)}, f32[2,1,32,512]{3,2,1,0:T(8,128)S(1)}, u32[]{:S(2)}, u32[]{:S(2)}) collective-permute-start(f32[2,1,32,512]{3,2,1,0:T(8,128)S(1)} %get-tuple-element.23), channel_id=1, source_target_pairs={{4,0},{8,4},{12,8},{5,1},{9,5},{13,9},{6,2},{10,6},{14,10},{7,3},{... | collective-permute-start | bytes 393224 | tf_op jit(solution)/shard_map/ppermute | solution.py:27
  30.3 1.6 %collective-permute-start.10 = (f32[2,4,1,512]{3,2,1,0:T(1,128)S(1)}, f32[2,4,1,512]{3,2,1,0:T(1,128)S(1)}, u32[]{:S(2)}, u32[]{:S(2)}) collective-permute-start(f32[2,4,1,512]{3,2,1,0:T(1,128)S(1)} %get-tuple-element.25), channel_id=1, source_target_pairs={{2,0},{0,2},{3,1},{1,3},{6,4},{4,6},{7,5},{5,7},{10,8},{8,10},{11,... | collective-permute-start | bytes 49160 | tf_op jit(solution)/shard_map/ppermute | solution.py:27
  31.9 0.5 collective-permute-start.9
  32.4 1.7 %collective-permute-done.10 = f32[2,4,1,512]{3,2,1,0:T(1,128)S(1)} collective-permute-done((f32[2,4,1,512]{3,2,1,0:T(1,128)S(1)}, f32[2,4,1,512]{3,2,1,0:T(1,128)S(1)}, u32[]{:S(2)}, u32[]{:S(2)}) %collective-permute-start.10) | collective-permute-done | bytes 16416 | tf_op jit(solution)/shard_map/ppermute | solution.py:27
  34.1 1.5 %collective-permute-done.9 = f32[2,4,1,512]{3,2,1,0:T(1,128)S(1)} collective-permute-done((f32[2,4,1,512]{3,2,1,0:T(1,128)S(1)}, f32[2,4,1,512]{3,2,1,0:T(1,128)S(1)}, u32[]{:S(2)}, u32[]{:S(2)}) %collective-permute-start.9) | collective-permute-done | bytes 16416 | tf_op jit(solution)/shard_map/ppermute | solution.py:26
  35.6 0.1 pad_maximum_fusion.49
  35.7 0.1 collective-permute-start.11
  35.8 0.5 collective-permute-start.12
  36.4 0.8 %collective-permute-done.11 = f32[2,4,34,1]{3,2,1,0:T(8,128)S(1)} collective-permute-done((f32[2,4,34,1]{3,2,1,0:T(8,128)S(1)}, f32[2,4,34,1]{3,2,1,0:T(8,128)S(1)}, u32[]{:S(2)}, u32[]{:S(2)}) %collective-permute-start.11) | collective-permute-done | bytes 1120 | tf_op jit(solution)/shard_map/ppermute | solution.py:26
  37.2 0.2 collective-permute-done.12
  37.4 0.3 multiply_add_fusion.3
  37.8 1.0 %multiply_add_fusion.2 = f32[1,4,32,512]{3,2,1,0:T(8,128)S(1)} fusion(f32[2,4,34,1]{3,2,1,0:T(8,128)S(1)} %collective-permute-done.12, f32[2,4,1,512]{3,2,1,0:T(1,128)S(1)} %collective-permute-done.10, f32[2,4,32,512]{3,2,1,0:T(8,128)S(1)} %fusion.1, f32[2,4,1,512]{3,2,1,0:T(1,128)S(1)} %collective-permute-done.9, ...), kind=kLoop, calls=%fused_computation.175 | loop fusion | flops 6619136 | bytes 1934336 | tf_op jit(solution)/shard_map/add | solution.py:73
  38.8 1.3 %collective-permute-start.13 = (f32[2,1,32,512]{3,2,1,0:T(8,128)S(1)}, f32[2,1,32,512]{3,2,1,0:T(8,128)S(1)}, u32[]{:S(2)}, u32[]{:S(2)}) collective-permute-start(f32[2,1,32,512]{3,2,1,0:T(8,128)S(1)} %fusion.96), channel_id=1, source_target_pairs={{4,0},{8,4},{12,8},{5,1},{9,5},{13,9},{6,2},{10,6},{14,10},{7,3},{... | collective-permute-start | bytes 393224 | tf_op jit(solution)/shard_map/ppermute | solution.py:35
  40.2 7.1 %collective-permute-done.13 = f32[2,1,32,512]{3,2,1,0:T(8,128)S(1)} collective-permute-done((f32[2,1,32,512]{3,2,1,0:T(8,128)S(1)}, f32[2,1,32,512]{3,2,1,0:T(8,128)S(1)}, u32[]{:S(2)}, u32[]{:S(2)}) %collective-permute-start.13) | collective-permute-done | bytes 131104 | tf_op jit(solution)/shard_map/ppermute | solution.py:35
  47.3 0.1 fusion
  47.5 0.6 collective-permute-start.16
  48.1 1.5 %collective-permute-start.17 = (f32[2,4,1,512]{3,2,1,0:T(1,128)S(1)}, f32[2,4,1,512]{3,2,1,0:T(1,128)S(1)}, u32[]{:S(2)}, u32[]{:S(2)}) collective-permute-start(f32[2,4,1,512]{3,2,1,0:T(1,128)S(1)} %get-tuple-element.18), channel_id=1, source_target_pairs={{2,0},{0,2},{3,1},{1,3},{6,4},{4,6},{7,5},{5,7},{10,8},{8,10},{11,... | collective-permute-start | bytes 49160 | tf_op jit(solution)/shard_map/ppermute | solution.py:27
  49.6 3.6 %collective-permute-start.14 = (f32[2,1,32,512]{3,2,1,0:T(8,128)S(1)}, f32[2,1,32,512]{3,2,1,0:T(8,128)S(1)}, u32[]{:S(2)}, u32[]{:S(2)}) collective-permute-start(f32[2,1,32,512]{3,2,1,0:T(8,128)S(1)} %get-tuple-element.17), channel_id=1, source_target_pairs={{0,4},{4,8},{8,12},{1,5},{5,9},{9,13},{2,6},{6,10},{10,14},{3,7},{... | collective-permute-start | bytes 393224 | tf_op jit(solution)/shard_map/ppermute | solution.py:26
  53.2 1.3 %collective-permute-start.15 = (f32[2,1,32,512]{3,2,1,0:T(8,128)S(1)}, f32[2,1,32,512]{3,2,1,0:T(8,128)S(1)}, u32[]{:S(2)}, u32[]{:S(2)}) collective-permute-start(f32[2,1,32,512]{3,2,1,0:T(8,128)S(1)} %get-tuple-element.16), channel_id=1, source_target_pairs={{4,0},{8,4},{12,8},{5,1},{9,5},{13,9},{6,2},{10,6},{14,10},{7,3},{... | collective-permute-start | bytes 393224 | tf_op jit(solution)/shard_map/ppermute | solution.py:27
  54.5 0.0 collective-permute-done.16
  54.5 0.0 collective-permute-done.17
  54.5 0.1 pad_maximum_fusion.44
  54.7 0.1 collective-permute-start.18
  54.7 0.5 collective-permute-start.19
  55.2 0.5 collective-permute-done.14
  55.7 4.4 %collective-permute-done.15 = f32[2,1,32,512]{3,2,1,0:T(8,128)S(1)} collective-permute-done((f32[2,1,32,512]{3,2,1,0:T(8,128)S(1)}, f32[2,1,32,512]{3,2,1,0:T(8,128)S(1)}, u32[]{:S(2)}, u32[]{:S(2)}) %collective-permute-start.15) | collective-permute-done | bytes 131104 | tf_op jit(solution)/shard_map/ppermute | solution.py:27
  60.1 0.0 collective-permute-done.18
  60.1 1.7 %multiply_add_fusion = f32[4,32,512]{2,1,0:T(8,128)} fusion(f32[2,4,34,1]{3,2,1,0:T(8,128)S(1)} %collective-permute-done.19, f32[2,4,1,512]{3,2,1,0:T(1,128)S(1)} %collective-permute-done.17, f32[2,4,32,512]{3,2,1,0:T(8,128)S(1)} %fusion, f32[2,4,1,512]{3,2,1,0:T(1,128)S(1)} %collective-permute-done.16, f32[2,4,34,1]{3,2,1,0:T(8,128)S(1)} %collective-permute-done.18, ...), kind=kLoop, calls=%fused_computation.172 | loop fusion | flops 6619136 | bytes 1934336 | tf_op jit(solution)/shard_map/add | solution.py:73
  61.8 1.0 %multiply_add_fusion.1 = f32[4,32,512]{2,1,0:T(8,128)} fusion(f32[2,4,32,512]{3,2,1,0:T(8,128)S(1)} %fusion, f32[4]{0:T(128)S(1)} %get-tuple-element.2, f32[4]{0:T(128)S(1)} %get-tuple-element.3, f32[2,4,1,512]{3,2,1,0:T(1,128)S(1)} %collective-permute-done.16, f32[2,4,1,512]{3,2,1,0:T(1,128)S(1)} %collective-permute-done.17, ...), kind=kLoop, calls=%fused_computation.173 | loop fusion | flops 2031616 | bytes 1934336 | tf_op jit(solution)/shard_map/add | solution.py:73
  (29 shorter events, 0.4 us)
Async XLA Ops:
  0.6 5.9 %copy-start = (f32[4,32,512]{2,1,0:T(8,128)S(1)}, f32[4,32,512]{2,1,0:T(8,128)}, u32[]{:S(2)}) copy-start(f32[4,32,512]{2,1,0:T(8,128)} %param.5) | copy-start | bytes 786436
  0.6 5.9 %copy-start.1 = (f32[4,32,512]{2,1,0:T(8,128)S(1)}, f32[4,32,512]{2,1,0:T(8,128)}, u32[]{:S(2)}) copy-start(f32[4,32,512]{2,1,0:T(8,128)} %param.4) | copy-start | bytes 786436
  1.6 7.8 %collective-permute-start = (f32[2,1,32,512]{3,2,1,0:T(8,128)S(1)}, f32[2,1,32,512]{3,2,1,0:T(8,128)S(1)}, u32[]{:S(2)}, u32[]{:S(2)}) collective-permute-start(f32[2,1,32,512]{3,2,1,0:T(8,128)S(1)} %fusion.95), channel_id=1, source_target_pairs={{0,4},{4,8},{8,12},{1,5},{5,9},{9,13},{2,6},{6,10},{10,14},{3,7},{... | collective-permute-start | bytes 393224 | tf_op jit(solution)/shard_map/ppermute | solution.py:26
  6.6 4.1 %collective-permute-start.2 = (f32[2,4,1,512]{3,2,1,0:T(1,128)S(1)}, f32[2,4,1,512]{3,2,1,0:T(1,128)S(1)}, u32[]{:S(2)}, u32[]{:S(2)}) collective-permute-start(f32[2,4,1,512]{3,2,1,0:T(1,128)S(1)} %get-tuple-element.26), channel_id=1, source_target_pairs={{0,2},{2,0},{1,3},{3,1},{4,6},{6,4},{5,7},{7,5},{8,10},{10,8},{9,1... | collective-permute-start | bytes 49160 | tf_op jit(solution)/shard_map/ppermute | solution.py:26
  8.2 3.7 %collective-permute-start.3 = (f32[2,4,1,512]{3,2,1,0:T(1,128)S(1)}, f32[2,4,1,512]{3,2,1,0:T(1,128)S(1)}, u32[]{:S(2)}, u32[]{:S(2)}) collective-permute-start(f32[2,4,1,512]{3,2,1,0:T(1,128)S(1)} %get-tuple-element.27), channel_id=1, source_target_pairs={{2,0},{0,2},{3,1},{1,3},{6,4},{4,6},{7,5},{5,7},{10,8},{8,10},{11,... | collective-permute-start | bytes 49160 | tf_op jit(solution)/shard_map/ppermute | solution.py:27
  9.4 7.2 %collective-permute-start.1 = (f32[2,1,32,512]{3,2,1,0:T(8,128)S(1)}, f32[2,1,32,512]{3,2,1,0:T(8,128)S(1)}, u32[]{:S(2)}, u32[]{:S(2)}) collective-permute-start(f32[2,1,32,512]{3,2,1,0:T(8,128)S(1)} %get-tuple-element.7), channel_id=1, source_target_pairs={{4,0},{8,4},{12,8},{5,1},{9,5},{13,9},{6,2},{10,6},{14,10},{7,3},{... | collective-permute-start | bytes 393224 | tf_op jit(solution)/shard_map/ppermute | solution.py:27
  12.0 4.6 %collective-permute-start.4 = (f32[2,4,34,1]{3,2,1,0:T(8,128)S(1)}, f32[2,4,34,1]{3,2,1,0:T(8,128)S(1)}, u32[]{:S(2)}, u32[]{:S(2)}) collective-permute-start(f32[2,4,34,1]{3,2,1,0:T(8,128)S(1)} %get-tuple-element.12), channel_id=1, source_target_pairs={{0,1},{1,0},{2,3},{3,2},{4,5},{5,4},{6,7},{7,6},{8,9},{9,8},{10,11... | collective-permute-start | bytes 3272 | tf_op jit(solution)/shard_map/ppermute | solution.py:26
  12.1 4.6 %collective-permute-start.5 = (f32[2,4,34,1]{3,2,1,0:T(8,128)S(1)}, f32[2,4,34,1]{3,2,1,0:T(8,128)S(1)}, u32[]{:S(2)}, u32[]{:S(2)}) collective-permute-start(f32[2,4,34,1]{3,2,1,0:T(8,128)S(1)} %get-tuple-element.13), channel_id=1, source_target_pairs={{1,0},{0,1},{3,2},{2,3},{5,4},{4,5},{7,6},{6,7},{9,8},{8,9},{11,10... | collective-permute-start | bytes 3272 | tf_op jit(solution)/shard_map/ppermute | solution.py:27
  18.0 1.3 %copy-start.2 = (s32[32,512]{1,0:T(8,128)S(1)}, s32[32,512]{1,0:T(8,128)}, u32[]{:S(2)}) copy-start(s32[32,512]{1,0:T(8,128)} %param.7) | copy-start | bytes 196612
  18.0 6.9 %collective-permute-start.6 = (f32[2,1,32,512]{3,2,1,0:T(8,128)S(1)}, f32[2,1,32,512]{3,2,1,0:T(8,128)S(1)}, u32[]{:S(2)}, u32[]{:S(2)}) collective-permute-start(f32[2,1,32,512]{3,2,1,0:T(8,128)S(1)} %fusion.97), channel_id=1, source_target_pairs={{4,0},{8,4},{12,8},{5,1},{9,5},{13,9},{6,2},{10,6},{14,10},{7,3},{... | collective-permute-start | bytes 393224 | tf_op jit(solution)/shard_map/ppermute | solution.py:35
  25.1 11.2 %collective-permute-start.7 = (f32[2,1,32,512]{3,2,1,0:T(8,128)S(1)}, f32[2,1,32,512]{3,2,1,0:T(8,128)S(1)}, u32[]{:S(2)}, u32[]{:S(2)}) collective-permute-start(f32[2,1,32,512]{3,2,1,0:T(8,128)S(1)} %get-tuple-element.22), channel_id=1, source_target_pairs={{0,4},{4,8},{8,12},{1,5},{5,9},{9,13},{2,6},{6,10},{10,14},{3,7},{... | collective-permute-start | bytes 393224 | tf_op jit(solution)/shard_map/ppermute | solution.py:26
  29.0 7.3 %collective-permute-start.8 = (f32[2,1,32,512]{3,2,1,0:T(8,128)S(1)}, f32[2,1,32,512]{3,2,1,0:T(8,128)S(1)}, u32[]{:S(2)}, u32[]{:S(2)}) collective-permute-start(f32[2,1,32,512]{3,2,1,0:T(8,128)S(1)} %get-tuple-element.23), channel_id=1, source_target_pairs={{4,0},{8,4},{12,8},{5,1},{9,5},{13,9},{6,2},{10,6},{14,10},{7,3},{... | collective-permute-start | bytes 393224 | tf_op jit(solution)/shard_map/ppermute | solution.py:27
  30.3 3.8 %collective-permute-start.10 = (f32[2,4,1,512]{3,2,1,0:T(1,128)S(1)}, f32[2,4,1,512]{3,2,1,0:T(1,128)S(1)}, u32[]{:S(2)}, u32[]{:S(2)}) collective-permute-start(f32[2,4,1,512]{3,2,1,0:T(1,128)S(1)} %get-tuple-element.25), channel_id=1, source_target_pairs={{2,0},{0,2},{3,1},{1,3},{6,4},{4,6},{7,5},{5,7},{10,8},{8,10},{11,... | collective-permute-start | bytes 49160 | tf_op jit(solution)/shard_map/ppermute | solution.py:27
  31.9 3.7 %collective-permute-start.9 = (f32[2,4,1,512]{3,2,1,0:T(1,128)S(1)}, f32[2,4,1,512]{3,2,1,0:T(1,128)S(1)}, u32[]{:S(2)}, u32[]{:S(2)}) collective-permute-start(f32[2,4,1,512]{3,2,1,0:T(1,128)S(1)} %get-tuple-element.24), channel_id=1, source_target_pairs={{0,2},{2,0},{1,3},{3,1},{4,6},{6,4},{5,7},{7,5},{8,10},{10,8},{9,1... | collective-permute-start | bytes 49160 | tf_op jit(solution)/shard_map/ppermute | solution.py:26
  35.7 1.5 %collective-permute-start.11 = (f32[2,4,34,1]{3,2,1,0:T(8,128)S(1)}, f32[2,4,34,1]{3,2,1,0:T(8,128)S(1)}, u32[]{:S(2)}, u32[]{:S(2)}) collective-permute-start(f32[2,4,34,1]{3,2,1,0:T(8,128)S(1)} %get-tuple-element.10), channel_id=1, source_target_pairs={{0,1},{1,0},{2,3},{3,2},{4,5},{5,4},{6,7},{7,6},{8,9},{9,8},{10,11... | collective-permute-start | bytes 3272 | tf_op jit(solution)/shard_map/ppermute | solution.py:26
  35.8 1.6 %collective-permute-start.12 = (f32[2,4,34,1]{3,2,1,0:T(8,128)S(1)}, f32[2,4,34,1]{3,2,1,0:T(8,128)S(1)}, u32[]{:S(2)}, u32[]{:S(2)}) collective-permute-start(f32[2,4,34,1]{3,2,1,0:T(8,128)S(1)} %get-tuple-element.11), channel_id=1, source_target_pairs={{1,0},{0,1},{3,2},{2,3},{5,4},{4,5},{7,6},{6,7},{9,8},{8,9},{11,10... | collective-permute-start | bytes 3272 | tf_op jit(solution)/shard_map/ppermute | solution.py:27
  38.8 8.5 %collective-permute-start.13 = (f32[2,1,32,512]{3,2,1,0:T(8,128)S(1)}, f32[2,1,32,512]{3,2,1,0:T(8,128)S(1)}, u32[]{:S(2)}, u32[]{:S(2)}) collective-permute-start(f32[2,1,32,512]{3,2,1,0:T(8,128)S(1)} %fusion.96), channel_id=1, source_target_pairs={{4,0},{8,4},{12,8},{5,1},{9,5},{13,9},{6,2},{10,6},{14,10},{7,3},{... | collective-permute-start | bytes 393224 | tf_op jit(solution)/shard_map/ppermute | solution.py:35
  47.5 7.1 %collective-permute-start.16 = (f32[2,4,1,512]{3,2,1,0:T(1,128)S(1)}, f32[2,4,1,512]{3,2,1,0:T(1,128)S(1)}, u32[]{:S(2)}, u32[]{:S(2)}) collective-permute-start(f32[2,4,1,512]{3,2,1,0:T(1,128)S(1)} %get-tuple-element.19), channel_id=1, source_target_pairs={{0,2},{2,0},{1,3},{3,1},{4,6},{6,4},{5,7},{7,5},{8,10},{10,8},{9,1... | collective-permute-start | bytes 49160 | tf_op jit(solution)/shard_map/ppermute | solution.py:26
  48.1 6.5 %collective-permute-start.17 = (f32[2,4,1,512]{3,2,1,0:T(1,128)S(1)}, f32[2,4,1,512]{3,2,1,0:T(1,128)S(1)}, u32[]{:S(2)}, u32[]{:S(2)}) collective-permute-start(f32[2,4,1,512]{3,2,1,0:T(1,128)S(1)} %get-tuple-element.18), channel_id=1, source_target_pairs={{2,0},{0,2},{3,1},{1,3},{6,4},{4,6},{7,5},{5,7},{10,8},{8,10},{11,... | collective-permute-start | bytes 49160 | tf_op jit(solution)/shard_map/ppermute | solution.py:27
  49.6 6.1 %collective-permute-start.14 = (f32[2,1,32,512]{3,2,1,0:T(8,128)S(1)}, f32[2,1,32,512]{3,2,1,0:T(8,128)S(1)}, u32[]{:S(2)}, u32[]{:S(2)}) collective-permute-start(f32[2,1,32,512]{3,2,1,0:T(8,128)S(1)} %get-tuple-element.17), channel_id=1, source_target_pairs={{0,4},{4,8},{8,12},{1,5},{5,9},{9,13},{2,6},{6,10},{10,14},{3,7},{... | collective-permute-start | bytes 393224 | tf_op jit(solution)/shard_map/ppermute | solution.py:26
  53.2 6.9 %collective-permute-start.15 = (f32[2,1,32,512]{3,2,1,0:T(8,128)S(1)}, f32[2,1,32,512]{3,2,1,0:T(8,128)S(1)}, u32[]{:S(2)}, u32[]{:S(2)}) collective-permute-start(f32[2,1,32,512]{3,2,1,0:T(8,128)S(1)} %get-tuple-element.16), channel_id=1, source_target_pairs={{4,0},{8,4},{12,8},{5,1},{9,5},{13,9},{6,2},{10,6},{14,10},{7,3},{... | collective-permute-start | bytes 393224 | tf_op jit(solution)/shard_map/ppermute | solution.py:27
  54.7 5.4 %collective-permute-start.18 = (f32[2,4,34,1]{3,2,1,0:T(8,128)S(1)}, f32[2,4,34,1]{3,2,1,0:T(8,128)S(1)}, u32[]{:S(2)}, u32[]{:S(2)}) collective-permute-start(f32[2,4,34,1]{3,2,1,0:T(8,128)S(1)} %get-tuple-element.9), channel_id=1, source_target_pairs={{0,1},{1,0},{2,3},{3,2},{4,5},{5,4},{6,7},{7,6},{8,9},{9,8},{10,11... | collective-permute-start | bytes 3272 | tf_op jit(solution)/shard_map/ppermute | solution.py:26
  54.7 5.4 %collective-permute-start.19 = (f32[2,4,34,1]{3,2,1,0:T(8,128)S(1)}, f32[2,4,34,1]{3,2,1,0:T(8,128)S(1)}, u32[]{:S(2)}, u32[]{:S(2)}) collective-permute-start(f32[2,4,34,1]{3,2,1,0:T(8,128)S(1)} %get-tuple-element.8), channel_id=1, source_target_pairs={{1,0},{0,1},{3,2},{2,3},{5,4},{4,5},{7,6},{6,7},{9,8},{8,9},{11,10... | collective-permute-start | bytes 3272 | tf_op jit(solution)/shard_map/ppermute | solution.py:27
where the time goes:
time: 63.2 us; the launch traced here: 62.9 us
  starting transfers between devices  27 us (43%)
  waiting for transfers between devices  26.9 us (43%)
  other arithmetic  7.19 us (11%)
  between operations  1.67 us (3%)
    ppermute x9, starting transfers between devices, extended(): before = lax.ppermute(last, axis, up)  15.4 us
    ppermute x2, waiting for transfers between devices, passed_along(): return lax.ppermute(shard, axis, pairs)  12.6 us
    ppermute x9, waiting for transfers between devices, extended(): after = lax.ppermute(first, axis, down)  11.5 us
    ppermute x9, starting transfers between devices, extended(): after = lax.ppermute(first, axis, down)  8.95 us
    ppermute x9, waiting for transfers between devices, extended(): before = lax.ppermute(last, axis, up)  2.79 us
    add x2, other arithmetic, advance(): solutes + time_step * solute_rate  2.72 us
    ppermute x2, starting transfers between devices, passed_along(): return lax.ppermute(shard, axis, pairs)  2.58 us
    another operation x6, other arithmetic, advance(): jnp.stack([phases + time_step * growth_rate, solutes + time_step * solute...  1.39 us
  transfers between devices with their start and end apart: 20, of which 10 were waited for; matrix products, arithmetic and copies ran while one was open for 1% of the time, Pallas kernels for 0%

commit v1 on v0

v1 whole, which is shorter than its diff:
```python
import functools

import jax
import jax.numpy as jnp
from jax import lax
from jax.experimental import pallas as pl
from jax.experimental.pallas import tpu as pltpu
from jax.sharding import PartitionSpec as P

ITERS = 3
LANES = 128
SUBLANES = 8

partition = 0.15
coupling = 2.0
diffusion = 2.0
spacing_sq = 0.64
time_step = 0.025
gradient_scale = 1.2
drift_rate = 0.01
seed_levels = 1024.0

BELOW = ITERS - 1
ABOVE = ITERS + 1
RIMMED = ITERS
F32 = jnp.float32


def ring(size, by):
    return [(i, (i + by) % size) for i in range(size)]


def chain(size, by):
    return [(i, i + by) for i in range(size) if 0 <= i + by < size]


def lane_of(shape):
    return lax.broadcasted_iota(jnp.int32, shape, len(shape) - 1)


def row_of(shape):
    return lax.broadcasted_iota(jnp.int32, shape, len(shape) - 2)


def level(seed):
    return seed.astype(F32) / seed_levels - 1.0


def whole(shape):
    return pl.BlockSpec(shape, lambda _: (0,) * len(shape))


def at_block(shape, index):
    return pl.BlockSpec(shape, lambda _: index)


def cost(count):
    return pl.CostEstimate(flops=count, bytes_accessed=4 * count, transcendentals=0)


def sides_kernel(planes, phi_a, phi_b, sol_a, sol_b, seed_a, seed_b, out):
    keep = lane_of(phi_a.shape[1:]) < LANES // 2
    for k in range(planes):
        out[k] = jnp.where(keep, phi_a[k], phi_b[k])
        out[planes + k] = jnp.where(keep, sol_a[k], sol_b[k])
    out[2 * planes] = level(jnp.where(keep, seed_a[...], seed_b[...]))


def pack_sides(phi, sol, seed):
    planes, rows, cols = phi.shape
    last = cols // LANES - 1
    edge = (planes, rows, LANES)
    return pl.pallas_call(
        functools.partial(sides_kernel, planes),
        out_shape=jax.ShapeDtypeStruct((2 * planes + 1, rows, LANES), F32),
        in_specs=[
            at_block(edge, (0, 0, 0)),
            at_block(edge, (0, 0, last)),
            at_block(edge, (0, 0, 0)),
            at_block(edge, (0, 0, last)),
            at_block((rows, LANES), (0, 0)),
            at_block((rows, LANES), (0, last)),
        ],
        out_specs=whole((2 * planes + 1, rows, LANES)),
        grid=(1,),
        cost_estimate=cost((2 * planes + 1) * rows * LANES),
        name="pack_sides",
    )(phi, phi, sol, sol, seed, seed)


def rows_kernel(planes, cols, phi_a, phi_b, sol_a, sol_b, seed_a, seed_b, side_a, side_b, out):
    keep = row_of((SUBLANES, cols)) < SUBLANES // 2
    for k in range(planes):
        out[k, :, :cols] = jnp.where(keep, phi_a[k], phi_b[k])
        out[planes + k, :, :cols] = jnp.where(keep, sol_a[k], sol_b[k])
    out[2 * planes, :, :cols] = level(jnp.where(keep, seed_a[...], seed_b[...]))
    keep = row_of((SUBLANES, LANES)) < SUBLANES // 2
    for k in range(2 * planes + 1):
        out[k, :, cols:] = jnp.where(keep, side_a[k], side_b[k])


def pack_rows(phi, sol, seed, side):
    planes, rows, cols = phi.shape
    last = rows // SUBLANES - 1
    edge = (planes, SUBLANES, cols)
    count = 2 * planes + 1
    return pl.pallas_call(
        functools.partial(rows_kernel, planes, cols),
        out_shape=jax.ShapeDtypeStruct((count, SUBLANES, cols + LANES), F32),
        in_specs=[
            at_block(edge, (0, 0, 0)),
            at_block(edge, (0, last, 0)),
            at_block(edge, (0, 0, 0)),
            at_block(edge, (0, last, 0)),
            at_block((SUBLANES, cols), (0, 0)),
            at_block((SUBLANES, cols), (last, 0)),
            at_block((count, SUBLANES, LANES), (0, 0, 0)),
            at_block((count, SUBLANES, LANES), (0, last, 0)),
        ],
        out_specs=whole((count, SUBLANES, cols + LANES)),
        grid=(1,),
        cost_estimate=cost(count * SUBLANES * (cols + LANES)),
        name="pack_rows",
    )(phi, phi, sol, sol, seed, seed, side, side)


def put_row_tile(out, place, tile):
    for t in range(tile.shape[1] // LANES):
        start = (place * (tile.shape[1] // LANES) + t) * SUBLANES
        out[start : start + SUBLANES, :] = tile[:, t * LANES : (t + 1) * LANES]


def get_row_tile(ref, place, width):
    tiles = width // LANES
    return [
        ref[(place * tiles + t) * SUBLANES : (place * tiles + t + 1) * SUBLANES, :]
        for t in range(tiles)
    ]


LANE_STEP = 2 * SUBLANES


def rims_kernel(planes, cross, side, down, up):
    half = SUBLANES // 2
    rows_iota = row_of(cross.shape[1:])
    lanes_iota = lane_of(side.shape[1:])

    def rows_pair(first, second):
        mixed = pltpu.roll(cross[second], half, 0)
        inner = (rows_iota == half - 1) | (rows_iota == half)
        return jnp.where(inner, mixed, cross[first])

    def rows_two(first, second):
        mixed = pltpu.roll(cross[second], half, 0)
        inner = (rows_iota >= half - 2) & (rows_iota < half + 2)
        return jnp.where(inner, mixed, cross[first])

    def columns(entries):
        packed = side[entries[0]]
        for k, entry in enumerate(entries[1:], 1):
            moved = pltpu.roll(side[entry], k * LANE_STEP, 1)
            near = (lanes_iota >= k * LANE_STEP - half) & (lanes_iota < k * LANE_STEP + half)
            packed = jnp.where(near, moved, packed)
        return packed

    put_row_tile(down, 0, rows_pair(0, 2))
    put_row_tile(down, 1, rows_pair(planes, planes + 2))
    put_row_tile(down, 2, rows_two(1, planes + 1))
    start = down.shape[0] - side.shape[1]
    down[start:, :] = columns([0, planes, 1, planes + 1, 2, planes + 2])
    put_row_tile(up, 0, rows_pair(planes - 1, 2 * planes - 1))
    start = up.shape[0] - side.shape[1]
    up[start:, :] = columns([planes - 1, 2 * planes - 1])


def pack_rims(planes, cross, side):
    tiles = cross.shape[2] // LANES
    rows = side.shape[1]
    down = (3 * tiles * SUBLANES + rows, LANES)
    up = (tiles * SUBLANES + rows, LANES)
    return pl.pallas_call(
        functools.partial(rims_kernel, planes),
        out_shape=(jax.ShapeDtypeStruct(down, F32), jax.ShapeDtypeStruct(up, F32)),
        in_specs=[whole(cross.shape), whole(side.shape)],
        out_specs=(whole(down), whole(up)),
        grid=(1,),
        cost_estimate=cost(down[0] * LANES),
        name="pack_rims",
    )(cross, side)


def evolve_kernel(
    planes,
    grid_planes,
    shift_ref,
    where_ref,
    phi_in,
    sol_in,
    phi_up,
    sol_up,
    lows,
    side,
    cross,
    rim_down,
    rim_up,
    seed,
    phi_out,
    sol_out,
    phi_a,
    sol_a,
    mob_a,
    mix_a,
    phi_b,
    sol_b,
    mob_b,
    mix_b,
    sol_top,
    rims_d,
    rims_u,
    levels,
    sems,
):
    _, rows, cols = phi_in.shape
    wide = cols + LANES
    strips = rows // SUBLANES
    base = BELOW
    top = base + planes
    half = SUBLANES // 2
    count = top + ABOVE
    body = (pl.ds(0, rows), pl.ds(0, cols))
    edge = (pl.ds(0, rows), pl.ds(cols, LANES))
    last = (pl.ds(rows, SUBLANES), pl.ds(0, wide))
    moves = []

    def move(source, target):
        copy = pltpu.make_async_copy(source, target, sems.at[len(moves)])
        copy.start()
        moves.append(copy)

    own = pl.ds(base, planes)
    move(phi_in, phi_a.at[(own, *body)])
    move(sol_in, sol_a.at[(own, *body)])
    move(phi_up.at[pl.ds(0, ABOVE)], phi_a.at[(pl.ds(top, ABOVE), *body)])
    move(sol_up.at[pl.ds(0, ABOVE)], sol_a.at[(pl.ds(top, ABOVE), *body)])
    move(lows.at[pl.ds(0, BELOW)], phi_a.at[(pl.ds(0, BELOW), *body)])
    move(lows.at[pl.ds(BELOW, BELOW)], sol_a.at[(pl.ds(0, BELOW), *body)])
    move(side.at[pl.ds(0, planes)], phi_a.at[(own, *edge)])
    move(side.at[pl.ds(planes, planes)], sol_a.at[(own, *edge)])
    move(side.at[2 * planes], sol_top.at[edge])
    move(cross.at[pl.ds(0, planes)], phi_a.at[(own, *last)])
    move(cross.at[pl.ds(planes, planes)], sol_a.at[(own, *last)])
    move(cross.at[2 * planes], sol_top.at[last])
    move(rim_down, rims_d)
    move(rim_up, rims_u)
    move(seed, levels)
    for copy in moves:
        copy.wait()

    rowsplit = row_of((SUBLANES, LANES))

    def put_rows(ref, plane, tiles, turn):
        for t, tile in enumerate(tiles):
            lanes = slice(t * LANES, (t + 1) * LANES)
            ref[plane, rows : rows + SUBLANES, lanes] = pltpu.roll(tile, half, 0) if turn else tile

    def put_columns(ref, plane, packed, k):
        turned = pltpu.roll(packed, LANES - k * LANE_STEP, 1) if k else packed
        ref[plane, 0:rows, cols:] = turned

    first = get_row_tile(rims_d, 0, wide)
    put_rows(phi_a, top, first, False)
    put_rows(phi_a, top + 2, first, True)
    first = get_row_tile(rims_d, 1, wide)
    put_rows(sol_a, top, first, False)
    put_rows(sol_a, top + 2, first, True)
    first = get_row_tile(rims_d, 2, wide)
    put_rows(phi_a, top + 1, first, False)
    put_rows(sol_a, top + 1, first, True)
    packed = rims_d[rims_d.shape[0] - rows :, :]
    for k, (ref, plane) in enumerate(
        [(phi_a, 0), (sol_a, 0), (phi_a, 1), (sol_a, 1), (phi_a, 2), (sol_a, 2)]
    ):
        put_columns(ref, top + plane, packed, k)
    first = get_row_tile(rims_u, 0, wide)
    put_rows(phi_a, base - 1, first, False)
    put_rows(sol_a, base - 1, first, True)
    packed = rims_u[rims_u.shape[0] - rows :, :]
    put_columns(phi_a, base - 1, packed, 0)
    put_columns(sol_a, base - 1, packed, 1)

    shift = shift_ref[0]
    grow_index = where_ref[0]
    at_bottom = where_ref[1] == 1
    at_top = where_ref[2] == 1

    def derive(phi, sol):
        mobile = 1.0 - jnp.clip(phi, -1.0, 1.0)
        return mobile, mobile * sol

    @pl.loop(0, count)
    def _(e):
        for r in range(strips + 1):
            at = (e, slice(r * SUBLANES, (r + 1) * SUBLANES), slice(None))
            mob_a[at], mix_a[at] = derive(phi_a[at], sol_a[at])

    @pl.when(at_top)
    def _():
        sol_top[0:rows, 0:cols] = level(levels[...])

    def bring_top(phi, sol, mob, mix):
        for r in range(strips + 1):
            at = slice(r * SUBLANES, (r + 1) * SUBLANES)
            value = sol_top[at, :]
            phi[top, at, :] = jnp.full((SUBLANES, wide), -1.0, F32)
            sol[top, at, :] = value
            mob[top, at, :] = jnp.full((SUBLANES, wide), 2.0, F32)
            mix[top, at, :] = 2.0 * value

    def step_plane(step, source, target, e, full):
        phi, sol, mob, mix = source
        moved = shift < step
        low_end = jnp.where(moved, base + 1, base)
        high_end = jnp.where(moved, top, top - 1)
        lower = jnp.where(at_bottom & (e == low_end), e, e - 1)
        upper = jnp.where(at_top & (e == high_end), e, e + 1)
        height = (grow_index * planes + e - base).astype(F32)
        height = jnp.broadcast_to(height, (SUBLANES, LANES))
        temper = gradient_scale * ((height + 0.5) * (1.0 / grid_planes) - 0.5) - drift_rate * step
        pace = time_step / (1.0 - (1.0 - partition) * temper)
        width = wide if full else cols
        across = width // LANES
        spread = lambda v: jnp.concatenate([v] * across, axis=1)
        temper, pace = spread(temper), spread(pace)
        pull = pace * (1.0 / spacing_sq)
        drive = pace * coupling
        rest = pull * 6.0
        kappa = 0.25 * diffusion * time_step / spacing_sq
        rowid = row_of((SUBLANES, wide))
        heads = rowid == 0
        tails = rowid == SUBLANES - 1
        for r in range(strips + (1 if full else 0)):
            before = (r + strips) % (strips + 1)
            after = (r + 1) % (strips + 1)
            cut = lambda k: slice(k * SUBLANES, (k + 1) * SUBLANES)

            def around(ref):
                mid = ref[e, cut(r), :]
                prev = ref[e, cut(before), :]
                nxt = ref[e, cut(after), :]
                rowsum = pltpu.roll(jnp.where(tails, prev, mid), 1, 0)
                rowsum = rowsum + pltpu.roll(jnp.where(heads, nxt, mid), SUBLANES - 1, 0)
                colsum = pltpu.roll(mid, 1, 1) + pltpu.roll(mid, wide - 1, 1)
                total = rowsum[:, :width] + colsum[:, :width]
                total = total + ref[lower, cut(r), :width] + ref[upper, cut(r), :width]
                return mid[:, :width], total

            p, sum_p = around(phi)
            u, sum_u = around(sol)
            m, sum_m = around(mob)
            _, sum_x = around(mix)
            well = 1.0 - p * p
            gain = pull * sum_p + p * (pace * well - rest) - drive * (well * well) * (u + temper)
            new_p = p + gain
            flow = m * sum_u + sum_x - u * (6.0 * m + sum_m)
            weight = partition + 0.5 * (1.0 - partition) * m
            change = kappa * flow + (0.5 + 0.5 * (1.0 - partition) * u) * gain
            new_u = u + change / weight
            target(e, cut(r), width, new_p, new_u)

    first = (phi_a, sol_a, mob_a, mix_a)
    second = (phi_b, sol_b, mob_b, mix_b)

    def into(refs):
        def write(e, at, width, new_p, new_u):
            mobile, mixed = derive(new_p, new_u)
            for ref, value in zip(refs, (new_p, new_u, mobile, mixed)):
                ref[e, at, :width] = value

        return write

    def finish(e, at, width, new_p, new_u):
        phi_out[e - base - 1, at, :] = new_p
        sol_out[e - base - 1, at, :] = new_u

    @pl.loop(base, top + 2)
    def _(e):
        step_plane(0, first, into(second), e, True)

    step_plane(0, first, into(second), base - 1, False)
    step_plane(0, first, into(second), top + 2, False)

    @pl.when(at_top & (shift == 0))
    def _():
        bring_top(*second)

    @pl.loop(base + 1, top + 1)
    def _(e):
        step_plane(1, second, into(first), e, True)

    step_plane(1, second, into(first), base, False)
    step_plane(1, second, into(first), top + 1, False)

    @pl.when(at_top & (shift == 1))
    def _():
        bring_top(*first)

    @pl.loop(base + 1, top + 1)
    def _(e):
        step_plane(2, first, finish, e, False)


def evolve(grid_planes, shift, where, phi, sol, phi_up, sol_up, lows, side, cross, down, up, seed):
    planes, rows, cols = phi.shape
    state = (planes + BELOW + ABOVE, rows + SUBLANES, cols + LANES)
    block = jax.ShapeDtypeStruct(phi.shape, F32)
    hbm = pl.BlockSpec(memory_space=pl.ANY)
    smem = pl.BlockSpec(memory_space=pltpu.SMEM)
    return pl.pallas_call(
        functools.partial(evolve_kernel, planes, grid_planes),
        out_shape=(block, block),
        in_specs=[smem, smem] + [hbm] * 10,
        out_specs=(whole(phi.shape), whole(phi.shape)),
        scratch_shapes=[pltpu.VMEM(state, F32)] * 8
        + [
            pltpu.VMEM(state[1:], F32),
            pltpu.VMEM(down.shape, F32),
            pltpu.VMEM(up.shape, F32),
            pltpu.VMEM(seed.shape, jnp.int32),
            pltpu.SemaphoreType.DMA((15,)),
        ],
        grid=(1,),
        cost_estimate=cost(3 * 64 * phi.size),
        name="evolve",
    )(shift, where, phi, sol, phi_up, sol_up, lows, side, cross, down, up, seed)


def swap_edges(message, axis, keep):
    size = lax.axis_size(axis)
    if size <= 2:
        return lax.ppermute(message, axis, ring(size, 1))
    after = lax.ppermute(message, axis, ring(size, -1))
    before = lax.ppermute(message, axis, ring(size, 1))
    return jnp.where(keep, after, before)


def shards(phi, sol, shift_step, seed):
    planes, rows, cols = phi.shape
    size = lax.axis_size("grow")
    index = lax.axis_index("grow")
    where = jnp.stack([index, index == 0, index == size - 1]).astype(jnp.int32)
    fall = chain(size, -1)
    rise = chain(size, 1)
    phi_up = lax.ppermute(phi, "grow", fall)
    sol_up = lax.ppermute(sol, "grow", fall)
    lows = jnp.concatenate([phi[planes - BELOW :], sol[planes - BELOW :]])
    lows = lax.ppermute(lows, "grow", rise)
    side = pack_sides(phi, sol, seed)
    side = swap_edges(side, "side", lane_of(side.shape) < LANES // 2)
    cross = pack_rows(phi, sol, seed, side)
    cross = swap_edges(cross, "cross", row_of(cross.shape) < SUBLANES // 2)
    down, up = pack_rims(planes, cross, side)
    down = lax.ppermute(down, "grow", fall)
    up = lax.ppermute(up, "grow", rise)
    return evolve(
        planes * size, shift_step, where, phi, sol, phi_up, sol_up, lows, side, cross, down, up, seed
    )


def solution(mesh):
    return jax.shard_map(
        shards,
        mesh=mesh,
        in_specs=(
            P(("groups", "grow"), "cross", "side"),
            P(("groups", "grow"), "cross", "side"),
            P("groups"),
            P(("groups", "cross"), "side"),
        ),
        out_specs=(P(("groups", "grow"), "cross", "side"), P(("groups", "grow"), "cross", "side")),
        check_vma=False,
    )
```

time: 63.2 us -> 39.3 us (0.62)
  waiting for transfers between devices: 26.9 us -> 5.39 us
  Pallas kernels: 0 us -> 13.6 us
  starting transfers between devices: 27 us -> 15.9 us
  other arithmetic: 7.19 us -> 0.63 us
  local copies, waits for them, and re-layouts: 0.11 us -> 1.98 us
    ppermute x20 -> x7, waiting for transfers between devices: 26.9 us -> 5.39 us  [the longest x1 3.34 us: shards(): sol_up = lax.ppermute(sol, 'grow', fall)]
    pallas_call x0 -> x4, Pallas kernels: none -> 13.6 us  [the longest x1 8.62 us: evolve(): pl.pallas_call(functools.partial(evolve_kernel, planes, grid_planes), out...]
    ppermute x20 -> x7, starting transfers between devices: 27 us -> 15.9 us  [the longest x1 5.16 us: shards(): up = lax.ppermute(up, 'grow', rise)]
    add x4 -> x0, other arithmetic: 4.1 us -> none  [the longest x2 2.72 us: advance(): solutes + time_step * solute_rate]
    unnamed x6 -> x18, local copies, waits for them, and re-layouts: 0.01 us -> 1.97 us
    another operation x9 -> x1, other arithmetic: 2.36 us -> 0.61 us  [shards(): where = jnp.stack([index, index == 0, index == size - 1]).astype(jnp.int32)]
  transfers between devices with their start and end apart: 20 -> 7, of which waited for: 10 -> 3; matrix products, arithmetic and copies ran while one was open for 1% -> 2% of each run, Pallas kernels for 0% -> 4%
where the time goes in v1:
time: 39.3 us; the launch traced here: 38.9 us
  starting transfers between devices  15.9 us (40%)
  Pallas kernels  13.6 us (35%)
  waiting for transfers between devices  5.39 us (14%)
  local copies, waits for them, and re-layouts  1.98 us (5%)
  between operations  1.43 us (4%)
  other arithmetic  0.63 us (2%)
    pallas_call x1, Pallas kernels, evolve(): pl.pallas_call(functools.partial(evolve_kernel, planes, grid_planes), out...  8.62 us
    ppermute x1, starting transfers between devices, shards(): up = lax.ppermute(up, 'grow', rise)  5.16 us
    ppermute x1, starting transfers between devices, shards(): lows = lax.ppermute(lows, 'grow', rise)  3.5 us
    ppermute x1, waiting for transfers between devices, shards(): sol_up = lax.ppermute(sol, 'grow', fall)  3.34 us
    ppermute x2, starting transfers between devices, swap_edges(): return lax.ppermute(message, axis, ring(size, 1))  3.33 us
    unnamed x18, local copies, waits for them, and re-layouts  1.97 us
    pallas_call x1, Pallas kernels, pack_rims(): pl.pallas_call(functools.partial(rims_kernel, planes), out_shape=(jax.Sha...  1.73 us
    pallas_call x1, Pallas kernels, pack_rows(): pl.pallas_call(functools.partial(rows_kernel, planes, cols), out_shape=ja...  1.65 us
  transfers between devices with their start and end apart: 7, of which 3 were waited for; matrix products, arithmetic and copies ran while one was open for 2% of the time, Pallas kernels for 4%

profile of v1, /device:TPU:0, one launch (start us, length us, event | category | flops | bytes accessed | tf_op | source)
XLA Modules:
  0.0 38.9 jit_solution(12829415363624920059)
XLA Ops:
  0.6 1.6 %pack_sides.1 = f32[9,32,128]{2,1,0:T(8,128)} custom-call(f32[4,32,512]{2,1,0:T(8,128)} %phi_in.1, f32[4,32,512]{2,1,0:T(8,128)} %phi_in.1, f32[4,32,512]{2,1,0:T(8,128)} %sol_in.1, f32[4,32,512]{2,1,0:T(8,128)} %sol_in.1, s32[32,512]{1,0:T(8,128)} %seed.1, s32[32,512]{1,0:T(8,128)} %seed.1), custom_call_target="tpu_custom_call" | custom-call | flops 36864 | bytes 147456 | tf_op jit(solution)/shard_map/pack_sides/pallas_call | solution.py:73
  2.3 0.5 %collective-permute-start.3 = (f32[9,32,128]{2,1,0:T(8,128)}, f32[9,32,128]{2,1,0:T(8,128)S(1)}, u32[]{:S(2)}, u32[]{:S(2)}) collective-permute-start(f32[9,32,128]{2,1,0:T(8,128)} %pack_sides.1), channel_id=1, source_target_pairs={{0,1},{1,0},{2,3},{3,2},{4,5},{5,4},{6,7},{7,6},{8,9},{9,8},{10,11... | collective-permute-start | bytes 442376 | tf_op jit(solution)/shard_map/ppermute | solution.py:441
  2.8 0.0 slice-start
  2.8 0.0 slice-start.1
  2.8 1.2 %collective-permute-done.3.side_a.side_b.side = f32[9,32,128]{2,1,0:T(8,128)S(1)} collective-permute-done((f32[9,32,128]{2,1,0:T(8,128)}, f32[9,32,128]{2,1,0:T(8,128)S(1)}, u32[]{:S(2)}, u32[]{:S(2)}) %collective-permute-start.3) | collective-permute-done | bytes 147488 | tf_op jit(solution)/shard_map/ppermute | solution.py:441
  4.0 0.0 copy-start.2
  4.0 0.7 %copy-done.2 = f32[9,32,128]{2,1,0:T(8,128)} copy-done((f32[9,32,128]{2,1,0:T(8,128)}, f32[9,32,128]{2,1,0:T(8,128)S(1)}, u32[]{:S(2)}) %copy-start.2) | copy-done | bytes 147480
  4.6 1.7 %pack_rows.1 = f32[9,8,640]{2,1,0:T(8,128)} custom-call(f32[4,32,512]{2,1,0:T(8,128)} %phi_in.1, f32[4,32,512]{2,1,0:T(8,128)} %phi_in.1, f32[4,32,512]{2,1,0:T(8,128)} %sol_in.1, f32[4,32,512]{2,1,0:T(8,128)} %sol_in.1, s32[32,512]{1,0:T(8,128)} %seed.1, s32[32,512]{1,0:T(8,128)} %seed.1, f32[9,32,128]{2,1,0:T(8,128)} %copy-done.2, f32[9,32,128]{2,1,0:T(8,128)} %copy-done.2), custom_call_target="tpu_custom_call" | custom-call | flops 46080 | bytes 184320 | tf_op jit(solution)/shard_map/pack_rows/pallas_call | solution.py:107
  6.3 0.0 copy-start
  6.3 0.0 copy-start.1
  6.3 2.8 %collective-permute-start.4 = (f32[9,8,640]{2,1,0:T(8,128)}, f32[9,8,640]{2,1,0:T(8,128)S(1)}, u32[]{:S(2)}, u32[]{:S(2)}) collective-permute-start(f32[9,8,640]{2,1,0:T(8,128)} %pack_rows.1), channel_id=1, source_target_pairs={{0,2},{2,0},{1,3},{3,1},{4,6},{6,4},{5,7},{7,5},{8,10},{10,8},{9,1... | collective-permute-start | bytes 552968 | tf_op jit(solution)/shard_map/ppermute | solution.py:441
  9.1 0.0 slice-done
  9.1 0.0 slice-done.1
  9.2 3.5 %collective-permute-start.2 = (f32[4,32,512]{2,1,0:T(8,128)S(1)}, f32[4,32,512]{2,1,0:T(8,128)S(1)}, u32[]{:S(2)}, u32[]{:S(2)}) collective-permute-start(f32[4,32,512]{2,1,0:T(8,128)S(1)} %pad_maximum_fusion), channel_id=1, source_target_pairs={{0,4},{4,8},{8,12},{1,5},{5,9},{9,13},{2,6},{6,10},{10,14},{3,7},{... | collective-permute-start | bytes 786440 | tf_op jit(solution)/shard_map/ppermute | solution.py:457
  12.7 0.0 copy-done
  12.7 1.3 %collective-permute-start = (f32[4,32,512]{2,1,0:T(8,128)S(1)}, f32[4,32,512]{2,1,0:T(8,128)S(1)}, u32[]{:S(2)}, u32[]{:S(2)}) collective-permute-start(f32[4,32,512]{2,1,0:T(8,128)S(1)} %copy-done), channel_id=1, source_target_pairs={{4,0},{8,4},{12,8},{5,1},{9,5},{13,9},{6,2},{10,6},{14,10},{7,3},{... | collective-permute-start | bytes 786440 | tf_op jit(solution)/shard_map/ppermute | solution.py:454
  14.0 0.0 copy-done.1
  14.0 1.3 %collective-permute-start.1 = (f32[4,32,512]{2,1,0:T(8,128)S(1)}, f32[4,32,512]{2,1,0:T(8,128)S(1)}, u32[]{:S(2)}, u32[]{:S(2)}) collective-permute-start(f32[4,32,512]{2,1,0:T(8,128)S(1)} %copy-done.1), channel_id=1, source_target_pairs={{4,0},{8,4},{12,8},{5,1},{9,5},{13,9},{6,2},{10,6},{14,10},{7,3},{... | collective-permute-start | bytes 786440 | tf_op jit(solution)/shard_map/ppermute | solution.py:455
  15.3 0.0 collective-permute-done.4.cross
  15.3 0.0 copy-start.3
  15.3 0.7 %copy-done.3 = f32[9,8,640]{2,1,0:T(8,128)} copy-done((f32[9,8,640]{2,1,0:T(8,128)}, f32[9,8,640]{2,1,0:T(8,128)S(1)}, u32[]{:S(2)}) %copy-start.3) | copy-done | bytes 184344
  16.0 1.7 %pack_rims.1 = (f32[152,128]{1,0:T(8,128)}, f32[72,128]{1,0:T(8,128)}) custom-call(f32[9,8,640]{2,1,0:T(8,128)} %copy-done.3, f32[9,32,128]{2,1,0:T(8,128)} %copy-done.2), custom_call_target="tpu_custom_call" | custom-call | flops 19456 | bytes 77824 | tf_op jit(solution)/shard_map/pack_rims/pallas_call | solution.py:182
  17.7 5.2 %collective-permute-start.6 = (f32[72,128]{1,0:T(8,128)}, f32[72,128]{1,0:T(8,128)S(1)}, u32[]{:S(2)}, u32[]{:S(2)}) collective-permute-start(f32[72,128]{1,0:T(8,128)} %get-tuple-element.5), channel_id=1, source_target_pairs={{0,4},{4,8},{8,12},{1,5},{5,9},{9,13},{2,6},{6,10},{10,14},{3,7},{... | collective-permute-start | bytes 110600 | tf_op jit(solution)/shard_map/ppermute | solution.py:464
  22.9 1.3 %collective-permute-start.5 = (f32[152,128]{1,0:T(8,128)}, f32[152,128]{1,0:T(8,128)S(1)}, u32[]{:S(2)}, u32[]{:S(2)}) collective-permute-start(f32[152,128]{1,0:T(8,128)} %get-tuple-element.4), channel_id=1, source_target_pairs={{4,0},{8,4},{12,8},{5,1},{9,5},{13,9},{6,2},{10,6},{14,10},{7,3},{... | collective-permute-start | bytes 233480 | tf_op jit(solution)/shard_map/ppermute | solution.py:463
  24.2 0.6 %pad_add_fusion.where_ref = s32[3]{0:T(128)} fusion(s32[1]{0:T(128)} %bitcast.2, s32[1]{0:T(128)} %bitcast.1, s32[1]{0:T(128)} %bitcast), kind=kLoop, calls=%fused_computation.1 | loop fusion | flops 6 | bytes 24 | tf_op jit(solution)/shard_map/stack | solution.py:451
  25.4 0.0 collective-permute-done.2.lows
  25.4 0.0 copy-start.4
  25.5 0.0 collective-permute-done.phi_up
  25.5 0.0 copy-start.5
  25.5 3.3 %collective-permute-done.1.sol_up = f32[4,32,512]{2,1,0:T(8,128)S(1)} collective-permute-done((f32[4,32,512]{2,1,0:T(8,128)S(1)}, f32[4,32,512]{2,1,0:T(8,128)S(1)}, u32[]{:S(2)}, u32[]{:S(2)}) %collective-permute-start.1) | collective-permute-done | bytes 262176 | tf_op jit(solution)/shard_map/ppermute | solution.py:455
  28.8 0.0 copy-start.6
  28.8 0.0 collective-permute-done.6.rim_up
  28.8 0.0 copy-start.8
  28.8 0.8 %collective-permute-done.5.rim_down = f32[152,128]{1,0:T(8,128)S(1)} collective-permute-done((f32[152,128]{1,0:T(8,128)}, f32[152,128]{1,0:T(8,128)S(1)}, u32[]{:S(2)}, u32[]{:S(2)}) %collective-permute-start.5) | collective-permute-done | bytes 77856 | tf_op jit(solution)/shard_map/ppermute | solution.py:463
  29.7 0.0 copy-done.4
  29.7 0.0 copy-done.5
  29.7 0.0 copy-done.6
  29.7 0.0 copy-done.8
  29.7 0.0 copy-start.7
  29.7 0.6 %copy-done.7 = f32[152,128]{1,0:T(8,128)} copy-done((f32[152,128]{1,0:T(8,128)}, f32[152,128]{1,0:T(8,128)S(1)}, u32[]{:S(2)}) %copy-start.7) | copy-done | bytes 77848
  30.3 8.6 %evolve.1 = (f32[4,32,512]{2,1,0:T(8,128)}, f32[4,32,512]{2,1,0:T(8,128)}) custom-call(s32[1]{0:T(128)S(6)} %copy.6.shift_ref, s32[3]{0:T(128)} %pad_add_fusion.where_ref, f32[4,32,512]{2,1,0:T(8,128)} %phi_in.1, f32[4,32,512]{2,1,0:T(8,128)} %sol_in.1, f32[4,32,512]{2,1,0:T(8,128)} %copy-done.5, f32[4,32,512]{2,1,0:T(8,128)} %copy-done.6, ...), custom_call_target="tpu_custom_call" | custom-call | flops 12582912 | bytes 50331648 | tf_op jit(solution)/shard_map/evolve/pallas_call | solution.py:419
  (1 shorter events, 0.0 us)
Async XLA Ops:
  2.3 1.7 %collective-permute-start.3 = (f32[9,32,128]{2,1,0:T(8,128)}, f32[9,32,128]{2,1,0:T(8,128)S(1)}, u32[]{:S(2)}, u32[]{:S(2)}) collective-permute-start(f32[9,32,128]{2,1,0:T(8,128)} %pack_sides.1), channel_id=1, source_target_pairs={{0,1},{1,0},{2,3},{3,2},{4,5},{5,4},{6,7},{7,6},{8,9},{9,8},{10,11... | collective-permute-start | bytes 442376 | tf_op jit(solution)/shard_map/ppermute | solution.py:441
  2.8 6.4 %slice-start = ((f32[4,32,512]{2,1,0:T(8,128)}), f32[2,32,512]{2,1,0:T(8,128)S(1)}, s32[]{:S(2)}) async-start(f32[4,32,512]{2,1,0:T(8,128)} %phi_in.1), calls=%async_computation | async-start | bytes 262144 | tf_op jit(solution)/shard_map/slice | solution.py:456
  2.8 6.4 %slice-start.1 = ((f32[4,32,512]{2,1,0:T(8,128)}), f32[2,32,512]{2,1,0:T(8,128)S(1)}, s32[]{:S(2)}) async-start(f32[4,32,512]{2,1,0:T(8,128)} %sol_in.1), calls=%async_computation.1 | async-start | bytes 262144 | tf_op jit(solution)/shard_map/slice | solution.py:456
  4.0 0.7 %copy-start.2 = (f32[9,32,128]{2,1,0:T(8,128)}, f32[9,32,128]{2,1,0:T(8,128)S(1)}, u32[]{:S(2)}) copy-start(f32[9,32,128]{2,1,0:T(8,128)S(1)} %collective-permute-done.3.side_a.side_b.side) | copy-start | bytes 442372
  6.3 6.4 %copy-start = (f32[4,32,512]{2,1,0:T(8,128)S(1)}, f32[4,32,512]{2,1,0:T(8,128)}, u32[]{:S(2)}) copy-start(f32[4,32,512]{2,1,0:T(8,128)} %phi_in.1) | copy-start | bytes 786436
  6.3 7.7 %copy-start.1 = (f32[4,32,512]{2,1,0:T(8,128)S(1)}, f32[4,32,512]{2,1,0:T(8,128)}, u32[]{:S(2)}) copy-start(f32[4,32,512]{2,1,0:T(8,128)} %sol_in.1) | copy-start | bytes 786436
  6.3 9.0 %collective-permute-start.4 = (f32[9,8,640]{2,1,0:T(8,128)}, f32[9,8,640]{2,1,0:T(8,128)S(1)}, u32[]{:S(2)}, u32[]{:S(2)}) collective-permute-start(f32[9,8,640]{2,1,0:T(8,128)} %pack_rows.1), channel_id=1, source_target_pairs={{0,2},{2,0},{1,3},{3,1},{4,6},{6,4},{5,7},{7,5},{8,10},{10,8},{9,1... | collective-permute-start | bytes 552968 | tf_op jit(solution)/shard_map/ppermute | solution.py:441
  9.2 16.3 %collective-permute-start.2 = (f32[4,32,512]{2,1,0:T(8,128)S(1)}, f32[4,32,512]{2,1,0:T(8,128)S(1)}, u32[]{:S(2)}, u32[]{:S(2)}) collective-permute-start(f32[4,32,512]{2,1,0:T(8,128)S(1)} %pad_maximum_fusion), channel_id=1, source_target_pairs={{0,4},{4,8},{8,12},{1,5},{5,9},{9,13},{2,6},{6,10},{10,14},{3,7},{... | collective-permute-start | bytes 786440 | tf_op jit(solution)/shard_map/ppermute | solution.py:457
  12.7 12.8 %collective-permute-start = (f32[4,32,512]{2,1,0:T(8,128)S(1)}, f32[4,32,512]{2,1,0:T(8,128)S(1)}, u32[]{:S(2)}, u32[]{:S(2)}) collective-permute-start(f32[4,32,512]{2,1,0:T(8,128)S(1)} %copy-done), channel_id=1, source_target_pairs={{4,0},{8,4},{12,8},{5,1},{9,5},{13,9},{6,2},{10,6},{14,10},{7,3},{... | collective-permute-start | bytes 786440 | tf_op jit(solution)/shard_map/ppermute | solution.py:454
  14.0 14.8 %collective-permute-start.1 = (f32[4,32,512]{2,1,0:T(8,128)S(1)}, f32[4,32,512]{2,1,0:T(8,128)S(1)}, u32[]{:S(2)}, u32[]{:S(2)}) collective-permute-start(f32[4,32,512]{2,1,0:T(8,128)S(1)} %copy-done.1), channel_id=1, source_target_pairs={{4,0},{8,4},{12,8},{5,1},{9,5},{13,9},{6,2},{10,6},{14,10},{7,3},{... | collective-permute-start | bytes 786440 | tf_op jit(solution)/shard_map/ppermute | solution.py:455
  15.3 0.7 %copy-start.3 = (f32[9,8,640]{2,1,0:T(8,128)}, f32[9,8,640]{2,1,0:T(8,128)S(1)}, u32[]{:S(2)}) copy-start(f32[9,8,640]{2,1,0:T(8,128)S(1)} %collective-permute-done.4.cross) | copy-start | bytes 552964
  17.7 11.1 %collective-permute-start.6 = (f32[72,128]{1,0:T(8,128)}, f32[72,128]{1,0:T(8,128)S(1)}, u32[]{:S(2)}, u32[]{:S(2)}) collective-permute-start(f32[72,128]{1,0:T(8,128)} %get-tuple-element.5), channel_id=1, source_target_pairs={{0,4},{4,8},{8,12},{1,5},{5,9},{9,13},{2,6},{6,10},{10,14},{3,7},{... | collective-permute-start | bytes 110600 | tf_op jit(solution)/shard_map/ppermute | solution.py:464
  22.9 6.8 %collective-permute-start.5 = (f32[152,128]{1,0:T(8,128)}, f32[152,128]{1,0:T(8,128)S(1)}, u32[]{:S(2)}, u32[]{:S(2)}) collective-permute-start(f32[152,128]{1,0:T(8,128)} %get-tuple-element.4), channel_id=1, source_target_pairs={{4,0},{8,4},{12,8},{5,1},{9,5},{13,9},{6,2},{10,6},{14,10},{7,3},{... | collective-permute-start | bytes 233480 | tf_op jit(solution)/shard_map/ppermute | solution.py:463
  25.4 4.2 %copy-start.4 = (f32[4,32,512]{2,1,0:T(8,128)}, f32[4,32,512]{2,1,0:T(8,128)S(1)}, u32[]{:S(2)}) copy-start(f32[4,32,512]{2,1,0:T(8,128)S(1)} %collective-permute-done.2.lows) | copy-start | bytes 786436
  25.5 4.2 %copy-start.5 = (f32[4,32,512]{2,1,0:T(8,128)}, f32[4,32,512]{2,1,0:T(8,128)S(1)}, u32[]{:S(2)}) copy-start(f32[4,32,512]{2,1,0:T(8,128)S(1)} %collective-permute-done.phi_up) | copy-start | bytes 786436
  28.8 0.8 %copy-start.6 = (f32[4,32,512]{2,1,0:T(8,128)}, f32[4,32,512]{2,1,0:T(8,128)S(1)}, u32[]{:S(2)}) copy-start(f32[4,32,512]{2,1,0:T(8,128)S(1)} %collective-permute-done.1.sol_up) | copy-start | bytes 786436
  28.8 0.8 %copy-start.8 = (f32[72,128]{1,0:T(8,128)}, f32[72,128]{1,0:T(8,128)S(1)}, u32[]{:S(2)}) copy-start(f32[72,128]{1,0:T(8,128)S(1)} %collective-permute-done.6.rim_up) | copy-start | bytes 110596
  29.7 0.6 %copy-start.7 = (f32[152,128]{1,0:T(8,128)}, f32[152,128]{1,0:T(8,128)S(1)}, u32[]{:S(2)}) copy-start(f32[152,128]{1,0:T(8,128)S(1)} %collective-permute-done.5.rim_down) | copy-start | bytes 233476

commit v2 on v0

v2 whole, which is shorter than its diff:
```python
import functools

import jax
import jax.numpy as jnp
from jax import lax
from jax.experimental import pallas as pl
from jax.experimental.pallas import tpu as pltpu
from jax.sharding import PartitionSpec as P


ITERS = 3
LANES = 128
SUBLANES = 8

partition = 0.15
coupling = 2.0
diffusion = 2.0
spacing_sq = 0.64
time_step = 0.025
gradient_scale = 1.2
drift_rate = 0.01
seed_levels = 1024.0

BELOW = ITERS - 1
ABOVE = ITERS + 1
RIMMED = ITERS
F32 = jnp.float32


def ring(size, by):
    return [(i, (i + by) % size) for i in range(size)]


def chain(size, by):
    return [(i, i + by) for i in range(size) if 0 <= i + by < size]


def lane_of(shape):
    return lax.broadcasted_iota(jnp.int32, shape, len(shape) - 1)


def row_of(shape):
    return lax.broadcasted_iota(jnp.int32, shape, len(shape) - 2)


def level(seed):
    return seed.astype(F32) / seed_levels - 1.0


VMEM = pl.BlockSpec(memory_space=pltpu.VMEM)
HBM = pl.BlockSpec(memory_space=pltpu.HBM)
SMEM = pl.BlockSpec(memory_space=pltpu.SMEM)
HALF = SUBLANES // 2
LANE_STEP = 2 * SUBLANES


def cost(count):
    return pl.CostEstimate(flops=count, bytes_accessed=4 * count, transcendentals=0)


def in_hbm(x):
    return pltpu.with_memory_space_constraint(x, pltpu.HBM)


def array(*shape):
    return jax.ShapeDtypeStruct(shape, F32)


def start_all(sems, pairs):
    copies = []
    for k, (source, target) in enumerate(pairs):
        copies.append(pltpu.make_async_copy(source, target, sems.at[k]))
        copies[-1].start()
    return copies


def guest_turns(k):
    return (HALF + k, HALF - k)


def edges_kernel(planes, phi, sol, seed, side, cross, lows, cols, rows, seed_cols, seed_rows, sems):
    depth, width = phi.shape[1:]
    left, right = pl.ds(0, LANES), pl.ds(width - LANES, LANES)
    first, last = pl.ds(0, SUBLANES), pl.ds(depth - SUBLANES, SUBLANES)
    kept = pl.ds(planes - BELOW, BELOW)
    copies = start_all(
        sems,
        [
            (phi.at[:, :, left], cols.at[0]),
            (phi.at[:, :, right], cols.at[1]),
            (sol.at[:, :, left], cols.at[2]),
            (sol.at[:, :, right], cols.at[3]),
            (seed.at[:, left], seed_cols.at[0]),
            (seed.at[:, right], seed_cols.at[1]),
            (phi.at[:, first, :], rows.at[0]),
            (phi.at[:, last, :], rows.at[1]),
            (sol.at[:, first, :], rows.at[2]),
            (sol.at[:, last, :], rows.at[3]),
            (seed.at[first, :], seed_rows.at[0]),
            (seed.at[last, :], seed_rows.at[1]),
            (phi.at[kept], lows.at[pl.ds(0, BELOW)]),
            (sol.at[kept], lows.at[pl.ds(BELOW, BELOW)]),
        ],
    )
    for copy in copies[:6]:
        copy.wait()
    keep = lane_of((depth, LANES)) < LANES // 2
    for k in range(planes):
        side[k] = jnp.where(keep, cols[0, k], cols[1, k])
        side[planes + k] = jnp.where(keep, cols[2, k], cols[3, k])
    side[2 * planes] = level(jnp.where(keep, seed_cols[0], seed_cols[1]))
    for copy in copies[6:]:
        copy.wait()
    rowid = row_of((SUBLANES, width))
    keep = rowid < HALF

    def edge(field, k):
        return jnp.where(keep, rows[2 * field, k], rows[2 * field + 1, k])

    for field in range(2):
        guest = edge(field, planes - 1)
        for k in range(planes - 1):
            cross[field * (planes - 1) + k] = host(rowid, edge(field, k), guest, k)
    cross[2 * (planes - 1)] = level(jnp.where(keep, seed_rows[0], seed_rows[1]))


def host(rowid, tile, guest, k):
    low, high = guest_turns(k)
    if k >= RIMMED:
        return tile
    tile = jnp.where(rowid == HALF - 1, pltpu.roll(guest, low, 0), tile)
    return jnp.where(rowid == HALF, pltpu.roll(guest, high, 0), tile)


def hosted(rowid, tiles):
    guest = None
    for k in range(RIMMED):
        low, high = guest_turns(k)
        part = pltpu.roll(tiles[k], SUBLANES - low, 0)
        guest = part if guest is None else jnp.where(rowid == SUBLANES - 1 - k, part, guest)
        part = pltpu.roll(tiles[k], SUBLANES - high, 0)
        guest = jnp.where(rowid == k, part, guest)
    return guest


def pack_edges(phi, sol, seed):
    planes, rows, cols = phi.shape
    return pl.pallas_call(
        functools.partial(edges_kernel, planes),
        out_shape=(
            array(2 * planes + 1, rows, LANES),
            array(2 * planes - 1, SUBLANES, cols),
            array(2 * BELOW, rows, cols),
        ),
        in_specs=[HBM, HBM, HBM],
        out_specs=(VMEM, VMEM, VMEM),
        scratch_shapes=[
            pltpu.VMEM((4, planes, rows, LANES), F32),
            pltpu.VMEM((4, planes, SUBLANES, cols), F32),
            pltpu.VMEM((2, rows, LANES), jnp.int32),
            pltpu.VMEM((2, SUBLANES, cols), jnp.int32),
            pltpu.SemaphoreType.DMA((14,)),
        ],
        cost_estimate=cost(phi.size),
        compiler_params=pltpu.CompilerParams(vmem_limit_bytes=4 << 20),
        name="pack_edges",
    )(*(in_hbm(x) for x in (phi, sol, seed)))


def rows_kernel(planes, main, side, out):
    width = main.shape[2]
    out[:, :, :width] = main[...]
    rowid = row_of((SUBLANES, LANES))
    keep = rowid < HALF
    depth = side.shape[1]

    def edge(entry):
        return jnp.where(keep, side[entry, :SUBLANES], side[entry, depth - SUBLANES :])

    for field in range(2):
        guest = edge((field + 1) * planes - 1)
        for k in range(planes - 1):
            tile = host(rowid, edge(field * planes + k), guest, k)
            out[field * (planes - 1) + k, :, width:] = tile
    out[2 * (planes - 1), :, width:] = edge(2 * planes)


def pack_rows(planes, main, side):
    count, _, cols = main.shape
    return pl.pallas_call(
        functools.partial(rows_kernel, planes),
        out_shape=array(count, SUBLANES, cols + LANES),
        in_specs=[VMEM, VMEM],
        out_specs=VMEM,
        cost_estimate=cost(main.size),
        compiler_params=pltpu.CompilerParams(vmem_limit_bytes=2 << 20),
        name="pack_rows",
    )(main, side)


def put_row_tile(out, place, tile):
    tiles = tile.shape[1] // LANES
    for t in range(tiles):
        start = (place * tiles + t) * SUBLANES
        out[start : start + SUBLANES, :] = tile[:, t * LANES : (t + 1) * LANES]


def get_row_tile(ref, place, tiles):
    return [
        ref[(place * tiles + t) * SUBLANES : (place * tiles + t + 1) * SUBLANES, :]
        for t in range(tiles)
    ]


def rims_kernel(planes, cross, side, down, up):
    other = planes - 1
    rowid = row_of(cross.shape[1:])
    lanes = lane_of(side.shape[1:])
    inner = (rowid == HALF - 1) | (rowid == HALF)
    middle = (rowid >= HALF - 2) & (rowid < HALF + 2)
    turn = lambda tile: pltpu.roll(tile, HALF, 0)

    def columns(entries):
        packed = side[entries[0]]
        for k, entry in enumerate(entries[1:], 1):
            moved = pltpu.roll(side[entry], k * LANE_STEP, 1)
            near = (lanes >= k * LANE_STEP - HALF) & (lanes < k * LANE_STEP + HALF)
            packed = jnp.where(near, moved, packed)
        return packed

    put_row_tile(down, 0, jnp.where(inner, turn(cross[2]), cross[0]))
    put_row_tile(down, 1, jnp.where(inner, turn(cross[other + 2]), cross[other]))
    put_row_tile(down, 2, jnp.where(middle, turn(cross[other + 1]), cross[1]))
    start = down.shape[0] - side.shape[1]
    down[start:, :] = columns([0, planes, 1, planes + 1, 2, planes + 2])
    put_row_tile(up, 0, jnp.where(inner, cross[other], turn(cross[0])))
    start = up.shape[0] - side.shape[1]
    up[start:, :] = columns([planes - 1, 2 * planes - 1])


def pack_rims(planes, cross, side):
    tiles = cross.shape[2] // LANES
    rows = side.shape[1]
    down = array(3 * tiles * SUBLANES + rows, LANES)
    up = array(tiles * SUBLANES + rows, LANES)
    return pl.pallas_call(
        functools.partial(rims_kernel, planes),
        out_shape=(down, up),
        in_specs=[VMEM, VMEM],
        out_specs=(VMEM, VMEM),
        cost_estimate=cost(down.size),
        compiler_params=pltpu.CompilerParams(vmem_limit_bytes=2 << 20),
        name="pack_rims",
    )(cross, side)


def mobility(phi):
    return 1.0 - jnp.clip(phi, -1.0, 1.0)


class Field:
    def __init__(self, phi, sol, mob, planes):
        self.phi, self.sol, self.mob = phi, sol, mob
        self.planes = planes
        self.tiles = phi.shape[1]
        self.rows = phi.shape[2] - 2 * SUBLANES
        self.base = BELOW
        self.top = BELOW + planes

    def put(self, e, t, at, p, u):
        self.phi[e, t, at, :] = p
        self.sol[e, t, at, :] = u
        self.mob[e, t, at, :] = mobility(p)

    def put_block(self, e, phi, sol, k, j):
        for t in range(self.tiles - 1):
            lanes = slice(t * LANES, (t + 1) * LANES)
            at = slice(SUBLANES, SUBLANES + self.rows)
            self.put(e, t, at, phi[k, :, lanes], sol[j, :, lanes])

    def put_columns(self, e, p, u):
        self.put(e, self.tiles - 1, slice(SUBLANES, SUBLANES + self.rows), p, u)

    def put_rows(self, e, p, u):
        for t in range(self.tiles):
            for start in (0, SUBLANES + self.rows):
                self.put(e, t, slice(start, start + SUBLANES), p[t], u[t])


def ends(step, shift, field, e):
    grow_index = lax.axis_index("grow")
    at_bottom = grow_index == 0
    at_top = grow_index == lax.axis_size("grow") - 1
    moved = shift < step
    low_end = jnp.where(moved, field.base + 1, field.base)
    high_end = jnp.where(moved, field.top, field.top - 1)
    lower = jnp.where(at_bottom & (e == low_end), e, e - 1)
    upper = jnp.where(at_top & (e == high_end), e, e + 1)
    return lower, upper


def step_plane(step, shift, source, e, halo, write):
    lower, upper = ends(step, shift, source, e)
    planes = source.planes
    grid_planes = planes * lax.axis_size("grow")
    height = (lax.axis_index("grow") * planes + e - source.base).astype(F32)
    height = jnp.broadcast_to(height, (SUBLANES, LANES))
    temper = gradient_scale * ((height + 0.5) * (1.0 / grid_planes) - 0.5) - drift_rate * step
    pace = time_step / (1.0 - (1.0 - partition) * temper)
    kappa = 0.25 * diffusion * time_step / spacing_sq
    pull = pace * (1.0 / spacing_sq)
    drive = pace * coupling
    rest = pull * 6.0
    tiles = source.tiles
    lanes = lane_of((SUBLANES, LANES))
    heads = lanes == 0
    tails = lanes == LANES - 1
    rows = source.rows + 2 * halo
    outputs = tiles if halo else tiles - 1
    for r in range(-(-rows // SUBLANES)):
        start = SUBLANES - halo + r * SUBLANES

        def load(ref, t, plane=e, by=0):
            return ref[plane, t, start + by : start + by + SUBLANES, :]

        def after(values, t):
            return pltpu.roll(jnp.where(heads, values[(t + 1) % tiles], values[t]), LANES - 1, 1)

        def before(values, t):
            return pltpu.roll(jnp.where(tails, values[t - 1], values[t]), 1, 1)

        p_all = [load(source.phi, t) for t in range(tiles)]
        u_all = [load(source.sol, t) for t in range(tiles)]
        m_all = [load(source.mob, t) for t in range(tiles)]
        flux = [
            (m_all[t] + after(m_all, t)) * (after(u_all, t) - u_all[t]) for t in range(tiles)
        ]
        for t in range(outputs):
            p, u, m = p_all[t], u_all[t], m_all[t]
            total = after(p_all, t) + before(p_all, t)
            flow = flux[t] - before(flux, t)
            for where in (dict(by=-1), dict(by=1), dict(plane=lower), dict(plane=upper)):
                total = total + load(source.phi, t, **where)
                other = load(source.sol, t, **where)
                flow = flow + (m + load(source.mob, t, **where)) * (other - u)
            well = 1.0 - p * p
            gain = pull * total + p * (pace * well - rest) - drive * (well * well) * (u + temper)
            weight = partition / kappa + (0.5 * (1.0 - partition) / kappa) * m
            change = flow + (0.5 / kappa + (0.5 * (1.0 - partition) / kappa) * u) * gain
            write(e, t, slice(start, start + SUBLANES), p + gain, u + change / weight)


def early_kernel(planes, shift_ref, phi, sol, phi_up, sol_up, side, cross, *rest):
    first = Field(*rest[:3], planes)
    second = Field(*rest[3:6], planes)
    own_phi, own_sol, sems = rest[6:]
    base, top, tiles = first.base, first.top, first.tiles
    copies = start_all(sems, [(phi, own_phi), (sol, own_sol)])
    rowid = row_of((SUBLANES, LANES))
    cut = lambda t: slice(t * LANES, (t + 1) * LANES)
    other = planes - 1
    for k in range(planes):
        first.put_columns(base + k, side[k], side[planes + k])
        if k < other:
            p = [cross[k, :, cut(t)] for t in range(tiles)]
            u = [cross[other + k, :, cut(t)] for t in range(tiles)]
        else:
            p, u = [
                [
                    hosted(rowid, [cross[f * other + j, :, cut(t)] for j in range(RIMMED)])
                    for t in range(tiles)
                ]
                for f in range(2)
            ]
        first.put_rows(base + k, p, u)
    for k in range(ABOVE):
        first.put_block(top + k, phi_up, sol_up, k, k)
    for copy in copies:
        copy.wait()
    for k in range(planes):
        first.put_block(base + k, own_phi, own_sol, k, k)

    @pl.loop(base + 1, top - 1)
    def _(e):
        step_plane(0, shift_ref[0], first, e, 2, second.put)


def late_kernel(planes, shift_ref, lows, side, cross, rim_down, rim_up, seed, *rest):
    phi_out, sol_out = rest[6:8]
    first = Field(*rest[8:11], planes)
    second = Field(*rest[11:14], planes)
    levels, phi_buf, sol_buf, sems = rest[14:]
    base, top, tiles, rows = first.base, first.top, first.tiles, first.rows
    shift = shift_ref[0]
    at_top = lax.axis_index("grow") == lax.axis_size("grow") - 1
    fetch = pltpu.make_async_copy(seed, levels, sems.at[0])
    fetch.start()
    turn = lambda group: [pltpu.roll(tile, HALF, 0) for tile in group]
    for k in range(BELOW):
        first.put_block(k, lows, lows, k, BELOW + k)
    p = get_row_tile(rim_down, 0, tiles)
    u = get_row_tile(rim_down, 1, tiles)
    first.put_rows(top, p, u)
    first.put_rows(top + 2, turn(p), turn(u))
    p = get_row_tile(rim_down, 2, tiles)
    first.put_rows(top + 1, p, turn(p))
    p = get_row_tile(rim_up, 0, tiles)
    first.put_rows(base - 1, p, turn(p))

    def spread(packed, k):
        return pltpu.roll(packed, LANES - k * LANE_STEP, 1) if k else packed

    packed = rim_down[rim_down.shape[0] - rows :, :]
    for k in range(RIMMED):
        first.put_columns(top + k, spread(packed, 2 * k), spread(packed, 2 * k + 1))
    packed = rim_up[rim_up.shape[0] - rows :, :]
    first.put_columns(base - 1, packed, spread(packed, 1))
    fetch.wait()

    def bring_top(field):
        def fill(t, at, value):
            field.put(top, t, at, jnp.full(value.shape, -1.0, F32), value)

        body = slice(SUBLANES, SUBLANES + rows)
        for t in range(tiles - 1):
            fill(t, body, level(levels[:, t * LANES : (t + 1) * LANES]))
        fill(tiles - 1, body, side[2 * planes])
        for t in range(tiles):
            value = cross[2 * (planes - 1), :, t * LANES : (t + 1) * LANES]
            fill(t, slice(0, SUBLANES), value)
            fill(t, slice(SUBLANES + rows, 2 * SUBLANES + rows), value)

    @pl.loop(0, 4)
    def _(k):
        e = jnp.where(k == 0, base, top - 2 + k)
        step_plane(0, shift, first, e, 2, second.put)

    @pl.loop(0, 2)
    def _(k):
        step_plane(0, shift, first, jnp.where(k == 0, base - 1, top + 2), 0, second.put)

    @pl.when(at_top & (shift == 0))
    def _():
        bring_top(second)

    @pl.loop(base + 1, top + 1)
    def _(e):
        step_plane(1, shift, second, e, 1, first.put)

    @pl.loop(0, 2)
    def _(k):
        step_plane(1, shift, second, jnp.where(k == 0, base, top + 1), 0, first.put)

    @pl.when(at_top & (shift == 1))
    def _():
        bring_top(first)

    def out_copy(which, j):
        buf, out = ((phi_buf, phi_out), (sol_buf, sol_out))[which]
        return pltpu.make_async_copy(buf.at[j], out.at[j], sems.at[1 + which * planes + j])

    @pl.loop(0, planes)
    def _(j):
        def finish(e, t, at, p, u):
            place = (j, slice(at.start - SUBLANES, at.stop - SUBLANES), slice(t * LANES, (t + 1) * LANES))
            phi_buf[place] = p
            sol_buf[place] = u

        step_plane(2, shift, first, j + base + 1, 0, finish)
        out_copy(0, j).start()
        out_copy(1, j).start()

    for j in range(planes):
        out_copy(0, j).wait()
        out_copy(1, j).wait()


def early(shift, phi, sol, phi_up, sol_up, side, cross):
    planes, rows, cols = phi.shape
    state = array(planes + BELOW + ABOVE, cols // LANES + 1, rows + 2 * SUBLANES, LANES)
    return pl.pallas_call(
        functools.partial(early_kernel, planes),
        out_shape=(state,) * 6,
        in_specs=[SMEM, HBM, HBM] + [VMEM] * 4,
        out_specs=(VMEM,) * 6,
        scratch_shapes=[
            pltpu.VMEM(phi.shape, F32),
            pltpu.VMEM(phi.shape, F32),
            pltpu.SemaphoreType.DMA((2,)),
        ],
        cost_estimate=cost(64 * phi.size),
        compiler_params=pltpu.CompilerParams(vmem_limit_bytes=12 << 20),
        name="early",
    )(shift, phi, sol, phi_up, sol_up, side, cross)


def late(shift, lows, side, cross, down, up, seed, state, shape):
    planes = shape[0]
    kept = tuple(jax.ShapeDtypeStruct(s.shape, s.dtype) for s in state)
    out = pl.pallas_call(
        functools.partial(late_kernel, planes),
        out_shape=(array(*shape), array(*shape)) + kept,
        in_specs=[SMEM] + [VMEM] * 5 + [HBM] + [VMEM] * 6,
        out_specs=(HBM, HBM) + (VMEM,) * 6,
        input_output_aliases={7 + k: 2 + k for k in range(6)},
        scratch_shapes=[
            pltpu.VMEM(seed.shape, jnp.int32),
            pltpu.VMEM(shape, F32),
            pltpu.VMEM(shape, F32),
            pltpu.SemaphoreType.DMA((1 + 2 * planes,)),
        ],
        cost_estimate=cost(3 * 64 * state[0].size),
        compiler_params=pltpu.CompilerParams(vmem_limit_bytes=12 << 20),
        name="late",
    )(shift, lows, side, cross, down, up, seed, *state)
    return out[0], out[1]


def swap_edges(message, axis, keep):
    size = lax.axis_size(axis)
    if size <= 2:
        return lax.ppermute(message, axis, ring(size, 1))
    after = lax.ppermute(message, axis, ring(size, -1))
    before = lax.ppermute(message, axis, ring(size, 1))
    return jnp.where(keep, after, before)


def steps(phi, sol, shift_step, seed):
    planes = phi.shape[0]
    size = lax.axis_size("grow")
    fall = chain(size, -1)
    rise = chain(size, 1)
    phi_up = lax.ppermute(phi, "grow", fall)
    sol_up = lax.ppermute(sol, "grow", fall)
    side, cross, lows = pack_edges(phi, sol, seed)
    lows = lax.ppermute(lows, "grow", rise)
    side = swap_edges(side, "side", lane_of(side.shape) < LANES // 2)
    cross = pack_rows(planes, cross, side)
    rowid = row_of(cross.shape)
    cross = swap_edges(cross, "cross", (rowid < HALF - 1) | (rowid == HALF))
    down, up = pack_rims(planes, cross, side)
    down = lax.ppermute(down, "grow", fall)
    up = lax.ppermute(up, "grow", rise)
    state = early(shift_step, phi, sol, phi_up, sol_up, side, cross)
    return late(shift_step, lows, side, cross, down, up, seed, state, phi.shape)


def solution(mesh):
    return jax.shard_map(
        steps,
        mesh=mesh,
        in_specs=(
            P(("groups", "grow"), "cross", "side"),
            P(("groups", "grow"), "cross", "side"),
            P("groups"),
            P(("groups", "cross"), "side"),
        ),
        out_specs=(P(("groups", "grow"), "cross", "side"), P(("groups", "grow"), "cross", "side")),
        check_vma=False,
    )
```

time: 63.2 us -> 30.1 us (0.48)
  waiting for transfers between devices: 26.9 us -> 4.01 us
  starting transfers between devices: 27 us -> 16.7 us
  Pallas kernels: 0 us -> 7.64 us
  other arithmetic: 7.19 us -> 0 us
    ppermute x20 -> x7, waiting for transfers between devices: 26.9 us -> 4.01 us  [the longest x2 3.94 us: swap_edges(): return lax.ppermute(message, axis, ring(size, 1))]
    ppermute x20 -> x7, starting transfers between devices: 27 us -> 16.7 us  [the longest x1 5.77 us: steps(): lows = lax.ppermute(lows, 'grow', rise)]
    pallas_call x0 -> x5, Pallas kernels: none -> 7.64 us  [the longest x1 5.25 us: late(): pl.pallas_call(functools.partial(late_kernel, planes), out_shape=(array(*...]
    add x4 -> x0, other arithmetic: 4.1 us -> none  [the longest x2 2.72 us: advance(): solutes + time_step * solute_rate]
    another operation x9 -> x0, other arithmetic: 2.36 us -> none  [the longest x6 1.39 us: advance(): jnp.stack([phases + time_step * growth_rate, solutes + time_step * solute...]
  transfers between devices with their start and end apart: 20 -> 7, of which waited for: 10 -> 2; matrix products, arithmetic and copies ran while one was open for 1% -> 0% of each run, Pallas kernels for 0% -> 3%
where the time goes in v2:
time: 30.1 us; the launch traced here: 29.8 us
  starting transfers between devices  16.7 us (55%)
  Pallas kernels  7.64 us (25%)
  waiting for transfers between devices  4.01 us (13%)
  between operations  1.42 us (5%)
    ppermute x1, starting transfers between devices, steps(): lows = lax.ppermute(lows, 'grow', rise)  5.77 us
    pallas_call x1, Pallas kernels, late(): pl.pallas_call(functools.partial(late_kernel, planes), out_shape=(array(*...  5.25 us
    ppermute x1, starting transfers between devices, steps(): up = lax.ppermute(up, 'grow', rise)  4.55 us
    ppermute x2, waiting for transfers between devices, swap_edges(): return lax.ppermute(message, axis, ring(size, 1))  3.94 us
    ppermute x2, starting transfers between devices, swap_edges(): return lax.ppermute(message, axis, ring(size, 1))  2.55 us
    pallas_call x1, Pallas kernels, pack_edges(): pl.pallas_call(functools.partial(edges_kernel, planes), out_shape=(array(...  1.44 us
    ppermute x1, starting transfers between devices, steps(): sol_up = lax.ppermute(sol, 'grow', fall)  1.29 us
    ppermute x1, starting transfers between devices, steps(): down = lax.ppermute(down, 'grow', fall)  1.29 us
  transfers between devices with their start and end apart: 7, of which 2 were waited for; matrix products, arithmetic and copies ran while one was open for 0% of the time, Pallas kernels for 3%

profile of v2, /device:TPU:0, one launch (start us, length us, event | category | flops | bytes accessed | tf_op | source)
XLA Modules:
  0.0 29.8 jit_solution(7545251982832732007)
XLA Ops:
  0.6 0.0 copy-start.1
  0.6 0.0 copy-start
  0.7 0.0 copy-start.2
  0.7 1.4 %pack_edges.1 = (f32[9,32,128]{2,1,0:T(8,128)S(1)}, f32[7,8,512]{2,1,0:T(8,128)S(1)}, f32[4,32,512]{2,1,0:T(8,128)S(1)}) custom-call(f32[4,32,512]{2,1,0:T(8,128)} %phi.3, f32[4,32,512]{2,1,0:T(8,128)} %sol.3, s32[32,512]{1,0:T(8,128)} %seed.3), custom_call_target="tpu_custom_call" | custom-call | flops 65536 | bytes 262144 | tf_op jit(solution)/shard_map/pack_edges/pallas_call | solution.py:148
  2.1 0.6 %collective-permute-start.1 = (f32[9,32,128]{2,1,0:T(8,128)S(1)}, f32[9,32,128]{2,1,0:T(8,128)S(1)}, u32[]{:S(2)}, u32[]{:S(2)}) collective-permute-start(f32[9,32,128]{2,1,0:T(8,128)S(1)} %get-tuple-element.16), channel_id=1, source_target_pairs={{0,1},{1,0},{2,3},{3,2},{4,5},{5,4},{6,7},{7,6},{8,9},{9,8},{10,11... | collective-permute-start | bytes 442376 | tf_op jit(solution)/shard_map/ppermute | solution.py:522
  2.7 1.3 %collective-permute-start.5 = (f32[4,32,512]{2,1,0:T(8,128)}, f32[4,32,512]{2,1,0:T(8,128)S(1)}, u32[]{:S(2)}, u32[]{:S(2)}) collective-permute-start(f32[4,32,512]{2,1,0:T(8,128)} %phi.3), channel_id=1, source_target_pairs={{4,0},{8,4},{12,8},{5,1},{9,5},{13,9},{6,2},{10,6},{14,10},{7,3},{... | collective-permute-start | bytes 786440 | tf_op jit(solution)/shard_map/ppermute | solution.py:533
  4.0 1.3 %collective-permute-start.6 = (f32[4,32,512]{2,1,0:T(8,128)}, f32[4,32,512]{2,1,0:T(8,128)S(1)}, u32[]{:S(2)}, u32[]{:S(2)}) collective-permute-start(f32[4,32,512]{2,1,0:T(8,128)} %sol.3), channel_id=1, source_target_pairs={{4,0},{8,4},{12,8},{5,1},{9,5},{13,9},{6,2},{10,6},{14,10},{7,3},{... | collective-permute-start | bytes 786440 | tf_op jit(solution)/shard_map/ppermute | solution.py:534
  5.3 5.8 %collective-permute-start = (f32[4,32,512]{2,1,0:T(8,128)S(1)}, f32[4,32,512]{2,1,0:T(8,128)S(1)}, u32[]{:S(2)}, u32[]{:S(2)}) collective-permute-start(f32[4,32,512]{2,1,0:T(8,128)S(1)} %get-tuple-element.15), channel_id=1, source_target_pairs={{0,4},{4,8},{8,12},{1,5},{5,9},{9,13},{2,6},{6,10},{10,14},{3,7},{... | collective-permute-start | bytes 786440 | tf_op jit(solution)/shard_map/ppermute | solution.py:536
  11.0 0.0 collective-permute-done.1.side
  11.1 2.0 %collective-permute-start.2 = (f32[7,8,640]{2,1,0:T(8,128)S(1)}, f32[7,8,640]{2,1,0:T(8,128)S(1)}, u32[]{:S(2)}, u32[]{:S(2)}) collective-permute-start(f32[7,8,640]{2,1,0:T(8,128)S(1)} %pack_rows.1), channel_id=1, source_target_pairs={{0,2},{2,0},{1,3},{3,1},{4,6},{6,4},{5,7},{7,5},{8,10},{10,8},{9,1... | collective-permute-start | bytes 430088 | tf_op jit(solution)/shard_map/ppermute | solution.py:522
  13.1 3.9 %collective-permute-done.2.cross = f32[7,8,640]{2,1,0:T(8,128)S(1)} collective-permute-done((f32[7,8,640]{2,1,0:T(8,128)S(1)}, f32[7,8,640]{2,1,0:T(8,128)S(1)}, u32[]{:S(2)}, u32[]{:S(2)}) %collective-permute-start.2) | collective-permute-done | bytes 143392 | tf_op jit(solution)/shard_map/ppermute | solution.py:522
  17.0 0.1 pack_rims.1
  17.1 1.3 %collective-permute-start.3 = (f32[152,128]{1,0:T(8,128)S(1)}, f32[152,128]{1,0:T(8,128)S(1)}, u32[]{:S(2)}, u32[]{:S(2)}) collective-permute-start(f32[152,128]{1,0:T(8,128)S(1)} %get-tuple-element.18), channel_id=1, source_target_pairs={{4,0},{8,4},{12,8},{5,1},{9,5},{13,9},{6,2},{10,6},{14,10},{7,3},{... | collective-permute-start | bytes 233480 | tf_op jit(solution)/shard_map/ppermute | solution.py:542
  18.4 4.5 %collective-permute-start.4 = (f32[72,128]{1,0:T(8,128)S(1)}, f32[72,128]{1,0:T(8,128)S(1)}, u32[]{:S(2)}, u32[]{:S(2)}) collective-permute-start(f32[72,128]{1,0:T(8,128)S(1)} %get-tuple-element.19), channel_id=1, source_target_pairs={{0,4},{4,8},{8,12},{1,5},{5,9},{9,13},{2,6},{6,10},{10,14},{3,7},{... | collective-permute-start | bytes 110600 | tf_op jit(solution)/shard_map/ppermute | solution.py:543
  23.6 0.0 collective-permute-done.5.phi_up
  23.6 0.0 collective-permute-done.6.sol_up
  23.6 0.0 copy-done.1
  23.6 0.0 copy-done
  23.6 0.9 %early.1 = (f32[10,5,48,128]{3,2,1,0:T(8,128)S(1)}, f32[10,5,48,128]{3,2,1,0:T(8,128)S(1)}, f32[10,5,48,128]{3,2,1,0:T(8,128)S(1)}, f32[10,5,48,128]{3,2,1,0:T(8...) custom-call(s32[1]{0:T(128)S(6)} %copy.18.shift_ref, f32[4,32,512]{2,1,0:T(8,128)S(1)} %copy-done, ...), custom_call_target="tpu_custom_call" | custom-call | flops 4194304 | bytes 16777216 | tf_op jit(solution)/shard_map/early/pallas_call | solution.py:481
  24.5 0.0 collective-permute-done.lows
  24.5 0.1 collective-permute-done.4.rim_up
  24.6 0.0 collective-permute-done.3.rim_down
  24.6 0.0 copy-done.2
  24.6 5.3 %late.1 = (f32[4,32,512]{2,1,0:T(8,128)}, f32[4,32,512]{2,1,0:T(8,128)}, f32[10,5,48,128]{3,2,1,0:T(8,128)S(1)}, f32[10,5,48,128]{3,2,1,0:T(8,128)S(1)}, f32[10,...) custom-call(s32[1]{0:T(128)S(6)} %copy.18.shift_ref, ...), custom_call_target="tpu_custom_call", output_to_operand_aliasing={{2}: (7, {}), {3}: (8, {}), {4}: (9, {}), {5}: (10, {}), {6... | custom-call | flops 58982400 | bytes 235929600 | tf_op jit(solution)/shard_map/late/pallas_call | solution.py:500
  (1 shorter events, 0.0 us)
Async XLA Ops:
  0.6 23.0 %copy-start.1 = (f32[4,32,512]{2,1,0:T(8,128)S(1)}, f32[4,32,512]{2,1,0:T(8,128)}, u32[]{:S(2)}) copy-start(f32[4,32,512]{2,1,0:T(8,128)} %sol.3) | copy-start | bytes 786436
  0.6 23.0 %copy-start = (f32[4,32,512]{2,1,0:T(8,128)S(1)}, f32[4,32,512]{2,1,0:T(8,128)}, u32[]{:S(2)}) copy-start(f32[4,32,512]{2,1,0:T(8,128)} %phi.3) | copy-start | bytes 786436
  0.7 23.9 %copy-start.2 = (s32[32,512]{1,0:T(8,128)S(1)}, s32[32,512]{1,0:T(8,128)}, u32[]{:S(2)}) copy-start(s32[32,512]{1,0:T(8,128)} %seed.3) | copy-start | bytes 196612
  2.1 8.9 %collective-permute-start.1 = (f32[9,32,128]{2,1,0:T(8,128)S(1)}, f32[9,32,128]{2,1,0:T(8,128)S(1)}, u32[]{:S(2)}, u32[]{:S(2)}) collective-permute-start(f32[9,32,128]{2,1,0:T(8,128)S(1)} %get-tuple-element.16), channel_id=1, source_target_pairs={{0,1},{1,0},{2,3},{3,2},{4,5},{5,4},{6,7},{7,6},{8,9},{9,8},{10,11... | collective-permute-start | bytes 442376 | tf_op jit(solution)/shard_map/ppermute | solution.py:522
  2.7 20.9 %collective-permute-start.5 = (f32[4,32,512]{2,1,0:T(8,128)}, f32[4,32,512]{2,1,0:T(8,128)S(1)}, u32[]{:S(2)}, u32[]{:S(2)}) collective-permute-start(f32[4,32,512]{2,1,0:T(8,128)} %phi.3), channel_id=1, source_target_pairs={{4,0},{8,4},{12,8},{5,1},{9,5},{13,9},{6,2},{10,6},{14,10},{7,3},{... | collective-permute-start | bytes 786440 | tf_op jit(solution)/shard_map/ppermute | solution.py:533
  4.0 19.7 %collective-permute-start.6 = (f32[4,32,512]{2,1,0:T(8,128)}, f32[4,32,512]{2,1,0:T(8,128)S(1)}, u32[]{:S(2)}, u32[]{:S(2)}) collective-permute-start(f32[4,32,512]{2,1,0:T(8,128)} %sol.3), channel_id=1, source_target_pairs={{4,0},{8,4},{12,8},{5,1},{9,5},{13,9},{6,2},{10,6},{14,10},{7,3},{... | collective-permute-start | bytes 786440 | tf_op jit(solution)/shard_map/ppermute | solution.py:534
  5.3 19.2 %collective-permute-start = (f32[4,32,512]{2,1,0:T(8,128)S(1)}, f32[4,32,512]{2,1,0:T(8,128)S(1)}, u32[]{:S(2)}, u32[]{:S(2)}) collective-permute-start(f32[4,32,512]{2,1,0:T(8,128)S(1)} %get-tuple-element.15), channel_id=1, source_target_pairs={{0,4},{4,8},{8,12},{1,5},{5,9},{9,13},{2,6},{6,10},{10,14},{3,7},{... | collective-permute-start | bytes 786440 | tf_op jit(solution)/shard_map/ppermute | solution.py:536
  11.1 5.9 %collective-permute-start.2 = (f32[7,8,640]{2,1,0:T(8,128)S(1)}, f32[7,8,640]{2,1,0:T(8,128)S(1)}, u32[]{:S(2)}, u32[]{:S(2)}) collective-permute-start(f32[7,8,640]{2,1,0:T(8,128)S(1)} %pack_rows.1), channel_id=1, source_target_pairs={{0,2},{2,0},{1,3},{3,1},{4,6},{6,4},{5,7},{7,5},{8,10},{10,8},{9,1... | collective-permute-start | bytes 430088 | tf_op jit(solution)/shard_map/ppermute | solution.py:522
  17.1 7.5 %collective-permute-start.3 = (f32[152,128]{1,0:T(8,128)S(1)}, f32[152,128]{1,0:T(8,128)S(1)}, u32[]{:S(2)}, u32[]{:S(2)}) collective-permute-start(f32[152,128]{1,0:T(8,128)S(1)} %get-tuple-element.18), channel_id=1, source_target_pairs={{4,0},{8,4},{12,8},{5,1},{9,5},{13,9},{6,2},{10,6},{14,10},{7,3},{... | collective-permute-start | bytes 233480 | tf_op jit(solution)/shard_map/ppermute | solution.py:542
  18.4 6.2 %collective-permute-start.4 = (f32[72,128]{1,0:T(8,128)S(1)}, f32[72,128]{1,0:T(8,128)S(1)}, u32[]{:S(2)}, u32[]{:S(2)}) collective-permute-start(f32[72,128]{1,0:T(8,128)S(1)} %get-tuple-element.19), channel_id=1, source_target_pairs={{0,4},{4,8},{8,12},{1,5},{5,9},{9,13},{2,6},{6,10},{10,14},{3,7},{... | collective-permute-start | bytes 110600 | tf_op jit(solution)/shard_map/ppermute | solution.py:543

commit v3 on v2

--- a/solution.py
+++ b/solution.py
@@ -35,6 +35,16 @@
     return [(i, i + by) for i in range(size) if 0 <= i + by < size]
 
 
+def two_way(size, lanes, even_by):
+    pairs = []
+    for g in range(size):
+        for c in range(lanes):
+            target = g + (even_by if c % 2 == 0 else -even_by)
+            inside = 0 <= target < size
+            pairs.append((g * lanes + c, target * lanes + c if inside else g * lanes + (c ^ 1)))
+    return pairs
+
+
 def lane_of(shape):
     return lax.broadcasted_iota(jnp.int32, shape, len(shape) - 1)
 
@@ -78,10 +88,15 @@
     return (HALF + k, HALF - k)
 
 
-def edges_kernel(planes, phi, sol, seed, side, cross, lows, cols, rows, seed_cols, seed_rows, sems):
+def odd_core():
+    return lax.axis_index("side") % 2 == 1
+
+
+def edges_kernel(planes, phi, sol, seed, side, cross, bulk_a, bulk_b, cols, rows, seed_cols, seed_rows, sems):
     depth, width = phi.shape[1:]
     left, right = pl.ds(0, LANES), pl.ds(width - LANES, LANES)
     first, last = pl.ds(0, SUBLANES), pl.ds(depth - SUBLANES, SUBLANES)
+    every = slice(None)
     kept = pl.ds(planes - BELOW, BELOW)
     copies = start_all(
         sems,
@@ -98,10 +113,21 @@
             (sol.at[:, last, :], rows.at[3]),
             (seed.at[first, :], seed_rows.at[0]),
             (seed.at[last, :], seed_rows.at[1]),
-            (phi.at[kept], lows.at[pl.ds(0, BELOW)]),
-            (sol.at[kept], lows.at[pl.ds(BELOW, BELOW)]),
         ],
     )
+
+    def fill(fall, rise):
+        low, high = pl.ds(0, BELOW), pl.ds(BELOW, BELOW)
+        start_all(sems.at[pl.ds(12, 3)], [(phi, fall), (phi.at[kept], rise.at[low]), (sol.at[kept], rise.at[high])])
+
+    @pl.when(jnp.logical_not(odd_core()))
+    def _():
+        fill(bulk_a, bulk_b)
+
+    @pl.when(odd_core())
+    def _():
+        fill(bulk_b, bulk_a)
+
     for copy in copies[:6]:
         copy.wait()
     keep = lane_of((depth, LANES)) < LANES // 2
@@ -122,6 +148,10 @@
         for k in range(planes - 1):
             cross[field * (planes - 1) + k] = host(rowid, edge(field, k), guest, k)
     cross[2 * (planes - 1)] = level(jnp.where(keep, seed_rows[0], seed_rows[1]))
+    pltpu.make_async_copy(phi, bulk_a, sems.at[12]).wait()
+    for k in range(2):
+        part = bulk_b.at[pl.ds(k * BELOW, BELOW)]
+        pltpu.make_async_copy(phi.at[kept], part, sems.at[13 + k]).wait()
 
 
 def host(rowid, tile, guest, k):
@@ -150,16 +180,17 @@
         out_shape=(
             array(2 * planes + 1, rows, LANES),
             array(2 * planes - 1, SUBLANES, cols),
-            array(2 * BELOW, rows, cols),
+            array(*phi.shape),
+            array(*phi.shape),
         ),
         in_specs=[HBM, HBM, HBM],
-        out_specs=(VMEM, VMEM, VMEM),
+        out_specs=(VMEM,) * 4,
         scratch_shapes=[
             pltpu.VMEM((4, planes, rows, LANES), F32),
             pltpu.VMEM((4, planes, SUBLANES, cols), F32),
             pltpu.VMEM((2, rows, LANES), jnp.int32),
             pltpu.VMEM((2, SUBLANES, cols), jnp.int32),
-            pltpu.SemaphoreType.DMA((14,)),
+            pltpu.SemaphoreType.DMA((15,)),
         ],
         cost_estimate=cost(phi.size),
         compiler_params=pltpu.CompilerParams(vmem_limit_bytes=4 << 20),
@@ -212,13 +243,14 @@
     ]
 
 
-def rims_kernel(planes, cross, side, down, up):
+def rims_kernel(planes, cross, side, rim_a, rim_b):
     other = planes - 1
     rowid = row_of(cross.shape[1:])
     lanes = lane_of(side.shape[1:])
     inner = (rowid == HALF - 1) | (rowid == HALF)
     middle = (rowid >= HALF - 2) & (rowid < HALF + 2)
     turn = lambda tile: pltpu.roll(tile, HALF, 0)
+    depth = side.shape[1]
 
     def columns(entries):
         packed = side[entries[0]]
@@ -228,30 +260,42 @@
             packed = jnp.where(near, moved, packed)
         return packed
 
-    put_row_tile(down, 0, jnp.where(inner, turn(cross[2]), cross[0]))
-    put_row_tile(down, 1, jnp.where(inner, turn(cross[other + 2]), cross[other]))
-    put_row_tile(down, 2, jnp.where(middle, turn(cross[other + 1]), cross[1]))
-    start = down.shape[0] - side.shape[1]
-    down[start:, :] = columns([0, planes, 1, planes + 1, 2, planes + 2])
-    put_row_tile(up, 0, jnp.where(inner, cross[other], turn(cross[0])))
-    start = up.shape[0] - side.shape[1]
-    up[start:, :] = columns([planes - 1, 2 * planes - 1])
+    def fill(down, up):
+        put_row_tile(down, 0, jnp.where(inner, turn(cross[2]), cross[0]))
+        put_row_tile(down, 1, jnp.where(inner, turn(cross[other + 2]), cross[other]))
+        put_row_tile(down, 2, jnp.where(middle, turn(cross[other + 1]), cross[1]))
+        down[down.shape[0] - depth :, :] = columns([0, planes, 1, planes + 1, 2, planes + 2])
+        put_row_tile(up, 0, jnp.where(inner, cross[other], turn(cross[0])))
+        up[up.shape[0] - depth :, :] = columns([planes - 1, 2 * planes - 1])
+
+    @pl.when(jnp.logical_not(odd_core()))
+    def _():
+        fill(rim_a, rim_b)
+
+    @pl.when(odd_core())
+    def _():
+        fill(rim_b, rim_a)
 
 
 def pack_rims(planes, cross, side):
-    tiles = cross.shape[2] // LANES
-    rows = side.shape[1]
-    down = array(3 * tiles * SUBLANES + rows, LANES)
-    up = array(tiles * SUBLANES + rows, LANES)
+    rim = array(3 * cross.shape[2] // LANES * SUBLANES + side.shape[1], LANES)
     return pl.pallas_call(
         functools.partial(rims_kernel, planes),
-        out_shape=(down, up),
+        out_shape=(rim, rim),
         in_specs=[VMEM, VMEM],
         out_specs=(VMEM, VMEM),
-        cost_estimate=cost(down.size),
+        cost_estimate=cost(rim.size),
         compiler_params=pltpu.CompilerParams(vmem_limit_bytes=2 << 20),
         name="pack_rims",
     )(cross, side)
+
+
+class Either:
+    def __init__(self, even, odd):
+        self.even, self.odd, self.shape = even, odd, even.shape
+
+    def __getitem__(self, at):
+        return jnp.where(odd_core(), self.odd[at], self.even[at])
 
 
 def mobility(phi):
@@ -350,7 +394,7 @@
             write(e, t, slice(start, start + SUBLANES), p + gain, u + change / weight)
 
 
-def early_kernel(planes, shift_ref, phi, sol, phi_up, sol_up, side, cross, *rest):
+def early_kernel(planes, shift_ref, phi, sol, bulk_a, bulk_b, sol_up, side, cross, *rest):
     first = Field(*rest[:3], planes)
     second = Field(*rest[3:6], planes)
     own_phi, own_sol, sems = rest[6:]
@@ -373,8 +417,11 @@
                 for f in range(2)
             ]
         first.put_rows(base + k, p, u)
+    phi_up, lows = Either(bulk_a, bulk_b), Either(bulk_b, bulk_a)
     for k in range(ABOVE):
         first.put_block(top + k, phi_up, sol_up, k, k)
+    for k in range(BELOW):
+        first.put_block(k, lows, lows, k, BELOW + k)
     for copy in copies:
         copy.wait()
     for k in range(planes):
@@ -385,7 +432,7 @@
         step_plane(0, shift_ref[0], first, e, 2, second.put)
 
 
-def late_kernel(planes, shift_ref, lows, side, cross, rim_down, rim_up, seed, *rest):
+def late_kernel(planes, shift_ref, side, cross, rim_a, rim_b, seed, *rest):
     phi_out, sol_out = rest[6:8]
     first = Field(*rest[8:11], planes)
     second = Field(*rest[11:14], planes)
@@ -396,8 +443,7 @@
     fetch = pltpu.make_async_copy(seed, levels, sems.at[0])
     fetch.start()
     turn = lambda group: [pltpu.roll(tile, HALF, 0) for tile in group]
-    for k in range(BELOW):
-        first.put_block(k, lows, lows, k, BELOW + k)
+    rim_down, rim_up = Either(rim_a, rim_b), Either(rim_b, rim_a)
     p = get_row_tile(rim_down, 0, tiles)
     u = get_row_tile(rim_down, 1, tiles)
     first.put_rows(top, p, u)
@@ -475,13 +521,13 @@
         out_copy(1, j).wait()
 
 
-def early(shift, phi, sol, phi_up, sol_up, side, cross):
+def early(shift, phi, sol, bulk_a, bulk_b, sol_up, side, cross):
     planes, rows, cols = phi.shape
     state = array(planes + BELOW + ABOVE, cols // LANES + 1, rows + 2 * SUBLANES, LANES)
     return pl.pallas_call(
         functools.partial(early_kernel, planes),
         out_shape=(state,) * 6,
-        in_specs=[SMEM, HBM, HBM] + [VMEM] * 4,
+        in_specs=[SMEM, HBM, HBM] + [VMEM] * 5,
         out_specs=(VMEM,) * 6,
         scratch_shapes=[
             pltpu.VMEM(phi.shape, F32),
@@ -491,18 +537,18 @@
         cost_estimate=cost(64 * phi.size),
         compiler_params=pltpu.CompilerParams(vmem_limit_bytes=12 << 20),
         name="early",
-    )(shift, phi, sol, phi_up, sol_up, side, cross)
-
-
-def late(shift, lows, side, cross, down, up, seed, state, shape):
+    )(shift, phi, sol, bulk_a, bulk_b, sol_up, side, cross)
+
+
+def late(shift, side, cross, rim_a, rim_b, seed, state, shape):
     planes = shape[0]
     kept = tuple(jax.ShapeDtypeStruct(s.shape, s.dtype) for s in state)
     out = pl.pallas_call(
         functools.partial(late_kernel, planes),
         out_shape=(array(*shape), array(*shape)) + kept,
-        in_specs=[SMEM] + [VMEM] * 5 + [HBM] + [VMEM] * 6,
+        in_specs=[SMEM] + [VMEM] * 4 + [HBM] + [VMEM] * 6,
         out_specs=(HBM, HBM) + (VMEM,) * 6,
-        input_output_aliases={7 + k: 2 + k for k in range(6)},
+        input_output_aliases={6 + k: 2 + k for k in range(6)},
         scratch_shapes=[
             pltpu.VMEM(seed.shape, jnp.int32),
             pltpu.VMEM(shape, F32),
@@ -512,7 +558,7 @@
         cost_estimate=cost(3 * 64 * state[0].size),
         compiler_params=pltpu.CompilerParams(vmem_limit_bytes=12 << 20),
         name="late",
-    )(shift, lows, side, cross, down, up, seed, *state)
+    )(shift, side, cross, rim_a, rim_b, seed, *state)
     return out[0], out[1]
 
 
@@ -527,22 +573,22 @@
 
 def steps(phi, sol, shift_step, seed):
     planes = phi.shape[0]
-    size = lax.axis_size("grow")
-    fall = chain(size, -1)
-    rise = chain(size, 1)
-    phi_up = lax.ppermute(phi, "grow", fall)
-    sol_up = lax.ppermute(sol, "grow", fall)
-    side, cross, lows = pack_edges(phi, sol, seed)
-    lows = lax.ppermute(lows, "grow", rise)
+    size, lanes = lax.axis_size("grow"), lax.axis_size("side")
+    both = ("grow", "side")
+    even_down, even_up = two_way(size, lanes, -1), two_way(size, lanes, 1)
+    sol_up = lax.ppermute(sol, "grow", chain(size, -1))
+    side, cross, bulk_a, bulk_b = pack_edges(phi, sol, seed)
     side = swap_edges(side, "side", lane_of(side.shape) < LANES // 2)
+    bulk_a = lax.ppermute(bulk_a, both, even_down)
     cross = pack_rows(planes, cross, side)
     rowid = row_of(cross.shape)
     cross = swap_edges(cross, "cross", (rowid < HALF - 1) | (rowid == HALF))
-    down, up = pack_rims(planes, cross, side)
-    down = lax.ppermute(down, "grow", fall)
-    up = lax.ppermute(up, "grow", rise)
-    state = early(shift_step, phi, sol, phi_up, sol_up, side, cross)
-    return late(shift_step, lows, side, cross, down, up, seed, state, phi.shape)
+    bulk_b = lax.ppermute(bulk_b, both, even_up)
+    rim_a, rim_b = pack_rims(planes, cross, side)
+    rim_a = lax.ppermute(rim_a, both, even_down)
+    rim_b = lax.ppermute(rim_b, both, even_up)
+    state = early(shift_step, phi, sol, bulk_a, bulk_b, sol_up, side, cross)
+    return late(shift_step, side, cross, rim_a, rim_b, seed, state, phi.shape)
 
 
 def solution(mesh):

time: 30.1 us -> 27.1 us (0.900)
  starting transfers between devices: 16.7 us -> 9.13 us
  waiting for transfers between devices: 4.01 us -> 8.66 us
    ppermute x5, starting transfers between devices: 14.2 us -> 6.58 us  [the longest x1 3.22 us: steps(): bulk_b = lax.ppermute(bulk_b, both, even_up)]
    ppermute x5, waiting for transfers between devices: 0.07 us -> 4.74 us  [the longest x1 4.17 us: steps(): bulk_a = lax.ppermute(bulk_a, both, even_down)]
  transfers between devices with their start and end apart: 7 -> 7, of which waited for: 2 -> 3; matrix products, arithmetic and copies ran while one was open for 0% -> 0% of each run, Pallas kernels for 3% -> 4%
where the time goes in v3:
time: 27.1 us; the launch traced here: 26.9 us
  starting transfers between devices  9.13 us (34%)
  waiting for transfers between devices  8.66 us (32%)
  Pallas kernels  7.73 us (29%)
  between operations  1.37 us (5%)
    pallas_call x1, Pallas kernels, late(): pl.pallas_call(functools.partial(late_kernel, planes), out_shape=(array(*...  5.22 us
    ppermute x1, waiting for transfers between devices, steps(): bulk_a = lax.ppermute(bulk_a, both, even_down)  4.17 us
    ppermute x2, waiting for transfers between devices, swap_edges(): return lax.ppermute(message, axis, ring(size, 1))  3.92 us
    ppermute x1, starting transfers between devices, steps(): bulk_b = lax.ppermute(bulk_b, both, even_up)  3.22 us
    ppermute x2, starting transfers between devices, swap_edges(): return lax.ppermute(message, axis, ring(size, 1))  2.55 us
    ppermute x1, starting transfers between devices, steps(): rim_b = lax.ppermute(rim_b, both, even_up)  2.01 us
    pallas_call x1, Pallas kernels, pack_edges(): pl.pallas_call(functools.partial(edges_kernel, planes), out_shape=(array(...  1.51 us
    ppermute x1, starting transfers between devices, steps(): sol_up = lax.ppermute(sol, 'grow', chain(size, -1))  1.28 us
  transfers between devices with their start and end apart: 7, of which 3 were waited for; matrix products, arithmetic and copies ran while one was open for 0% of the time, Pallas kernels for 4%

profile of v3, /device:TPU:0, one launch (start us, length us, event | category | flops | bytes accessed | tf_op | source)
XLA Modules:
  0.0 26.9 jit_solution(4493885803042207029)
XLA Ops:
  0.6 0.0 copy-start.1
  0.6 0.0 copy-start
  0.7 1.5 %pack_edges.1 = (f32[9,32,128]{2,1,0:T(8,128)S(1)}, f32[7,8,512]{2,1,0:T(8,128)S(1)}, f32[4,32,512]{2,1,0:T(8,128)S(1)}, f32[4,32,512]{2,1,0:T(8,128)S(1)}) custom-call(f32[4,32,512]{2,1,0:T(8,128)} %phi.3, f32[4,32,512]{2,1,0:T(8,128)} %sol.3, s32[32,512]{1,0:T(8,128)} %seed.3), custom_call_target="tpu_custom_call" | custom-call | flops 65536 | bytes 262144 | tf_op jit(solution)/shard_map/pack_edges/pallas_call | solution.py:178
  2.2 0.0 copy-start.2
  2.2 0.6 %collective-permute-start = (f32[9,32,128]{2,1,0:T(8,128)S(1)}, f32[9,32,128]{2,1,0:T(8,128)S(1)}, u32[]{:S(2)}, u32[]{:S(2)}) collective-permute-start(f32[9,32,128]{2,1,0:T(8,128)S(1)} %get-tuple-element.16), channel_id=1, source_target_pairs={{0,1},{1,0},{2,3},{3,2},{4,5},{5,4},{6,7},{7,6},{8,9},{9,8},{10,11... | collective-permute-start | bytes 442376 | tf_op jit(solution)/shard_map/ppermute | solution.py:568
  2.7 1.3 %collective-permute-start.6 = (f32[4,32,512]{2,1,0:T(8,128)}, f32[4,32,512]{2,1,0:T(8,128)S(1)}, u32[]{:S(2)}, u32[]{:S(2)}) collective-permute-start(f32[4,32,512]{2,1,0:T(8,128)} %sol.3), channel_id=1, source_target_pairs={{4,0},{8,4},{12,8},{5,1},{9,5},{13,9},{6,2},{10,6},{14,10},{7,3},{... | collective-permute-start | bytes 786440 | tf_op jit(solution)/shard_map/ppermute | solution.py:579
  4.0 0.0 collective-permute-start.4
  4.1 3.2 %collective-permute-start.5 = (f32[4,32,512]{2,1,0:T(8,128)S(1)}, f32[4,32,512]{2,1,0:T(8,128)S(1)}, u32[]{:S(2)}, u32[]{:S(2)}) collective-permute-start(f32[4,32,512]{2,1,0:T(8,128)S(1)} %get-tuple-element.21), channel_id=1, source_target_pairs={{0,4},{1,0},{4,8},{5,1},{8,12},{9,5},{12,13},{13,9},{2,6},{3,2},{6... | collective-permute-start | bytes 786440 | tf_op jit(solution)/shard_map/ppermute | solution.py:586
  7.3 0.0 collective-permute-done.side
  7.3 2.0 %collective-permute-start.1 = (f32[7,8,640]{2,1,0:T(8,128)S(1)}, f32[7,8,640]{2,1,0:T(8,128)S(1)}, u32[]{:S(2)}, u32[]{:S(2)}) collective-permute-start(f32[7,8,640]{2,1,0:T(8,128)S(1)} %pack_rows.1), channel_id=1, source_target_pairs={{0,2},{2,0},{1,3},{3,1},{4,6},{6,4},{5,7},{7,5},{8,10},{10,8},{9,1... | collective-permute-start | bytes 430088 | tf_op jit(solution)/shard_map/ppermute | solution.py:568
  9.3 3.9 %collective-permute-done.1.cross = f32[7,8,640]{2,1,0:T(8,128)S(1)} collective-permute-done((f32[7,8,640]{2,1,0:T(8,128)S(1)}, f32[7,8,640]{2,1,0:T(8,128)S(1)}, u32[]{:S(2)}, u32[]{:S(2)}) %collective-permute-start.1) | collective-permute-done | bytes 143392 | tf_op jit(solution)/shard_map/ppermute | solution.py:568
  13.2 0.1 pack_rims.1
  13.3 0.0 collective-permute-start.2
  13.4 2.0 %collective-permute-start.3 = (f32[152,128]{1,0:T(8,128)S(1)}, f32[152,128]{1,0:T(8,128)S(1)}, u32[]{:S(2)}, u32[]{:S(2)}) collective-permute-start(f32[152,128]{1,0:T(8,128)S(1)} %get-tuple-element.19), channel_id=1, source_target_pairs={{0,4},{1,0},{4,8},{5,1},{8,12},{9,5},{12,13},{13,9},{2,6},{3,2},{6... | collective-permute-start | bytes 233480 | tf_op jit(solution)/shard_map/ppermute | solution.py:589
  16.0 0.0 collective-permute-done.6.sol_up
  16.0 4.2 %collective-permute-done.4.bulk_a = f32[4,32,512]{2,1,0:T(8,128)S(1)} collective-permute-done((f32[4,32,512]{2,1,0:T(8,128)S(1)}, f32[4,32,512]{2,1,0:T(8,128)S(1)}, u32[]{:S(2)}, u32[]{:S(2)}) %collective-permute-start.4) | collective-permute-done | bytes 262176 | tf_op jit(solution)/shard_map/ppermute | solution.py:582
  20.2 0.0 collective-permute-done.5.bulk_b
  20.2 0.0 copy-done.1
  20.2 0.0 copy-done
  20.2 0.9 %early.1 = (f32[10,5,48,128]{3,2,1,0:T(8,128)S(1)}, f32[10,5,48,128]{3,2,1,0:T(8,128)S(1)}, f32[10,5,48,128]{3,2,1,0:T(8,128)S(1)}, f32[10,5,48,128]{3,2,1,0:T(8...) custom-call(s32[1]{0:T(128)S(6)} %copy.18.shift_ref, f32[4,32,512]{2,1,0:T(8,128)S(1)} %copy-done, ...), custom_call_target="tpu_custom_call" | custom-call | flops 4194304 | bytes 16777216 | tf_op jit(solution)/shard_map/early/pallas_call | solution.py:527
  21.1 0.6 %collective-permute-done.2.rim_a = f32[152,128]{1,0:T(8,128)S(1)} collective-permute-done((f32[152,128]{1,0:T(8,128)S(1)}, f32[152,128]{1,0:T(8,128)S(1)}, u32[]{:S(2)}, u32[]{:S(2)}) %collective-permute-start.2) | collective-permute-done | bytes 77856 | tf_op jit(solution)/shard_map/ppermute | solution.py:588
  21.7 0.0 collective-permute-done.3.rim_b
  21.7 0.0 copy-done.2
  21.7 5.2 %late.1 = (f32[4,32,512]{2,1,0:T(8,128)}, f32[4,32,512]{2,1,0:T(8,128)}, f32[10,5,48,128]{3,2,1,0:T(8,128)S(1)}, f32[10,5,48,128]{3,2,1,0:T(8,128)S(1)}, f32[10,...) custom-call(s32[1]{0:T(128)S(6)} %copy.18.shift_ref, ...), custom_call_target="tpu_custom_call", output_to_operand_aliasing={{2}: (6, {}), {3}: (7, {}), {4}: (8, {}), {5}: (9, {}), {6}... | custom-call | flops 58982400 | bytes 235929600 | tf_op jit(solution)/shard_map/late/pallas_call | solution.py:546
  (1 shorter events, 0.0 us)
Async XLA Ops:
  0.6 19.6 %copy-start.1 = (f32[4,32,512]{2,1,0:T(8,128)S(1)}, f32[4,32,512]{2,1,0:T(8,128)}, u32[]{:S(2)}) copy-start(f32[4,32,512]{2,1,0:T(8,128)} %sol.3) | copy-start | bytes 786436
  0.6 19.6 %copy-start = (f32[4,32,512]{2,1,0:T(8,128)S(1)}, f32[4,32,512]{2,1,0:T(8,128)}, u32[]{:S(2)}) copy-start(f32[4,32,512]{2,1,0:T(8,128)} %phi.3) | copy-start | bytes 786436
  2.2 19.5 %copy-start.2 = (s32[32,512]{1,0:T(8,128)S(1)}, s32[32,512]{1,0:T(8,128)}, u32[]{:S(2)}) copy-start(s32[32,512]{1,0:T(8,128)} %seed.3) | copy-start | bytes 196612
  2.2 5.1 %collective-permute-start = (f32[9,32,128]{2,1,0:T(8,128)S(1)}, f32[9,32,128]{2,1,0:T(8,128)S(1)}, u32[]{:S(2)}, u32[]{:S(2)}) collective-permute-start(f32[9,32,128]{2,1,0:T(8,128)S(1)} %get-tuple-element.16), channel_id=1, source_target_pairs={{0,1},{1,0},{2,3},{3,2},{4,5},{5,4},{6,7},{7,6},{8,9},{9,8},{10,11... | collective-permute-start | bytes 442376 | tf_op jit(solution)/shard_map/ppermute | solution.py:568
  2.7 13.3 %collective-permute-start.6 = (f32[4,32,512]{2,1,0:T(8,128)}, f32[4,32,512]{2,1,0:T(8,128)S(1)}, u32[]{:S(2)}, u32[]{:S(2)}) collective-permute-start(f32[4,32,512]{2,1,0:T(8,128)} %sol.3), channel_id=1, source_target_pairs={{4,0},{8,4},{12,8},{5,1},{9,5},{13,9},{6,2},{10,6},{14,10},{7,3},{... | collective-permute-start | bytes 786440 | tf_op jit(solution)/shard_map/ppermute | solution.py:579
  4.0 16.2 %collective-permute-start.4 = (f32[4,32,512]{2,1,0:T(8,128)S(1)}, f32[4,32,512]{2,1,0:T(8,128)S(1)}, u32[]{:S(2)}, u32[]{:S(2)}) collective-permute-start(f32[4,32,512]{2,1,0:T(8,128)S(1)} %get-tuple-element.20), channel_id=1, source_target_pairs={{0,1},{1,5},{4,0},{5,9},{8,4},{9,13},{12,8},{13,12},{2,3},{3,7},{6... | collective-permute-start | bytes 786440 | tf_op jit(solution)/shard_map/ppermute | solution.py:582
  4.1 16.1 %collective-permute-start.5 = (f32[4,32,512]{2,1,0:T(8,128)S(1)}, f32[4,32,512]{2,1,0:T(8,128)S(1)}, u32[]{:S(2)}, u32[]{:S(2)}) collective-permute-start(f32[4,32,512]{2,1,0:T(8,128)S(1)} %get-tuple-element.21), channel_id=1, source_target_pairs={{0,4},{1,0},{4,8},{5,1},{8,12},{9,5},{12,13},{13,9},{2,6},{3,2},{6... | collective-permute-start | bytes 786440 | tf_op jit(solution)/shard_map/ppermute | solution.py:586
  7.3 5.9 %collective-permute-start.1 = (f32[7,8,640]{2,1,0:T(8,128)S(1)}, f32[7,8,640]{2,1,0:T(8,128)S(1)}, u32[]{:S(2)}, u32[]{:S(2)}) collective-permute-start(f32[7,8,640]{2,1,0:T(8,128)S(1)} %pack_rows.1), channel_id=1, source_target_pairs={{0,2},{2,0},{1,3},{3,1},{4,6},{6,4},{5,7},{7,5},{8,10},{10,8},{9,1... | collective-permute-start | bytes 430088 | tf_op jit(solution)/shard_map/ppermute | solution.py:568
  13.3 8.3 %collective-permute-start.2 = (f32[152,128]{1,0:T(8,128)S(1)}, f32[152,128]{1,0:T(8,128)S(1)}, u32[]{:S(2)}, u32[]{:S(2)}) collective-permute-start(f32[152,128]{1,0:T(8,128)S(1)} %get-tuple-element.18), channel_id=1, source_target_pairs={{0,1},{1,5},{4,0},{5,9},{8,4},{9,13},{12,8},{13,12},{2,3},{3,7},{6... | collective-permute-start | bytes 233480 | tf_op jit(solution)/shard_map/ppermute | solution.py:588
  13.4 8.3 %collective-permute-start.3 = (f32[152,128]{1,0:T(8,128)S(1)}, f32[152,128]{1,0:T(8,128)S(1)}, u32[]{:S(2)}, u32[]{:S(2)}) collective-permute-start(f32[152,128]{1,0:T(8,128)S(1)} %get-tuple-element.19), channel_id=1, source_target_pairs={{0,4},{1,0},{4,8},{5,1},{8,12},{9,5},{12,13},{13,9},{2,6},{3,2},{6... | collective-permute-start | bytes 233480 | tf_op jit(solution)/shard_map/ppermute | solution.py:589

commit v4 on v3

--- a/solution.py
+++ b/solution.py
@@ -31,10 +31,6 @@
     return [(i, (i + by) % size) for i in range(size)]
 
 
-def chain(size, by):
-    return [(i, i + by) for i in range(size) if 0 <= i + by < size]
-
-
 def two_way(size, lanes, even_by):
     pairs = []
     for g in range(size):
@@ -92,12 +88,11 @@
     return lax.axis_index("side") % 2 == 1
 
 
-def edges_kernel(planes, phi, sol, seed, side, cross, bulk_a, bulk_b, cols, rows, seed_cols, seed_rows, sems):
+def edges_kernel(planes, phi, sol, seed, side, cross, cols, rows, seed_cols, seed_rows, sems):
     depth, width = phi.shape[1:]
     left, right = pl.ds(0, LANES), pl.ds(width - LANES, LANES)
     first, last = pl.ds(0, SUBLANES), pl.ds(depth - SUBLANES, SUBLANES)
     every = slice(None)
-    kept = pl.ds(planes - BELOW, BELOW)
     copies = start_all(
         sems,
         [
@@ -115,19 +110,6 @@
             (seed.at[last, :], seed_rows.at[1]),
         ],
     )
-
-    def fill(fall, rise):
-        low, high = pl.ds(0, BELOW), pl.ds(BELOW, BELOW)
-        start_all(sems.at[pl.ds(12, 3)], [(phi, fall), (phi.at[kept], rise.at[low]), (sol.at[kept], rise.at[high])])
-
-    @pl.when(jnp.logical_not(odd_core()))
-    def _():
-        fill(bulk_a, bulk_b)
-
-    @pl.when(odd_core())
-    def _():
-        fill(bulk_b, bulk_a)
-
     for copy in copies[:6]:
         copy.wait()
     keep = lane_of((depth, LANES)) < LANES // 2
@@ -148,10 +130,36 @@
         for k in range(planes - 1):
             cross[field * (planes - 1) + k] = host(rowid, edge(field, k), guest, k)
     cross[2 * (planes - 1)] = level(jnp.where(keep, seed_rows[0], seed_rows[1]))
-    pltpu.make_async_copy(phi, bulk_a, sems.at[12]).wait()
-    for k in range(2):
-        part = bulk_b.at[pl.ds(k * BELOW, BELOW)]
-        pltpu.make_async_copy(phi.at[kept], part, sems.at[13 + k]).wait()
+
+
+def parts_kernel(phi, part_a, part_b, final):
+    count = part_a.shape[0]
+    planes = phi.shape[0]
+    low, high = slice(0, count), slice(planes - count, planes)
+    final[...] = phi[ABOVE - 1 : ABOVE]
+
+    @pl.when(jnp.logical_not(odd_core()))
+    def _():
+        part_a[...] = phi[low]
+        part_b[...] = phi[high]
+
+    @pl.when(odd_core())
+    def _():
+        part_a[...] = phi[high]
+        part_b[...] = phi[low]
+
+
+def pack_parts(phi):
+    part = array(ABOVE - 1, *phi.shape[1:])
+    return pl.pallas_call(
+        parts_kernel,
+        out_shape=(part, part, array(1, *phi.shape[1:])),
+        in_specs=[VMEM],
+        out_specs=(VMEM,) * 3,
+        cost_estimate=cost(phi.size),
+        compiler_params=pltpu.CompilerParams(vmem_limit_bytes=1 << 20),
+        name="pack_parts",
+    )(phi)
 
 
 def host(rowid, tile, guest, k):
@@ -180,17 +188,15 @@
         out_shape=(
             array(2 * planes + 1, rows, LANES),
             array(2 * planes - 1, SUBLANES, cols),
-            array(*phi.shape),
-            array(*phi.shape),
         ),
         in_specs=[HBM, HBM, HBM],
-        out_specs=(VMEM,) * 4,
+        out_specs=(VMEM, VMEM),
         scratch_shapes=[
             pltpu.VMEM((4, planes, rows, LANES), F32),
             pltpu.VMEM((4, planes, SUBLANES, cols), F32),
             pltpu.VMEM((2, rows, LANES), jnp.int32),
             pltpu.VMEM((2, SUBLANES, cols), jnp.int32),
-            pltpu.SemaphoreType.DMA((15,)),
+            pltpu.SemaphoreType.DMA((12,)),
         ],
         cost_estimate=cost(phi.size),
         compiler_params=pltpu.CompilerParams(vmem_limit_bytes=4 << 20),
@@ -343,7 +349,18 @@
     return lower, upper
 
 
-def step_plane(step, shift, source, e, halo, write):
+def covered(field, halo):
+    tiles = range(field.tiles if halo else field.tiles - 1)
+    first, rows = SUBLANES - halo, field.rows + 2 * halo
+    return [(first + k * SUBLANES, tiles) for k in range(-(-rows // SUBLANES))]
+
+
+def rimmed(field):
+    parts = [(1, range(field.tiles)), (SUBLANES + field.rows - 1, range(field.tiles))]
+    return parts + [(start, [field.tiles - 1]) for start, _ in covered(field, 0)]
+
+
+def step_plane(step, shift, source, e, parts, write):
     lower, upper = ends(step, shift, source, e)
     planes = source.planes
     grid_planes = planes * lax.axis_size("grow")
@@ -359,10 +376,7 @@
     lanes = lane_of((SUBLANES, LANES))
     heads = lanes == 0
     tails = lanes == LANES - 1
-    rows = source.rows + 2 * halo
-    outputs = tiles if halo else tiles - 1
-    for r in range(-(-rows // SUBLANES)):
-        start = SUBLANES - halo + r * SUBLANES
+    for start, outputs in parts:
 
         def load(ref, t, plane=e, by=0):
             return ref[plane, t, start + by : start + by + SUBLANES, :]
@@ -379,7 +393,7 @@
         flux = [
             (m_all[t] + after(m_all, t)) * (after(u_all, t) - u_all[t]) for t in range(tiles)
         ]
-        for t in range(outputs):
+        for t in outputs:
             p, u, m = p_all[t], u_all[t], m_all[t]
             total = after(p_all, t) + before(p_all, t)
             flow = flux[t] - before(flux, t)
@@ -394,12 +408,10 @@
             write(e, t, slice(start, start + SUBLANES), p + gain, u + change / weight)
 
 
-def early_kernel(planes, shift_ref, phi, sol, bulk_a, bulk_b, sol_up, side, cross, *rest):
+def early_kernel(planes, shift_ref, phi, sol, side, cross, *rest):
     first = Field(*rest[:3], planes)
     second = Field(*rest[3:6], planes)
-    own_phi, own_sol, sems = rest[6:]
     base, top, tiles = first.base, first.top, first.tiles
-    copies = start_all(sems, [(phi, own_phi), (sol, own_sol)])
     rowid = row_of((SUBLANES, LANES))
     cut = lambda t: slice(t * LANES, (t + 1) * LANES)
     other = planes - 1
@@ -417,26 +429,41 @@
                 for f in range(2)
             ]
         first.put_rows(base + k, p, u)
-    phi_up, lows = Either(bulk_a, bulk_b), Either(bulk_b, bulk_a)
-    for k in range(ABOVE):
-        first.put_block(top + k, phi_up, sol_up, k, k)
-    for k in range(BELOW):
-        first.put_block(k, lows, lows, k, BELOW + k)
-    for copy in copies:
-        copy.wait()
     for k in range(planes):
-        first.put_block(base + k, own_phi, own_sol, k, k)
+        first.put_block(base + k, phi, sol, k, k)
 
     @pl.loop(base + 1, top - 1)
     def _(e):
-        step_plane(0, shift_ref[0], first, e, 2, second.put)
+        step_plane(0, shift_ref[0], first, e, covered(first, 2), second.put)
+
+
+def levels_of(refs, planes):
+    return [Field(*refs[k : k + 3], planes) for k in (0, 3, 6)]
+
+
+def middle_kernel(planes, shift_ref, phi_a, phi_b, sol_a, sol_b, *rest):
+    first, second, third = levels_of(rest[6:], planes)
+    shift = shift_ref[0]
+    base, top = first.base, first.top
+    for k in range(ABOVE - 1):
+        first.put_block(top + k, Either(phi_a, phi_b), Either(sol_a, sol_b), k, k)
+    for k in range(BELOW):
+        j = ABOVE - 1 - BELOW + k
+        first.put_block(k, Either(phi_b, phi_a), Either(sol_b, sol_a), j, planes - BELOW + k)
+
+    @pl.loop(0, 2)
+    def _(k):
+        step_plane(0, shift, first, jnp.where(k == 0, base, top - 1), covered(first, 0), second.put)
+
+    @pl.loop(base + 1, top - 1)
+    def _(e):
+        step_plane(1, shift, second, e, covered(second, 0), third.put)
 
 
 def late_kernel(planes, shift_ref, side, cross, rim_a, rim_b, seed, *rest):
-    phi_out, sol_out = rest[6:8]
-    first = Field(*rest[8:11], planes)
-    second = Field(*rest[11:14], planes)
-    levels, phi_buf, sol_buf, sems = rest[14:]
+    first, second, third = levels_of(rest[11:], planes)
+    phi_out, sol_out = rest[9:11]
+    levels, sems = rest[20:]
     base, top, tiles, rows = first.base, first.top, first.tiles, first.rows
     shift = shift_ref[0]
     at_top = lax.axis_index("grow") == lax.axis_size("grow") - 1
@@ -476,89 +503,135 @@
             fill(t, slice(0, SUBLANES), value)
             fill(t, slice(SUBLANES + rows, 2 * SUBLANES + rows), value)
 
-    @pl.loop(0, 4)
-    def _(k):
-        e = jnp.where(k == 0, base, top - 2 + k)
-        step_plane(0, shift, first, e, 2, second.put)
+    @pl.loop(top, top + 2)
+    def _(e):
+        step_plane(0, shift, first, e, covered(first, 2), second.put)
 
     @pl.loop(0, 2)
     def _(k):
-        step_plane(0, shift, first, jnp.where(k == 0, base - 1, top + 2), 0, second.put)
+        step_plane(0, shift, first, jnp.where(k == 0, base, top - 1), rimmed(first), second.put)
+
+    step_plane(0, shift, first, base - 1, covered(first, 0), second.put)
 
     @pl.when(at_top & (shift == 0))
     def _():
         bring_top(second)
 
-    @pl.loop(base + 1, top + 1)
+    @pl.loop(top - 1, top + 1)
     def _(e):
-        step_plane(1, shift, second, e, 1, first.put)
-
-    @pl.loop(0, 2)
-    def _(k):
-        step_plane(1, shift, second, jnp.where(k == 0, base, top + 1), 0, first.put)
+        step_plane(1, shift, second, e, covered(second, 1), third.put)
+
+    @pl.loop(base + 1, top - 1)
+    def _(e):
+        step_plane(1, shift, second, e, rimmed(second), third.put)
+
+    step_plane(1, shift, second, base, covered(second, 0), third.put)
 
     @pl.when(at_top & (shift == 1))
     def _():
-        bring_top(first)
-
-    def out_copy(which, j):
-        buf, out = ((phi_buf, phi_out), (sol_buf, sol_out))[which]
-        return pltpu.make_async_copy(buf.at[j], out.at[j], sems.at[1 + which * planes + j])
-
-    @pl.loop(0, planes)
-    def _(j):
-        def finish(e, t, at, p, u):
-            place = (j, slice(at.start - SUBLANES, at.stop - SUBLANES), slice(t * LANES, (t + 1) * LANES))
-            phi_buf[place] = p
-            sol_buf[place] = u
-
-        step_plane(2, shift, first, j + base + 1, 0, finish)
-        out_copy(0, j).start()
-        out_copy(1, j).start()
-
-    for j in range(planes):
-        out_copy(0, j).wait()
-        out_copy(1, j).wait()
-
-
-def early(shift, phi, sol, bulk_a, bulk_b, sol_up, side, cross):
+        bring_top(third)
+
+    @pl.loop(base + 1, top)
+    def _(e):
+        step_plane(2, shift, third, e, covered(third, 0), into(phi_out, sol_out, base + 1))
+
+
+def into(phi_out, sol_out, lowest):
+    def write(e, t, at, p, u):
+        at = slice(at.start - SUBLANES, at.stop - SUBLANES)
+        lanes = slice(t * LANES, (t + 1) * LANES)
+        phi_out[e - lowest, at, lanes] = p
+        sol_out[e - lowest, at, lanes] = u
+
+    return write
+
+
+def final_kernel(planes, shift_ref, phi_last, sol_a, sol_b, phi_in, sol_in, *rest):
+    phi_out, sol_out = rest[9:11]
+    first, second, third = levels_of(rest[11:], planes)
+    phi_buf, sol_buf, sems = rest[20:]
+    shift = shift_ref[0]
+    top = first.top
+    done = pl.ds(0, planes - 1)
+    copies = start_all(
+        sems, [(phi_in.at[done], phi_out.at[done]), (sol_in.at[done], sol_out.at[done])]
+    )
+    edge = top + ABOVE - 1
+    first.put_block(edge, phi_last, Either(sol_a, sol_b), 0, ABOVE - 1)
+    step_plane(0, shift, first, edge - 1, covered(first, 0), second.put)
+    step_plane(1, shift, second, edge - 2, covered(second, 0), third.put)
+    step_plane(2, shift, third, edge - 3, covered(third, 0), into(phi_buf, sol_buf, edge - 3))
+    copies += start_all(
+        sems.at[pl.ds(2, 2)],
+        [(phi_buf.at[0], phi_out.at[planes - 1]), (sol_buf.at[0], sol_out.at[planes - 1])],
+    )
+    for copy in copies:
+        copy.wait()
+
+
+def early(shift, phi, sol, side, cross):
     planes, rows, cols = phi.shape
     state = array(planes + BELOW + ABOVE, cols // LANES + 1, rows + 2 * SUBLANES, LANES)
     return pl.pallas_call(
         functools.partial(early_kernel, planes),
         out_shape=(state,) * 6,
-        in_specs=[SMEM, HBM, HBM] + [VMEM] * 5,
+        in_specs=[SMEM] + [VMEM] * 4,
         out_specs=(VMEM,) * 6,
-        scratch_shapes=[
-            pltpu.VMEM(phi.shape, F32),
-            pltpu.VMEM(phi.shape, F32),
-            pltpu.SemaphoreType.DMA((2,)),
-        ],
         cost_estimate=cost(64 * phi.size),
-        compiler_params=pltpu.CompilerParams(vmem_limit_bytes=12 << 20),
+        compiler_params=pltpu.CompilerParams(vmem_limit_bytes=8 << 20),
         name="early",
-    )(shift, phi, sol, bulk_a, bulk_b, sol_up, side, cross)
+    )(shift, phi, sol, side, cross)
+
+
+def same(arrays):
+    return tuple(array(*a.shape) for a in arrays)
+
+
+def middle(planes, shift, received, state):
+    return pl.pallas_call(
+        functools.partial(middle_kernel, planes),
+        out_shape=same(state) + same(state[:3]),
+        in_specs=[SMEM] + [VMEM] * 10,
+        out_specs=(VMEM,) * 9,
+        input_output_aliases={5 + k: k for k in range(6)},
+        cost_estimate=cost(64 * received[0].size),
+        compiler_params=pltpu.CompilerParams(vmem_limit_bytes=8 << 20),
+        name="middle",
+    )(shift, *received, *state)
 
 
 def late(shift, side, cross, rim_a, rim_b, seed, state, shape):
-    planes = shape[0]
-    kept = tuple(jax.ShapeDtypeStruct(s.shape, s.dtype) for s in state)
     out = pl.pallas_call(
-        functools.partial(late_kernel, planes),
-        out_shape=(array(*shape), array(*shape)) + kept,
-        in_specs=[SMEM] + [VMEM] * 4 + [HBM] + [VMEM] * 6,
-        out_specs=(HBM, HBM) + (VMEM,) * 6,
-        input_output_aliases={6 + k: 2 + k for k in range(6)},
-        scratch_shapes=[
-            pltpu.VMEM(seed.shape, jnp.int32),
-            pltpu.VMEM(shape, F32),
-            pltpu.VMEM(shape, F32),
-            pltpu.SemaphoreType.DMA((1 + 2 * planes,)),
-        ],
+        functools.partial(late_kernel, shape[0]),
+        out_shape=(array(*shape), array(*shape)) + same(state),
+        in_specs=[SMEM] + [VMEM] * 4 + [HBM] + [VMEM] * 9,
+        out_specs=(VMEM,) * 11,
+        input_output_aliases={6 + k: 2 + k for k in range(9)},
+        scratch_shapes=[pltpu.VMEM(seed.shape, jnp.int32), pltpu.SemaphoreType.DMA((1,))],
         cost_estimate=cost(3 * 64 * state[0].size),
-        compiler_params=pltpu.CompilerParams(vmem_limit_bytes=12 << 20),
+        compiler_params=pltpu.CompilerParams(vmem_limit_bytes=8 << 20),
         name="late",
     )(shift, side, cross, rim_a, rim_b, seed, *state)
+    return out[:2], out[2:]
+
+
+def final(shift, phi_last, sol_a, sol_b, outs, state, shape):
+    planes = shape[0]
+    out = pl.pallas_call(
+        functools.partial(final_kernel, planes),
+        out_shape=(array(*shape), array(*shape)) + same(state),
+        in_specs=[SMEM] + [VMEM] * 14,
+        out_specs=(HBM, HBM) + (VMEM,) * 9,
+        input_output_aliases={6 + k: 2 + k for k in range(9)},
+        scratch_shapes=[
+            pltpu.VMEM((1,) + shape[1:], F32),
+            pltpu.VMEM((1,) + shape[1:], F32),
+            pltpu.SemaphoreType.DMA((4,)),
+        ],
+        cost_estimate=cost(64 * phi_last.size),
+        compiler_params=pltpu.CompilerParams(vmem_limit_bytes=8 << 20),
+        name="final",
+    )(shift, phi_last, sol_a, sol_b, *outs, *state)
     return out[0], out[1]
 
 
@@ -576,19 +649,24 @@
     size, lanes = lax.axis_size("grow"), lax.axis_size("side")
     both = ("grow", "side")
     even_down, even_up = two_way(size, lanes, -1), two_way(size, lanes, 1)
-    sol_up = lax.ppermute(sol, "grow", chain(size, -1))
-    side, cross, bulk_a, bulk_b = pack_edges(phi, sol, seed)
+    sol_a = lax.ppermute(sol, both, even_down)
+    sol_b = lax.ppermute(sol, both, even_up)
+    phi_a, phi_b, phi_last = pack_parts(phi)
+    phi_a = lax.ppermute(phi_a, both, even_down)
+    phi_b = lax.ppermute(phi_b, both, even_up)
+    side, cross = pack_edges(phi, sol, seed)
     side = swap_edges(side, "side", lane_of(side.shape) < LANES // 2)
-    bulk_a = lax.ppermute(bulk_a, both, even_down)
     cross = pack_rows(planes, cross, side)
     rowid = row_of(cross.shape)
     cross = swap_edges(cross, "cross", (rowid < HALF - 1) | (rowid == HALF))
-    bulk_b = lax.ppermute(bulk_b, both, even_up)
     rim_a, rim_b = pack_rims(planes, cross, side)
     rim_a = lax.ppermute(rim_a, both, even_down)
     rim_b = lax.ppermute(rim_b, both, even_up)
-    state = early(shift_step, phi, sol, bulk_a, bulk_b, sol_up, side, cross)
-    return late(shift_step, side, cross, rim_a, rim_b, seed, state, phi.shape)
+    phi_last = lax.ppermute(phi_last, "grow", ring(size, -1))
+    state = early(shift_step, phi, sol, side, cross)
+    state = middle(planes, shift_step, (phi_a, phi_b, sol_a, sol_b), state)
+    outs, state = late(shift_step, side, cross, rim_a, rim_b, seed, state, phi.shape)
+    return final(shift_step, phi_last, sol_a, sol_b, outs, state, phi.shape)
 
 
 def solution(mesh):

time: 27.1 us -> 29.5 us (1.089)
  starting transfers between devices: 9.13 us -> 13.8 us
  waiting for transfers between devices: 8.66 us -> 4.97 us
  local copies, waits for them, and re-layouts: 0.02 us -> 0.97 us
  Pallas kernels: 7.73 us -> 8.06 us
    ppermute x3 -> x5, starting transfers between devices: 4.54 us -> 9.27 us  [the longest x1 4.62 us: steps(): phi_last = lax.ppermute(phi_last, 'grow', ring(size, -1))]
    ppermute x3 -> x5, waiting for transfers between devices: 4.18 us -> 1.58 us  [the longest x1 1.57 us: steps(): phi_b = lax.ppermute(phi_b, both, even_up)]
    unnamed x6 -> x8, local copies, waits for them, and re-layouts: 0.02 us -> 0.97 us
    pallas_call x1 -> x4, Pallas kernels: 5.22 us -> 5.93 us  [the longest x1 3.43 us: late(): pl.pallas_call(functools.partial(late_kernel, shape[0]), out_shape=(array...]
    ppermute x1, waiting for transfers between devices: 0.56 us -> 0.01 us  [steps(): rim_a = lax.ppermute(rim_a, both, even_down)]
    ppermute x2, waiting for transfers between devices: 3.92 us -> 3.38 us  [swap_edges(): return lax.ppermute(message, axis, ring(size, 1))]
  transfers between devices with their start and end apart: 7 -> 9, of which waited for: 3 -> 2; matrix products, arithmetic and copies ran while one was open for 0% -> 0% of each run, Pallas kernels for 4% -> 18%
where the time goes in v4:
time: 29.5 us; the launch traced here: 29.3 us
  starting transfers between devices  13.8 us (47%)
  Pallas kernels  8.06 us (27%)
  waiting for transfers between devices  4.97 us (17%)
  between operations  1.44 us (5%)
  local copies, waits for them, and re-layouts  0.97 us (3%)
    ppermute x1, starting transfers between devices, steps(): phi_last = lax.ppermute(phi_last, 'grow', ring(size, -1))  4.62 us
    pallas_call x1, Pallas kernels, late(): pl.pallas_call(functools.partial(late_kernel, shape[0]), out_shape=(array...  3.43 us
    ppermute x2, waiting for transfers between devices, swap_edges(): return lax.ppermute(message, axis, ring(size, 1))  3.38 us
    ppermute x1, starting transfers between devices, steps(): sol_b = lax.ppermute(sol, both, even_up)  2.59 us
    ppermute x2, starting transfers between devices, swap_edges(): return lax.ppermute(message, axis, ring(size, 1))  2.53 us
    ppermute x1, starting transfers between devices, steps(): rim_b = lax.ppermute(rim_b, both, even_up)  2.01 us
    ppermute x1, starting transfers between devices, steps(): phi_b = lax.ppermute(phi_b, both, even_up)  1.84 us
    ppermute x1, waiting for transfers between devices, steps(): phi_b = lax.ppermute(phi_b, both, even_up)  1.57 us
  transfers between devices with their start and end apart: 9, of which 2 were waited for; matrix products, arithmetic and copies ran while one was open for 0% of the time, Pallas kernels for 18%

profile of v4, /device:TPU:0, one launch (start us, length us, event | category | flops | bytes accessed | tf_op | source)
XLA Modules:
  0.0 29.3 jit_solution(17815777843190786364)
XLA Ops:
  0.6 0.0 copy-start.2
  0.6 0.0 copy-start.1
  0.7 1.3 %pack_edges.1 = (f32[9,32,128]{2,1,0:T(8,128)S(1)}, f32[7,8,512]{2,1,0:T(8,128)S(1)}) custom-call(f32[4,32,512]{2,1,0:T(8,128)} %phi.5, f32[4,32,512]{2,1,0:T(8,128)} %sol.3, s32[32,512]{1,0:T(8,128)} %seed.3), custom_call_target="tpu_custom_call" | custom-call | flops 65536 | bytes 262144 | tf_op jit(solution)/shard_map/pack_edges/pallas_call | solution.py:186
  1.9 0.6 %collective-permute-start.3 = (f32[9,32,128]{2,1,0:T(8,128)S(1)}, f32[9,32,128]{2,1,0:T(8,128)S(1)}, u32[]{:S(2)}, u32[]{:S(2)}) collective-permute-start(f32[9,32,128]{2,1,0:T(8,128)S(1)} %get-tuple-element.38), channel_id=1, source_target_pairs={{0,1},{1,0},{2,3},{3,2},{4,5},{5,4},{6,7},{7,6},{8,9},{9,8},{10,11... | collective-permute-start | bytes 442376 | tf_op jit(solution)/shard_map/ppermute | solution.py:641
  2.5 0.0 copy-start
  2.5 0.9 %copy-done = f32[4,32,512]{2,1,0:T(8,128)S(1)} copy-done((f32[4,32,512]{2,1,0:T(8,128)S(1)}, f32[4,32,512]{2,1,0:T(8,128)}, u32[]{:S(2)}) %copy-start) | copy-done | bytes 262168
  3.5 0.0 collective-permute-start.7
  3.5 2.6 %collective-permute-start.2 = (f32[4,32,512]{2,1,0:T(8,128)}, f32[4,32,512]{2,1,0:T(8,128)S(1)}, u32[]{:S(2)}, u32[]{:S(2)}) collective-permute-start(f32[4,32,512]{2,1,0:T(8,128)} %sol.3), channel_id=1, source_target_pairs={{0,4},{1,0},{4,8},{5,1},{8,12},{9,5},{12,13},{13,9},{2,6},{3,2},{6... | collective-permute-start | bytes 786440 | tf_op jit(solution)/shard_map/ppermute | solution.py:653
  6.1 0.2 collective-permute-start.1
  6.3 1.8 %collective-permute-start.8 = (f32[3,32,512]{2,1,0:T(8,128)S(1)}, f32[3,32,512]{2,1,0:T(8,128)S(1)}, u32[]{:S(2)}, u32[]{:S(2)}) collective-permute-start(f32[3,32,512]{2,1,0:T(8,128)S(1)} %get-tuple-element.43), channel_id=1, source_target_pairs={{0,4},{1,0},{4,8},{5,1},{8,12},{9,5},{12,13},{13,9},{2,6},{3,2},{6... | collective-permute-start | bytes 589832 | tf_op jit(solution)/shard_map/ppermute | solution.py:656
  8.1 0.0 collective-permute-done.3.side
  8.2 2.0 %collective-permute-start.4 = (f32[7,8,640]{2,1,0:T(8,128)S(1)}, f32[7,8,640]{2,1,0:T(8,128)S(1)}, u32[]{:S(2)}, u32[]{:S(2)}) collective-permute-start(f32[7,8,640]{2,1,0:T(8,128)S(1)} %pack_rows.1), channel_id=1, source_target_pairs={{0,2},{2,0},{1,3},{3,1},{4,6},{6,4},{5,7},{7,5},{8,10},{10,8},{9,1... | collective-permute-start | bytes 430088 | tf_op jit(solution)/shard_map/ppermute | solution.py:641
  10.1 3.4 %collective-permute-done.4.cross = f32[7,8,640]{2,1,0:T(8,128)S(1)} collective-permute-done((f32[7,8,640]{2,1,0:T(8,128)S(1)}, f32[7,8,640]{2,1,0:T(8,128)S(1)}, u32[]{:S(2)}, u32[]{:S(2)}) %collective-permute-start.4) | collective-permute-done | bytes 143392 | tf_op jit(solution)/shard_map/ppermute | solution.py:641
  13.5 0.1 pack_rims.1
  13.6 0.0 collective-permute-start.5
  13.6 0.0 collective-permute-done.7.phi_a
  13.7 2.0 %collective-permute-start.6 = (f32[152,128]{1,0:T(8,128)S(1)}, f32[152,128]{1,0:T(8,128)S(1)}, u32[]{:S(2)}, u32[]{:S(2)}) collective-permute-start(f32[152,128]{1,0:T(8,128)S(1)} %get-tuple-element.41), channel_id=1, source_target_pairs={{0,4},{1,0},{4,8},{5,1},{8,12},{9,5},{12,13},{13,9},{2,6},{3,2},{6... | collective-permute-start | bytes 233480 | tf_op jit(solution)/shard_map/ppermute | solution.py:664
  15.7 1.6 %collective-permute-done.8.phi_b = f32[3,32,512]{2,1,0:T(8,128)S(1)} collective-permute-done((f32[3,32,512]{2,1,0:T(8,128)S(1)}, f32[3,32,512]{2,1,0:T(8,128)S(1)}, u32[]{:S(2)}, u32[]{:S(2)}) %collective-permute-start.8) | collective-permute-done | bytes 196640 | tf_op jit(solution)/shard_map/ppermute | solution.py:656
  17.2 4.6 %collective-permute-start = (f32[1,32,512]{2,1,0:T(8,128)S(1)}, f32[1,32,512]{2,1,0:T(8,128)S(1)}, u32[]{:S(2)}, u32[]{:S(2)}) collective-permute-start(f32[1,32,512]{2,1,0:T(8,128)S(1)} %get-tuple-element.37), channel_id=1, source_target_pairs={{0,12},{4,0},{8,4},{12,8},{1,13},{5,1},{9,5},{13,9},{2,14},{6,2},{... | collective-permute-start | bytes 196616 | tf_op jit(solution)/shard_map/ppermute | solution.py:665
  22.5 0.0 copy-done.2
  22.5 0.0 copy-done.1
  22.5 0.7 %early.1 = (f32[10,5,48,128]{3,2,1,0:T(8,128)S(1)}, f32[10,5,48,128]{3,2,1,0:T(8,128)S(1)}, f32[10,5,48,128]{3,2,1,0:T(8,128)S(1)}, f32[10,5,48,128]{3,2,1,0:T(8...) custom-call(s32[1]{0:T(128)S(6)} %copy.54.shift_ref, f32[4,32,512]{2,1,0:T(8,128)S(1)} %copy-done.1, ...), custom_call_target="tpu_custom_call" | custom-call | flops 4194304 | bytes 16777216 | tf_op jit(solution)/shard_map/early/pallas_call | solution.py:575
  23.3 0.0 collective-permute-done.2.sol_b
  23.3 0.0 collective-permute-done.1.sol_a
  23.3 0.0 copy-start.3
  23.3 1.0 %middle.1 = (f32[10,5,48,128]{3,2,1,0:T(8,128)S(1)}, f32[10,5,48,128]{3,2,1,0:T(8,128)S(1)}, f32[10,5,48,128]{3,2,1,0:T(8,128)S(1)}, f32[10,5,48,128]{3,2,1,0:T(...) custom-call(s32[1]{0:T(128)S(6)} %copy.54.shift_ref, ...), custom_call_target="tpu_custom_call", output_to_operand_aliasing={{0}: (5, {}), {1}: (6, {}), {2}: (7, {}), {3}: (8, {}), {4}... | custom-call | flops 3145728 | bytes 12582912 | tf_op jit(solution)/shard_map/middle/pallas_call | solution.py:591
  24.3 0.0 collective-permute-done.5.rim_a
  24.3 0.0 collective-permute-done.6.rim_b
  24.3 0.0 copy-done.3
  24.3 3.4 %late.1 = (f32[4,32,512]{2,1,0:T(8,128)S(1)}, f32[4,32,512]{2,1,0:T(8,128)S(1)}, f32[10,5,48,128]{3,2,1,0:T(8,128)S(1)}, f32[10,5,48,128]{3,2,1,0:T(8,128)S(1)},...) custom-call(s32[1]{0:T(128)S(6)} %copy.54.shift_ref, ...), custom_call_target="tpu_custom_call", output_to_operand_aliasing={{2}: (6, {}), {3}: (7, {}), {4}: (8, {}), {5}: (9, {}), {6}... | custom-call | flops 58982400 | bytes 235929600 | tf_op jit(solution)/shard_map/late/pallas_call | solution.py:604
  27.7 0.0 collective-permute-done.phi_last
  27.8 1.5 %final.1 = (f32[4,32,512]{2,1,0:T(8,128)}, f32[4,32,512]{2,1,0:T(8,128)}, f32[10,5,48,128]{3,2,1,0:T(8,128)S(1)}, f32[10,5,48,128]{3,2,1,0:T(8,128)S(1)}, f32[10...) custom-call(s32[1]{0:T(128)S(6)} %copy.54.shift_ref, ...), custom_call_target="tpu_custom_call", output_to_operand_aliasing={{2}: (6, {}), {3}: (7, {}), {4}: (8, {}), {5}: (9, {}), {6}... | custom-call | flops 1048576 | bytes 4194304 | tf_op jit(solution)/shard_map/final/pallas_call | solution.py:620
  (2 shorter events, 0.0 us)
Async XLA Ops:
  0.6 21.9 %copy-start.2 = (f32[4,32,512]{2,1,0:T(8,128)S(1)}, f32[4,32,512]{2,1,0:T(8,128)}, u32[]{:S(2)}) copy-start(f32[4,32,512]{2,1,0:T(8,128)} %sol.3) | copy-start | bytes 786436
  0.6 21.9 %copy-start.1 = (f32[4,32,512]{2,1,0:T(8,128)S(1)}, f32[4,32,512]{2,1,0:T(8,128)}, u32[]{:S(2)}) copy-start(f32[4,32,512]{2,1,0:T(8,128)} %phi.5) | copy-start | bytes 786436
  1.9 6.2 %collective-permute-start.3 = (f32[9,32,128]{2,1,0:T(8,128)S(1)}, f32[9,32,128]{2,1,0:T(8,128)S(1)}, u32[]{:S(2)}, u32[]{:S(2)}) collective-permute-start(f32[9,32,128]{2,1,0:T(8,128)S(1)} %get-tuple-element.38), channel_id=1, source_target_pairs={{0,1},{1,0},{2,3},{3,2},{4,5},{5,4},{6,7},{7,6},{8,9},{9,8},{10,11... | collective-permute-start | bytes 442376 | tf_op jit(solution)/shard_map/ppermute | solution.py:641
  2.5 0.9 %copy-start = (f32[4,32,512]{2,1,0:T(8,128)S(1)}, f32[4,32,512]{2,1,0:T(8,128)}, u32[]{:S(2)}) copy-start(f32[4,32,512]{2,1,0:T(8,128)} %phi.5) | copy-start | bytes 786436
  3.5 10.2 %collective-permute-start.7 = (f32[3,32,512]{2,1,0:T(8,128)S(1)}, f32[3,32,512]{2,1,0:T(8,128)S(1)}, u32[]{:S(2)}, u32[]{:S(2)}) collective-permute-start(f32[3,32,512]{2,1,0:T(8,128)S(1)} %get-tuple-element.42), channel_id=1, source_target_pairs={{0,1},{1,5},{4,0},{5,9},{8,4},{9,13},{12,8},{13,12},{2,3},{3,7},{6... | collective-permute-start | bytes 589832 | tf_op jit(solution)/shard_map/ppermute | solution.py:655
  3.5 19.7 %collective-permute-start.2 = (f32[4,32,512]{2,1,0:T(8,128)}, f32[4,32,512]{2,1,0:T(8,128)S(1)}, u32[]{:S(2)}, u32[]{:S(2)}) collective-permute-start(f32[4,32,512]{2,1,0:T(8,128)} %sol.3), channel_id=1, source_target_pairs={{0,4},{1,0},{4,8},{5,1},{8,12},{9,5},{12,13},{13,9},{2,6},{3,2},{6... | collective-permute-start | bytes 786440 | tf_op jit(solution)/shard_map/ppermute | solution.py:653
  6.1 17.2 %collective-permute-start.1 = (f32[4,32,512]{2,1,0:T(8,128)}, f32[4,32,512]{2,1,0:T(8,128)S(1)}, u32[]{:S(2)}, u32[]{:S(2)}) collective-permute-start(f32[4,32,512]{2,1,0:T(8,128)} %sol.3), channel_id=1, source_target_pairs={{0,1},{1,5},{4,0},{5,9},{8,4},{9,13},{12,8},{13,12},{2,3},{3,7},{6... | collective-permute-start | bytes 786440 | tf_op jit(solution)/shard_map/ppermute | solution.py:652
  6.3 10.9 %collective-permute-start.8 = (f32[3,32,512]{2,1,0:T(8,128)S(1)}, f32[3,32,512]{2,1,0:T(8,128)S(1)}, u32[]{:S(2)}, u32[]{:S(2)}) collective-permute-start(f32[3,32,512]{2,1,0:T(8,128)S(1)} %get-tuple-element.43), channel_id=1, source_target_pairs={{0,4},{1,0},{4,8},{5,1},{8,12},{9,5},{12,13},{13,9},{2,6},{3,2},{6... | collective-permute-start | bytes 589832 | tf_op jit(solution)/shard_map/ppermute | solution.py:656
  8.2 5.4 %collective-permute-start.4 = (f32[7,8,640]{2,1,0:T(8,128)S(1)}, f32[7,8,640]{2,1,0:T(8,128)S(1)}, u32[]{:S(2)}, u32[]{:S(2)}) collective-permute-start(f32[7,8,640]{2,1,0:T(8,128)S(1)} %pack_rows.1), channel_id=1, source_target_pairs={{0,2},{2,0},{1,3},{3,1},{4,6},{6,4},{5,7},{7,5},{8,10},{10,8},{9,1... | collective-permute-start | bytes 430088 | tf_op jit(solution)/shard_map/ppermute | solution.py:641
  13.6 10.7 %collective-permute-start.5 = (f32[152,128]{1,0:T(8,128)S(1)}, f32[152,128]{1,0:T(8,128)S(1)}, u32[]{:S(2)}, u32[]{:S(2)}) collective-permute-start(f32[152,128]{1,0:T(8,128)S(1)} %get-tuple-element.40), channel_id=1, source_target_pairs={{0,1},{1,5},{4,0},{5,9},{8,4},{9,13},{12,8},{13,12},{2,3},{3,7},{6... | collective-permute-start | bytes 233480 | tf_op jit(solution)/shard_map/ppermute | solution.py:663
  13.7 10.6 %collective-permute-start.6 = (f32[152,128]{1,0:T(8,128)S(1)}, f32[152,128]{1,0:T(8,128)S(1)}, u32[]{:S(2)}, u32[]{:S(2)}) collective-permute-start(f32[152,128]{1,0:T(8,128)S(1)} %get-tuple-element.41), channel_id=1, source_target_pairs={{0,4},{1,0},{4,8},{5,1},{8,12},{9,5},{12,13},{13,9},{2,6},{3,2},{6... | collective-permute-start | bytes 233480 | tf_op jit(solution)/shard_map/ppermute | solution.py:664
  17.2 10.5 %collective-permute-start = (f32[1,32,512]{2,1,0:T(8,128)S(1)}, f32[1,32,512]{2,1,0:T(8,128)S(1)}, u32[]{:S(2)}, u32[]{:S(2)}) collective-permute-start(f32[1,32,512]{2,1,0:T(8,128)S(1)} %get-tuple-element.37), channel_id=1, source_target_pairs={{0,12},{4,0},{8,4},{12,8},{1,13},{5,1},{9,5},{13,9},{2,14},{6,2},{... | collective-permute-start | bytes 196616 | tf_op jit(solution)/shard_map/ppermute | solution.py:665
  23.3 1.0 %copy-start.3 = (s32[32,512]{1,0:T(8,128)S(1)}, s32[32,512]{1,0:T(8,128)}, u32[]{:S(2)}) copy-start(s32[32,512]{1,0:T(8,128)} %seed.3) | copy-start | bytes 196612

commit v5 on v4

v5 whole, which is shorter than its diff:
```python
import functools

import jax
import jax.numpy as jnp
from jax import lax
from jax.experimental import pallas as pl
from jax.experimental.pallas import tpu as pltpu
from jax.sharding import PartitionSpec as P


ITERS = 3
LANES = 128
SUBLANES = 8

partition = 0.15
coupling = 2.0
diffusion = 2.0
spacing_sq = 0.64
time_step = 0.025
gradient_scale = 1.2
drift_rate = 0.01
seed_levels = 1024.0

BELOW = ITERS - 1
ABOVE = ITERS + 1
RIMMED = ITERS
F32 = jnp.float32


def ring(size, by):
    return [(i, (i + by) % size) for i in range(size)]


def two_way(size, lanes, even_by):
    pairs = []
    for g in range(size):
        for c in range(lanes):
            target = g + (even_by if c % 2 == 0 else -even_by)
            inside = 0 <= target < size
            pairs.append((g * lanes + c, target * lanes + c if inside else g * lanes + (c ^ 1)))
    return pairs


def lane_of(shape):
    return lax.broadcasted_iota(jnp.int32, shape, len(shape) - 1)


def row_of(shape):
    return lax.broadcasted_iota(jnp.int32, shape, len(shape) - 2)


def level(seed):
    return seed.astype(F32) / seed_levels - 1.0


VMEM = pl.BlockSpec(memory_space=pltpu.VMEM)
HBM = pl.BlockSpec(memory_space=pltpu.HBM)
SMEM = pl.BlockSpec(memory_space=pltpu.SMEM)
HALF = SUBLANES // 2
LANE_STEP = 2 * SUBLANES


def cost(count):
    return pl.CostEstimate(flops=count, bytes_accessed=4 * count, transcendentals=0)


def in_hbm(x):
    return pltpu.with_memory_space_constraint(x, pltpu.HBM)


def array(*shape):
    return jax.ShapeDtypeStruct(shape, F32)


def start_all(sems, pairs):
    copies = []
    for k, (source, target) in enumerate(pairs):
        copies.append(pltpu.make_async_copy(source, target, sems.at[k]))
        copies[-1].start()
    return copies


def guest_turns(k):
    return (HALF + k, HALF - k)


def odd_core():
    return lax.axis_index("side") % 2 == 1


def edges_kernel(planes, phi_in, sol_in, seed_in, side, cross, part, phi, sol, seed, sems):
    depth, width = phi.shape[1:]
    keep = lane_of((depth, LANES)) < LANES // 2
    copies = start_all(sems, [(phi_in, phi), (sol_in, sol), (seed_in, seed)])
    for copy in copies:
        copy.wait()

    def columns(ref, *at):
        first, last = slice(0, LANES), slice(width - LANES, width)
        return jnp.where(keep, ref[(*at, slice(None), first)], ref[(*at, slice(None), last)])

    for k in range(planes):
        side[k] = columns(phi, k)
        side[planes + k] = columns(sol, k)
    side[2 * planes] = level(columns(seed))
    rowid = row_of((SUBLANES, width))
    upper = rowid < HALF

    def edge(ref, *at):
        first, last = slice(0, SUBLANES), slice(depth - SUBLANES, depth)
        return jnp.where(upper, ref[(*at, first)], ref[(*at, last)])

    for field, ref in enumerate((phi, sol)):
        guest = edge(ref, planes - 1)
        for k in range(planes - 1):
            cross[field * (planes - 1) + k] = host(rowid, edge(ref, k), guest, k)
    cross[2 * (planes - 1)] = level(edge(seed))
    count = part.shape[0]

    @pl.when(jnp.logical_not(odd_core()))
    def _():
        part[...] = sol[planes - count : planes]

    @pl.when(odd_core())
    def _():
        part[...] = sol[0:count]


def parts_kernel(phi, sol, part_a, part_b, tops):
    count = part_a.shape[0]
    planes = phi.shape[0]
    low, high = slice(0, count), slice(planes - count, planes)
    tops[0] = phi[ABOVE - 1]
    tops[1] = sol[ABOVE - 1]

    @pl.when(jnp.logical_not(odd_core()))
    def _():
        part_a[...] = phi[low]
        part_b[...] = phi[high]

    @pl.when(odd_core())
    def _():
        part_a[...] = phi[high]
        part_b[...] = phi[low]


def pack_parts(phi, sol):
    part = array(ABOVE - 1, *phi.shape[1:])
    return pl.pallas_call(
        parts_kernel,
        out_shape=(part, part, array(2, *phi.shape[1:])),
        in_specs=[VMEM, VMEM],
        out_specs=(VMEM,) * 3,
        cost_estimate=cost(phi.size),
        compiler_params=pltpu.CompilerParams(vmem_limit_bytes=1 << 20),
        name="pack_parts",
    )(phi, sol)


def host(rowid, tile, guest, k):
    low, high = guest_turns(k)
    if k >= RIMMED:
        return tile
    tile = jnp.where(rowid == HALF - 1, pltpu.roll(guest, low, 0), tile)
    return jnp.where(rowid == HALF, pltpu.roll(guest, high, 0), tile)


def hosted(rowid, tiles):
    guest = None
    for k in range(RIMMED):
        low, high = guest_turns(k)
        part = pltpu.roll(tiles[k], SUBLANES - low, 0)
        guest = part if guest is None else jnp.where(rowid == SUBLANES - 1 - k, part, guest)
        part = pltpu.roll(tiles[k], SUBLANES - high, 0)
        guest = jnp.where(rowid == k, part, guest)
    return guest


def pack_edges(phi, sol, seed):
    planes, rows, cols = phi.shape
    return pl.pallas_call(
        functools.partial(edges_kernel, planes),
        out_shape=(
            array(2 * planes + 1, rows, LANES),
            array(2 * planes - 1, SUBLANES, cols),
            array(ABOVE - 1, rows, cols),
            array(*phi.shape),
            array(*phi.shape),
        ),
        in_specs=[HBM, HBM, HBM],
        out_specs=(VMEM,) * 5,
        scratch_shapes=[pltpu.VMEM(seed.shape, jnp.int32), pltpu.SemaphoreType.DMA((3,))],
        cost_estimate=cost(phi.size),
        compiler_params=pltpu.CompilerParams(vmem_limit_bytes=4 << 20),
        name="pack_edges",
    )(*(in_hbm(x) for x in (phi, sol, seed)))


def rows_kernel(planes, main, side, out):
    across = main.shape[2] // LANES
    for k in range(main.shape[0]):
        for t in range(across):
            out[k * across + t] = main[k, :, t * LANES : (t + 1) * LANES]
    rowid = row_of((SUBLANES, LANES))
    lanes = lane_of((SUBLANES, LANES))
    keep = rowid < HALF
    depth = side.shape[1]

    def edge(entry):
        return jnp.where(keep, side[entry, :SUBLANES], side[entry, depth - SUBLANES :])

    corners = []
    for field in range(2):
        guest = edge((field + 1) * planes - 1)
        for k in range(planes - 1):
            corners.append(host(rowid, edge(field * planes + k), guest, k))
    corners.append(edge(2 * planes))
    packed = corners[0]
    for k, corner in enumerate(corners[1:], 1):
        near = (lanes >= k * LANE_STEP - HALF) & (lanes < k * LANE_STEP + HALF)
        packed = jnp.where(near, pltpu.roll(corner, k * LANE_STEP, 1), packed)
    out[main.shape[0] * across] = packed


def pack_rows(planes, main, side):
    count, _, cols = main.shape
    return pl.pallas_call(
        functools.partial(rows_kernel, planes),
        out_shape=array(count * (cols // LANES) + 1, SUBLANES, LANES),
        in_specs=[VMEM, VMEM],
        out_specs=VMEM,
        cost_estimate=cost(main.size),
        compiler_params=pltpu.CompilerParams(vmem_limit_bytes=2 << 20),
        name="pack_rows",
    )(main, side)


class Rows:
    def __init__(self, ref, planes):
        self.ref, self.main = ref, (ref.shape[0] - 1) // (2 * planes - 1)

    def tile(self, k, t):
        if t < self.main:
            return self.ref[k * self.main + t]
        corner = self.ref[self.ref.shape[0] - 1]
        return pltpu.roll(corner, LANES - k * LANE_STEP, 1) if k else corner

    def __getitem__(self, k):
        return jnp.concatenate([self.tile(k, t) for t in range(self.main + 1)], axis=1)


RIM_TILES = 3


def put_rims(out, tiles, columns):
    lanes = lane_of((SUBLANES, LANES))
    place, corners = 0, None
    for k, tile in enumerate(tiles):
        for start in range(0, tile.shape[1] - LANES, LANES):
            out[place : place + SUBLANES, :] = tile[:, start : start + LANES]
            place += SUBLANES
        corner = tile[:, tile.shape[1] - LANES :]
        if k:
            near = (lanes >= k * LANE_STEP - HALF) & (lanes < k * LANE_STEP + HALF)
            corner = jnp.where(near, pltpu.roll(corner, k * LANE_STEP, 1), corners)
        corners = corner
    place = RIM_TILES * (tiles[0].shape[1] - LANES) // LANES * SUBLANES
    out[place : place + SUBLANES, :] = corners
    depth = columns.shape[0] // 2
    lanes = lane_of((depth, LANES))
    moved = pltpu.roll(columns[depth:], LANES // 2, 1)
    away = (lanes >= LANES // 2 - SUBLANES) & (lanes < LANES - SUBLANES)
    out[place + SUBLANES :, :] = jnp.where(away, moved, columns[:depth])


def get_row_tile(ref, k, tiles):
    main = tiles - 1
    at = lambda n: slice(n * SUBLANES, (n + 1) * SUBLANES)
    corner = ref[at(RIM_TILES * main), :]
    corner = pltpu.roll(corner, LANES - k * LANE_STEP, 1) if k else corner
    return [ref[at(k * main + t), :] for t in range(main)] + [corner]


def get_columns(ref, k, tiles):
    packed = ref[(RIM_TILES * (tiles - 1) + 1) * SUBLANES :, :]
    low = pltpu.roll(packed, LANES - k * SUBLANES, 1) if k else packed
    high = pltpu.roll(packed, LANES // 2 - k * SUBLANES, 1)
    return jnp.concatenate([low, high], axis=0)


def rims_kernel(planes, cross, side, rim_a, rim_b):
    other = planes - 1
    cross = Rows(cross, planes)
    rowid = row_of((SUBLANES, (cross.main + 1) * LANES))
    lanes = lane_of(side.shape[1:])
    inner = (rowid == HALF - 1) | (rowid == HALF)
    middle = (rowid >= HALF - 2) & (rowid < HALF + 2)
    turn = lambda tile: pltpu.roll(tile, HALF, 0)

    def columns(entries):
        packed = side[entries[0]]
        for k, entry in enumerate(entries[1:], 1):
            moved = pltpu.roll(side[entry], k * SUBLANES, 1)
            near = (lanes >= k * SUBLANES - HALF) & (lanes < k * SUBLANES + HALF)
            packed = jnp.where(near, moved, packed)
        return packed

    def fill(down, up):
        tiles = [
            jnp.where(inner, turn(cross[2]), cross[0]),
            jnp.where(inner, turn(cross[other + 2]), cross[other]),
            jnp.where(middle, turn(cross[other + 1]), cross[1]),
        ]
        put_rims(down, tiles, columns([0, planes, 1, planes + 1, 2, planes + 2]))
        tiles = [jnp.where(inner, cross[other], turn(cross[0]))]
        put_rims(up, tiles, columns([planes - 1, 2 * planes - 1]))

    @pl.when(jnp.logical_not(odd_core()))
    def _():
        fill(rim_a, rim_b)

    @pl.when(odd_core())
    def _():
        fill(rim_b, rim_a)


def pack_rims(planes, cross, side):
    main = (cross.shape[0] - 1) // (2 * planes - 1)
    rim = array((RIM_TILES * main + 1) * SUBLANES + side.shape[1] // 2, LANES)
    return pl.pallas_call(
        functools.partial(rims_kernel, planes),
        out_shape=(rim, rim),
        in_specs=[VMEM, VMEM],
        out_specs=(VMEM, VMEM),
        cost_estimate=cost(rim.size),
        compiler_params=pltpu.CompilerParams(vmem_limit_bytes=2 << 20),
        name="pack_rims",
    )(cross, side)


def mobility(phi):
    return 1.0 - jnp.clip(phi, -1.0, 1.0)


class Either:
    def __init__(self, even, odd, even_skip=0, odd_skip=0):
        self.even, self.odd, self.shape = even, odd, even.shape
        self.skips = (even_skip, odd_skip)

    def __getitem__(self, at):
        if any(self.skips):
            even, odd = ((at[0] + skip, *at[1:]) for skip in self.skips)
        else:
            even = odd = at
        return jnp.where(odd_core(), self.odd[odd], self.even[even])


class Field:
    def __init__(self, phi, sol, mob, planes):
        self.phi, self.sol, self.mob = phi, sol, mob
        self.planes = planes
        self.tiles = phi.shape[1]
        self.rows = phi.shape[2] - 2 * SUBLANES
        self.base = BELOW
        self.top = BELOW + planes

    def put(self, e, t, at, p, u):
        self.phi[e, t, at, :] = p
        self.sol[e, t, at, :] = u
        self.mob[e, t, at, :] = mobility(p)

    def put_block(self, e, phi, sol, k, j):
        for t in range(self.tiles - 1):
            lanes = slice(t * LANES, (t + 1) * LANES)
            at = slice(SUBLANES, SUBLANES + self.rows)
            self.put(e, t, at, phi[k, :, lanes], sol[j, :, lanes])

    def put_columns(self, e, p, u):
        self.put(e, self.tiles - 1, slice(SUBLANES, SUBLANES + self.rows), p, u)

    def put_rows(self, e, p, u):
        for t in range(self.tiles):
            for start in (0, SUBLANES + self.rows):
                self.put(e, t, slice(start, start + SUBLANES), p[t], u[t])


def ends(moved, field, e):
    grow_index = lax.axis_index("grow")
    at_bottom = grow_index == 0
    at_top = grow_index == lax.axis_size("grow") - 1
    low_end = jnp.where(moved, field.base + 1, field.base)
    high_end = jnp.where(moved, field.top, field.top - 1)
    lower = jnp.where(at_bottom & (e == low_end), e, e - 1)
    upper = jnp.where(at_top & (e == high_end), e, e + 1)
    return lower, upper


def covered(field, halo):
    tiles = range(field.tiles if halo else field.tiles - 1)
    parts = [(SUBLANES + start, tiles) for start in range(0, field.rows, SUBLANES)]
    return parts + ([halo_part(field, halo)] if halo else [])


def halo_part(field, halo):
    return (SUBLANES + field.rows, range(field.tiles if halo > 1 else field.tiles - 1))


def rimmed(field, halo):
    last = [field.tiles - 1]
    return [halo_part(field, halo)] + [(start, last) for start, _ in covered(field, 0)]


def step_plane(step, moved, source, e, parts, write):
    lower, upper = ends(moved, source, e)
    planes = source.planes
    grid_planes = planes * lax.axis_size("grow")
    height = (lax.axis_index("grow") * planes + e - source.base).astype(F32)
    height = jnp.broadcast_to(height, (SUBLANES, LANES))
    temper = gradient_scale * ((height + 0.5) * (1.0 / grid_planes) - 0.5) - drift_rate * step
    pace = time_step / (1.0 - (1.0 - partition) * temper)
    kappa = 0.25 * diffusion * time_step / spacing_sq
    pull = pace * (1.0 / spacing_sq)
    drive = pace * coupling
    rest = pull * 6.0
    tiles = source.tiles
    lanes = lane_of((SUBLANES, LANES))
    heads = lanes == 0
    tails = lanes == LANES - 1
    for start, outputs in parts:

        outside = start == SUBLANES + source.rows

        def load(ref, t, plane=e, by=0):
            low = 1 if outside and by > 0 else start + by
            return ref[plane, t, low : low + SUBLANES, :]

        def after(values, t):
            return pltpu.roll(jnp.where(heads, values[(t + 1) % tiles], values[t]), LANES - 1, 1)

        def before(values, t):
            return pltpu.roll(jnp.where(tails, values[t - 1], values[t]), 1, 1)

        p_all = [load(source.phi, t) for t in range(tiles)]
        u_all = [load(source.sol, t) for t in range(tiles)]
        m_all = [load(source.mob, t) for t in range(tiles)]
        p_next = [after(p_all, t) for t in range(tiles)]
        flux = [
            (m_all[t] + mobility(p_next[t])) * (after(u_all, t) - u_all[t]) for t in range(tiles)
        ]
        for t in outputs:
            p, u, m = p_all[t], u_all[t], m_all[t]
            total = p_next[t] + before(p_all, t)
            flow = flux[t] - before(flux, t)
            for where in (dict(by=-1), dict(by=1), dict(plane=lower), dict(plane=upper)):
                total = total + load(source.phi, t, **where)
                other = load(source.sol, t, **where)
                flow = flow + (m + load(source.mob, t, **where)) * (other - u)
            well = 1.0 - p * p
            gain = pull * total + p * (pace * well - rest) - drive * (well * well) * (u + temper)
            weight = partition / kappa + (0.5 * (1.0 - partition) / kappa) * m
            change = flow + (0.5 / kappa + (0.5 * (1.0 - partition) / kappa) * u) * gain
            new_p, new_u = p + gain, u + change / weight
            write(e, t, slice(start, start + SUBLANES), new_p, new_u)
            if outside:
                write(e, t, slice(0, SUBLANES), new_p, new_u)


def early_kernel(planes, phi, sol, side, cross, *rest):
    first = Field(*rest[:3], planes)
    second = Field(*rest[3:6], planes)
    base, top, tiles = first.base, first.top, first.tiles
    rowid = row_of((SUBLANES, LANES))
    cross = Rows(cross, planes)
    other = planes - 1
    for k in range(planes):
        first.put_columns(base + k, side[k], side[planes + k])
        if k < other:
            p = [cross.tile(k, t) for t in range(tiles)]
            u = [cross.tile(other + k, t) for t in range(tiles)]
        else:
            p, u = [
                [
                    hosted(rowid, [cross.tile(f * other + j, t) for j in range(RIMMED)])
                    for t in range(tiles)
                ]
                for f in range(2)
            ]
        first.put_rows(base + k, p, u)
    for k in range(planes):
        first.put_block(base + k, phi, sol, k, k)

    @pl.loop(base + 1, top - 1)
    def _(e):
        step_plane(0, False, first, e, covered(first, 2), second.put)


def levels_of(refs, planes):
    return [Field(*refs[k : k + 3], planes) for k in (0, 3, 6)]


def fetch(source, target, sem):
    copy = pltpu.make_async_copy(source, target, sem)
    copy.start()

    def value():
        copy.wait()
        return target[0]

    return value


FETCHED = [pltpu.SMEM((1,), jnp.int32), pltpu.SemaphoreType.DMA]


def middle_kernel(planes, shift_ref, phi_a, phi_b, sol_a, sol_b, *rest):
    first, second, third = levels_of(rest[6:15], planes)
    fetched = fetch(shift_ref, *rest[15:])
    base, top = first.base, first.top
    for k in range(ABOVE - 1):
        first.put_block(top + k, Either(phi_a, phi_b), Either(sol_a, sol_b), k, k)
    for k in range(BELOW):
        j = ABOVE - 1 - BELOW + k
        sol = Either(sol_b, sol_a, 0, planes - ABOVE + 1)
        first.put_block(k, Either(phi_b, phi_a), sol, j, j)

    @pl.loop(0, 2)
    def _(k):
        step_plane(0, False, first, jnp.where(k == 0, base, top - 1), covered(first, 0), second.put)

    moved = fetched() < 1

    @pl.loop(base + 1, top - 1)
    def _(e):
        step_plane(1, moved, second, e, covered(second, 0), third.put)


def late_kernel(planes, shift_ref, side, cross, rim_a, rim_b, levels, *rest):
    first, second, third = levels_of(rest[11:20], planes)
    phi_out, sol_out = rest[9:11]
    fetched = fetch(shift_ref, *rest[20:])
    base, top, tiles, rows = first.base, first.top, first.tiles, first.rows
    at_top = lax.axis_index("grow") == lax.axis_size("grow") - 1
    turn = lambda group: [pltpu.roll(tile, HALF, 0) for tile in group]
    rim_down, rim_up = Either(rim_a, rim_b), Either(rim_b, rim_a)
    p = get_row_tile(rim_down, 0, tiles)
    u = get_row_tile(rim_down, 1, tiles)
    first.put_rows(top, p, u)
    first.put_rows(top + 2, turn(p), turn(u))
    p = get_row_tile(rim_down, 2, tiles)
    first.put_rows(top + 1, p, turn(p))
    p = get_row_tile(rim_up, 0, tiles)
    first.put_rows(base - 1, p, turn(p))

    for k in range(RIMMED):
        p, u = (get_columns(rim_down, 2 * k + f, tiles) for f in range(2))
        first.put_columns(top + k, p, u)
    first.put_columns(base - 1, get_columns(rim_up, 0, tiles), get_columns(rim_up, 1, tiles))

    def bring_top(field):
        def fill(t, at, value):
            field.put(top, t, at, jnp.full(value.shape, -1.0, F32), value)

        body = slice(SUBLANES, SUBLANES + rows)
        for t in range(tiles - 1):
            fill(t, body, level(levels[:, t * LANES : (t + 1) * LANES]))
        fill(tiles - 1, body, side[2 * planes])
        for t in range(tiles):
            value = Rows(cross, planes).tile(2 * (planes - 1), t)
            fill(t, slice(0, SUBLANES), value)
            fill(t, slice(SUBLANES + rows, 2 * SUBLANES + rows), value)

    @pl.loop(top, top + 2)
    def _(e):
        step_plane(0, False, first, e, covered(first, 2), second.put)

    @pl.loop(0, 2)
    def _(k):
        step_plane(0, False, first, jnp.where(k == 0, base, top - 1), rimmed(first, 2), second.put)

    step_plane(0, False, first, base - 1, covered(first, 0), second.put)
    shift = fetched()
    moved = shift < 1

    @pl.when(at_top & (shift == 0))
    def _():
        bring_top(second)

    @pl.loop(top - 1, top + 1)
    def _(e):
        step_plane(1, moved, second, e, covered(second, 1), third.put)

    @pl.loop(base + 1, top - 1)
    def _(e):
        step_plane(1, moved, second, e, rimmed(second, 1), third.put)

    step_plane(1, moved, second, base, covered(second, 0), third.put)

    @pl.when(at_top & (shift == 1))
    def _():
        bring_top(third)

    @pl.loop(base + 1, top)
    def _(e):
        step_plane(2, True, third, e, covered(third, 0), into(phi_out, sol_out, base + 1))


def into(phi_out, sol_out, lowest):
    def write(e, t, at, p, u):
        at = slice(at.start - SUBLANES, at.stop - SUBLANES)
        lanes = slice(t * LANES, (t + 1) * LANES)
        phi_out[e - lowest, at, lanes] = p
        sol_out[e - lowest, at, lanes] = u

    return write


def final_kernel(planes, tops, sol_a, phi_in, sol_in, *rest):
    phi_out, sol_out = rest[9:11]
    first, second, third = levels_of(rest[11:20], planes)
    phi_buf, sol_buf, sems = rest[20:]
    top = first.top
    done = pl.ds(0, planes - 1)
    copies = start_all(
        sems, [(phi_in.at[done], phi_out.at[done]), (sol_in.at[done], sol_out.at[done])]
    )
    edge = top + ABOVE - 1
    first.put_block(edge, tops, Either(sol_a, tops, ABOVE - 1, 1), 0, 0)
    step_plane(0, False, first, edge - 1, covered(first, 0), second.put)
    step_plane(1, False, second, edge - 2, covered(second, 0), third.put)
    step_plane(2, True, third, edge - 3, covered(third, 0), into(phi_buf, sol_buf, edge - 3))
    copies += start_all(
        sems.at[pl.ds(2, 2)],
        [(phi_buf.at[0], phi_out.at[planes - 1]), (sol_buf.at[0], sol_out.at[planes - 1])],
    )
    for copy in copies:
        copy.wait()


def early(phi, sol, side, cross):
    planes, rows, cols = phi.shape
    state = array(planes + BELOW + ABOVE, cols // LANES + 1, rows + 2 * SUBLANES, LANES)
    return pl.pallas_call(
        functools.partial(early_kernel, planes),
        out_shape=(state,) * 6,
        in_specs=[VMEM] * 4,
        out_specs=(VMEM,) * 6,
        cost_estimate=cost(64 * phi.size),
        compiler_params=pltpu.CompilerParams(vmem_limit_bytes=8 << 20),
        name="early",
    )(phi, sol, side, cross)


def same(arrays):
    return tuple(array(*a.shape) for a in arrays)


def middle(planes, shift, received, state):
    return pl.pallas_call(
        functools.partial(middle_kernel, planes),
        out_shape=same(state) + same(state[:3]),
        in_specs=[HBM] + [VMEM] * 10,
        out_specs=(VMEM,) * 9,
        scratch_shapes=FETCHED,
        input_output_aliases={5 + k: k for k in range(6)},
        cost_estimate=cost(64 * received[0].size),
        compiler_params=pltpu.CompilerParams(vmem_limit_bytes=8 << 20),
        name="middle",
    )(shift, *received, *state)


def late(shift, side, cross, rim_a, rim_b, seed, state, shape):
    out = pl.pallas_call(
        functools.partial(late_kernel, shape[0]),
        out_shape=(array(*shape), array(*shape)) + same(state),
        in_specs=[HBM] + [VMEM] * 14,
        out_specs=(VMEM,) * 11,
        scratch_shapes=FETCHED,
        input_output_aliases={6 + k: 2 + k for k in range(9)},
        cost_estimate=cost(3 * 64 * state[0].size),
        compiler_params=pltpu.CompilerParams(vmem_limit_bytes=8 << 20),
        name="late",
    )(shift, side, cross, rim_a, rim_b, seed, *state)
    return out[:2], out[2:]


def final(tops, sol_a, outs, state, shape):
    planes = shape[0]
    out = pl.pallas_call(
        functools.partial(final_kernel, planes),
        out_shape=(array(*shape), array(*shape)) + same(state),
        in_specs=[VMEM] * 13,
        out_specs=(HBM, HBM) + (VMEM,) * 9,
        input_output_aliases={4 + k: 2 + k for k in range(9)},
        scratch_shapes=[
            pltpu.VMEM((1,) + shape[1:], F32),
            pltpu.VMEM((1,) + shape[1:], F32),
            pltpu.SemaphoreType.DMA((4,)),
        ],
        cost_estimate=cost(64 * tops.size),
        compiler_params=pltpu.CompilerParams(vmem_limit_bytes=8 << 20),
        name="final",
    )(tops, sol_a, *outs, *state)
    return out[0], out[1]


def swap_edges(message, axis, keep):
    size = lax.axis_size(axis)
    if size <= 2:
        return lax.ppermute(message, axis, ring(size, 1))
    after = lax.ppermute(message, axis, ring(size, -1))
    before = lax.ppermute(message, axis, ring(size, 1))
    return jnp.where(keep, after, before)


def steps(phi, sol, shift_step, seed):
    planes = phi.shape[0]
    size, lanes = lax.axis_size("grow"), lax.axis_size("side")
    both = ("grow", "side")
    even_down, even_up = two_way(size, lanes, -1), two_way(size, lanes, 1)
    sol_a = lax.ppermute(sol, both, even_down)
    side, cross, sol_b, phi, sol = pack_edges(phi, sol, seed)
    sol_b = lax.ppermute(sol_b, both, even_up)
    phi_a, phi_b, tops = pack_parts(phi, sol)
    phi_a = lax.ppermute(phi_a, both, even_down)
    phi_b = lax.ppermute(phi_b, both, even_up)
    side = swap_edges(side, "side", lane_of(side.shape) < LANES // 2)
    cross = pack_rows(planes, cross, side)
    rowid = row_of(cross.shape)
    cross = swap_edges(cross, "cross", (rowid < HALF - 1) | (rowid == HALF))
    rim_a, rim_b = pack_rims(planes, cross, side)
    rim_a = lax.ppermute(rim_a, both, even_down)
    rim_b = lax.ppermute(rim_b, both, even_up)
    tops = lax.ppermute(tops, "grow", ring(size, -1))
    state = early(phi, sol, side, cross)
    state = middle(planes, shift_step, (phi_a, phi_b, sol_a, sol_b), state)
    outs, state = late(shift_step, side, cross, rim_a, rim_b, seed, state, phi.shape)
    return final(tops, sol_a, outs, state, phi.shape)


def solution(mesh):
    return jax.shard_map(
        steps,
        mesh=mesh,
        in_specs=(
            P(("groups", "grow"), "cross", "side"),
            P(("groups", "grow"), "cross", "side"),
            P("groups"),
            P(("groups", "cross"), "side"),
        ),
        out_specs=(P(("groups", "grow"), "cross", "side"), P(("groups", "grow"), "cross", "side")),
        check_vma=False,
    )
```

time: 29.5 us -> 25.2 us (0.85)
  waiting for transfers between devices: 4.97 us -> 2.73 us
  local copies, waits for them, and re-layouts: 0.97 us -> 0.01 us
  starting transfers between devices: 13.8 us -> 13.1 us
    ppermute x1, waiting for transfers between devices: 1.57 us -> 0.01 us  [steps(): phi_b = lax.ppermute(phi_b, both, even_up)]
    ppermute x2, waiting for transfers between devices: 3.38 us -> 1.85 us  [swap_edges(): return lax.ppermute(message, axis, ring(size, 1))]
    ppermute x2, starting transfers between devices: 7.21 us -> 6.1 us  [the longest x1 3.52 us: steps(): tops = lax.ppermute(tops, 'grow', ring(size, -1))]
    unnamed x8 -> x2, local copies, waits for them, and re-layouts: 0.97 us -> 0.01 us
    ppermute x1, waiting for transfers between devices: 0.01 us -> 0.86 us  [steps(): phi_a = lax.ppermute(phi_a, both, even_down)]
    ppermute x1, starting transfers between devices: 2.01 us -> 2.46 us  [steps(): rim_b = lax.ppermute(rim_b, both, even_up)]
  transfers between devices with their start and end apart: 9 -> 9, of which waited for: 2 -> 2; matrix products, arithmetic and copies ran while one was open for 0% -> 0% of each run, Pallas kernels for 18% -> 21%
where the time goes in v5:
time: 25.2 us; the launch traced here: 25.1 us
  starting transfers between devices  13.1 us (52%)
  Pallas kernels  7.79 us (31%)
  waiting for transfers between devices  2.73 us (11%)
  between operations  1.39 us (6%)
    ppermute x1, starting transfers between devices, steps(): tops = lax.ppermute(tops, 'grow', ring(size, -1))  3.52 us
    pallas_call x1, Pallas kernels, late(): pl.pallas_call(functools.partial(late_kernel, shape[0]), out_shape=(array...  3.22 us
    ppermute x1, starting transfers between devices, steps(): sol_b = lax.ppermute(sol_b, both, even_up)  2.59 us
    ppermute x1, starting transfers between devices, steps(): rim_b = lax.ppermute(rim_b, both, even_up)  2.46 us
    ppermute x2, starting transfers between devices, swap_edges(): return lax.ppermute(message, axis, ring(size, 1))  2.34 us
    ppermute x1, starting transfers between devices, steps(): phi_b = lax.ppermute(phi_b, both, even_up)  2 us
    ppermute x2, waiting for transfers between devices, swap_edges(): return lax.ppermute(message, axis, ring(size, 1))  1.85 us
    pallas_call x1, Pallas kernels, final(): pl.pallas_call(functools.partial(final_kernel, planes), out_shape=(array(...  1.42 us
  transfers between devices with their start and end apart: 9, of which 2 were waited for; matrix products, arithmetic and copies ran while one was open for 0% of the time, Pallas kernels for 21%

profile of v5, /device:TPU:0, one launch (start us, length us, event | category | flops | bytes accessed | tf_op | source)
XLA Modules:
  0.0 25.1 jit_solution(9111297693117284087)
XLA Ops:
  0.6 1.1 %pack_edges.1 = (f32[9,32,128]{2,1,0:T(8,128)S(1)}, f32[7,8,512]{2,1,0:T(8,128)S(1)}, f32[3,32,512]{2,1,0:T(8,128)S(1)}, f32[4,32,512]{2,1,0:T(8,128)S(1)}, f32[4,32,512]{2,1,0:T(8,128)S(1)}) custom-call(f32[4,32,512]{2,1,0:T(8,128)} %phi_in.1, f32[4,32,512]{2,1,0:T(8,128)} %sol_in.1, s32[32,512]{1,0:T(8,128)} %levels.1), custom_call_target="tpu_custom_call" | custom-call | flops 65536 | bytes 262144 | tf_op jit(solution)/shard_map/pack_edges/pallas_call | solution.py:181
  1.7 0.6 %collective-permute-start.2 = (f32[9,32,128]{2,1,0:T(8,128)S(1)}, f32[9,32,128]{2,1,0:T(8,128)S(1)}, u32[]{:S(2)}, u32[]{:S(2)}) collective-permute-start(f32[9,32,128]{2,1,0:T(8,128)S(1)} %get-tuple-element.43), channel_id=1, source_target_pairs={{0,1},{1,0},{2,3},{3,2},{4,5},{5,4},{6,7},{7,6},{8,9},{9,8},{10,11... | collective-permute-start | bytes 442376 | tf_op jit(solution)/shard_map/ppermute | solution.py:709
  2.3 0.0 collective-permute-start.1
  2.3 2.6 %collective-permute-start.8 = (f32[3,32,512]{2,1,0:T(8,128)S(1)}, f32[3,32,512]{2,1,0:T(8,128)S(1)}, u32[]{:S(2)}, u32[]{:S(2)}) collective-permute-start(f32[3,32,512]{2,1,0:T(8,128)S(1)} %get-tuple-element.49), channel_id=1, source_target_pairs={{0,4},{1,0},{4,8},{5,1},{8,12},{9,5},{12,13},{13,9},{2,6},{3,2},{6... | collective-permute-start | bytes 589832 | tf_op jit(solution)/shard_map/ppermute | solution.py:722
  5.0 0.2 collective-permute-start.6
  5.2 0.0 collective-permute-done.2.side
  5.2 0.1 pack_rows.1
  5.2 1.8 %collective-permute-start.3 = (f32[29,8,128]{2,1,0:T(8,128)S(1)}, f32[29,8,128]{2,1,0:T(8,128)S(1)}, u32[]{:S(2)}, u32[]{:S(2)}) collective-permute-start(f32[29,8,128]{2,1,0:T(8,128)S(1)} %pack_rows.1), channel_id=1, source_target_pairs={{0,2},{2,0},{1,3},{3,1},{4,6},{6,4},{5,7},{7,5},{8,10},{10,8},{9,1... | collective-permute-start | bytes 356360 | tf_op jit(solution)/shard_map/ppermute | solution.py:709
  7.0 2.0 %collective-permute-start.7 = (f32[3,32,512]{2,1,0:T(8,128)S(1)}, f32[3,32,512]{2,1,0:T(8,128)S(1)}, u32[]{:S(2)}, u32[]{:S(2)}) collective-permute-start(f32[3,32,512]{2,1,0:T(8,128)S(1)} %get-tuple-element.48), channel_id=1, source_target_pairs={{0,4},{1,0},{4,8},{5,1},{8,12},{9,5},{12,13},{13,9},{2,6},{3,2},{6... | collective-permute-start | bytes 589832 | tf_op jit(solution)/shard_map/ppermute | solution.py:725
  9.0 1.9 %collective-permute-done.3.cross = f32[29,8,128]{2,1,0:T(8,128)S(1)} collective-permute-done((f32[29,8,128]{2,1,0:T(8,128)S(1)}, f32[29,8,128]{2,1,0:T(8,128)S(1)}, u32[]{:S(2)}, u32[]{:S(2)}) %collective-permute-start.3) | collective-permute-done | bytes 118816 | tf_op jit(solution)/shard_map/ppermute | solution.py:709
  10.9 3.5 %collective-permute-start = (f32[2,32,512]{2,1,0:T(8,128)S(1)}, f32[2,32,512]{2,1,0:T(8,128)S(1)}, u32[]{:S(2)}, u32[]{:S(2)}) collective-permute-start(f32[2,32,512]{2,1,0:T(8,128)S(1)} %get-tuple-element.42), channel_id=1, source_target_pairs={{0,12},{4,0},{8,4},{12,8},{1,13},{5,1},{9,5},{13,9},{2,14},{6,2},{... | collective-permute-start | bytes 393224 | tf_op jit(solution)/shard_map/ppermute | solution.py:733
  14.4 0.1 pack_rims.1
  14.5 0.0 collective-permute-done.8.sol_b
  14.6 0.0 collective-permute-start.4
  14.6 0.9 %collective-permute-done.6.phi_a = f32[3,32,512]{2,1,0:T(8,128)S(1)} collective-permute-done((f32[3,32,512]{2,1,0:T(8,128)S(1)}, f32[3,32,512]{2,1,0:T(8,128)S(1)}, u32[]{:S(2)}, u32[]{:S(2)}) %collective-permute-start.6) | collective-permute-done | bytes 196640 | tf_op jit(solution)/shard_map/ppermute | solution.py:724
  15.4 2.5 %collective-permute-start.5 = (f32[120,128]{1,0:T(8,128)S(1)}, f32[120,128]{1,0:T(8,128)S(1)}, u32[]{:S(2)}, u32[]{:S(2)}) collective-permute-start(f32[120,128]{1,0:T(8,128)S(1)} %get-tuple-element.46), channel_id=1, source_target_pairs={{0,4},{1,0},{4,8},{5,1},{8,12},{9,5},{12,13},{13,9},{2,6},{3,2},{6... | collective-permute-start | bytes 184328 | tf_op jit(solution)/shard_map/ppermute | solution.py:732
  18.5 0.7 %early.1 = (f32[10,5,48,128]{3,2,1,0:T(8,128)S(1)}, f32[10,5,48,128]{3,2,1,0:T(8,128)S(1)}, f32[10,5,48,128]{3,2,1,0:T(8,128)S(1)}, f32[10,5,48,128]{3,2,1,0:T(8...) custom-call(f32[4,32,512]{2,1,0:T(8,128)S(1)} %get-tuple-element.40.phi, ...), custom_call_target="tpu_custom_call" | custom-call | flops 4194304 | bytes 16777216 | tf_op jit(solution)/shard_map/early/pallas_call | solution.py:642
  19.3 0.0 collective-permute-done.7.phi_b
  19.3 0.0 collective-permute-done.1.sol_a
  19.3 0.0 copy-start
  19.3 1.1 %middle.1 = (f32[10,5,48,128]{3,2,1,0:T(8,128)S(1)}, f32[10,5,48,128]{3,2,1,0:T(8,128)S(1)}, f32[10,5,48,128]{3,2,1,0:T(8,128)S(1)}, f32[10,5,48,128]{3,2,1,0:T(...) custom-call(s32[1]{0:T(128)S(6)} %copy.54.shift_ref, ...), custom_call_target="tpu_custom_call", output_to_operand_aliasing={{0}: (5, {}), {1}: (6, {}), {2}: (7, {}), {3}: (8, {}), {4}... | custom-call | flops 3145728 | bytes 12582912 | tf_op jit(solution)/shard_map/middle/pallas_call | solution.py:658
  20.4 0.0 collective-permute-done.4.rim_a
  20.4 0.0 collective-permute-done.5.rim_b
  20.4 0.0 copy-done
  20.4 3.2 %late.1 = (f32[4,32,512]{2,1,0:T(8,128)S(1)}, f32[4,32,512]{2,1,0:T(8,128)S(1)}, f32[10,5,48,128]{3,2,1,0:T(8,128)S(1)}, f32[10,5,48,128]{3,2,1,0:T(8,128)S(1)},...) custom-call(s32[1]{0:T(128)S(6)} %copy.54.shift_ref, ...), custom_call_target="tpu_custom_call", output_to_operand_aliasing={{2}: (6, {}), {3}: (7, {}), {4}: (8, {}), {5}: (9, {}), {6}... | custom-call | flops 58982400 | bytes 235929600 | tf_op jit(solution)/shard_map/late/pallas_call | solution.py:672
  23.6 0.0 collective-permute-done.tops
  23.6 1.4 %final.1 = (f32[4,32,512]{2,1,0:T(8,128)}, f32[4,32,512]{2,1,0:T(8,128)}, f32[10,5,48,128]{3,2,1,0:T(8,128)S(1)}, f32[10,5,48,128]{3,2,1,0:T(8,128)S(1)}, f32[10...) custom-call(f32[2,32,512]{2,1,0:T(8,128)S(1)} %collective-permute-do, ...), custom_call_target="tpu_custom_call", output_to_operand_aliasing={{2}: (4, {}), {3}: (5, {}), {4}: (6, {}), {5}: (7, {}), {6}... | custom-call | flops 2097152 | bytes 8388608 | tf_op jit(solution)/shard_map/final/pallas_call | solution.py:688
  (1 shorter events, 0.0 us)
Async XLA Ops:
  1.7 3.4 %collective-permute-start.2 = (f32[9,32,128]{2,1,0:T(8,128)S(1)}, f32[9,32,128]{2,1,0:T(8,128)S(1)}, u32[]{:S(2)}, u32[]{:S(2)}) collective-permute-start(f32[9,32,128]{2,1,0:T(8,128)S(1)} %get-tuple-element.43), channel_id=1, source_target_pairs={{0,1},{1,0},{2,3},{3,2},{4,5},{5,4},{6,7},{7,6},{8,9},{9,8},{10,11... | collective-permute-start | bytes 442376 | tf_op jit(solution)/shard_map/ppermute | solution.py:709
  2.3 17.0 %collective-permute-start.1 = (f32[4,32,512]{2,1,0:T(8,128)}, f32[4,32,512]{2,1,0:T(8,128)S(1)}, u32[]{:S(2)}, u32[]{:S(2)}) collective-permute-start(f32[4,32,512]{2,1,0:T(8,128)} %sol_in.1), channel_id=1, source_target_pairs={{0,1},{1,5},{4,0},{5,9},{8,4},{9,13},{12,8},{13,12},{2,3},{3,7},{6... | collective-permute-start | bytes 786440 | tf_op jit(solution)/shard_map/ppermute | solution.py:720
  2.3 12.2 %collective-permute-start.8 = (f32[3,32,512]{2,1,0:T(8,128)S(1)}, f32[3,32,512]{2,1,0:T(8,128)S(1)}, u32[]{:S(2)}, u32[]{:S(2)}) collective-permute-start(f32[3,32,512]{2,1,0:T(8,128)S(1)} %get-tuple-element.49), channel_id=1, source_target_pairs={{0,4},{1,0},{4,8},{5,1},{8,12},{9,5},{12,13},{13,9},{2,6},{3,2},{6... | collective-permute-start | bytes 589832 | tf_op jit(solution)/shard_map/ppermute | solution.py:722
  5.0 10.5 %collective-permute-start.6 = (f32[3,32,512]{2,1,0:T(8,128)S(1)}, f32[3,32,512]{2,1,0:T(8,128)S(1)}, u32[]{:S(2)}, u32[]{:S(2)}) collective-permute-start(f32[3,32,512]{2,1,0:T(8,128)S(1)} %get-tuple-element.47), channel_id=1, source_target_pairs={{0,1},{1,5},{4,0},{5,9},{8,4},{9,13},{12,8},{13,12},{2,3},{3,7},{6... | collective-permute-start | bytes 589832 | tf_op jit(solution)/shard_map/ppermute | solution.py:724
  5.2 5.6 %collective-permute-start.3 = (f32[29,8,128]{2,1,0:T(8,128)S(1)}, f32[29,8,128]{2,1,0:T(8,128)S(1)}, u32[]{:S(2)}, u32[]{:S(2)}) collective-permute-start(f32[29,8,128]{2,1,0:T(8,128)S(1)} %pack_rows.1), channel_id=1, source_target_pairs={{0,2},{2,0},{1,3},{3,1},{4,6},{6,4},{5,7},{7,5},{8,10},{10,8},{9,1... | collective-permute-start | bytes 356360 | tf_op jit(solution)/shard_map/ppermute | solution.py:709
  7.0 12.3 %collective-permute-start.7 = (f32[3,32,512]{2,1,0:T(8,128)S(1)}, f32[3,32,512]{2,1,0:T(8,128)S(1)}, u32[]{:S(2)}, u32[]{:S(2)}) collective-permute-start(f32[3,32,512]{2,1,0:T(8,128)S(1)} %get-tuple-element.48), channel_id=1, source_target_pairs={{0,4},{1,0},{4,8},{5,1},{8,12},{9,5},{12,13},{13,9},{2,6},{3,2},{6... | collective-permute-start | bytes 589832 | tf_op jit(solution)/shard_map/ppermute | solution.py:725
  10.9 12.8 %collective-permute-start = (f32[2,32,512]{2,1,0:T(8,128)S(1)}, f32[2,32,512]{2,1,0:T(8,128)S(1)}, u32[]{:S(2)}, u32[]{:S(2)}) collective-permute-start(f32[2,32,512]{2,1,0:T(8,128)S(1)} %get-tuple-element.42), channel_id=1, source_target_pairs={{0,12},{4,0},{8,4},{12,8},{1,13},{5,1},{9,5},{13,9},{2,14},{6,2},{... | collective-permute-start | bytes 393224 | tf_op jit(solution)/shard_map/ppermute | solution.py:733
  14.6 5.8 %collective-permute-start.4 = (f32[120,128]{1,0:T(8,128)S(1)}, f32[120,128]{1,0:T(8,128)S(1)}, u32[]{:S(2)}, u32[]{:S(2)}) collective-permute-start(f32[120,128]{1,0:T(8,128)S(1)} %get-tuple-element.45), channel_id=1, source_target_pairs={{0,1},{1,5},{4,0},{5,9},{8,4},{9,13},{12,8},{13,12},{2,3},{3,7},{6... | collective-permute-start | bytes 184328 | tf_op jit(solution)/shard_map/ppermute | solution.py:731
  15.4 5.0 %collective-permute-start.5 = (f32[120,128]{1,0:T(8,128)S(1)}, f32[120,128]{1,0:T(8,128)S(1)}, u32[]{:S(2)}, u32[]{:S(2)}) collective-permute-start(f32[120,128]{1,0:T(8,128)S(1)} %get-tuple-element.46), channel_id=1, source_target_pairs={{0,4},{1,0},{4,8},{5,1},{8,12},{9,5},{12,13},{13,9},{2,6},{3,2},{6... | collective-permute-start | bytes 184328 | tf_op jit(solution)/shard_map/ppermute | solution.py:732
  19.3 1.1 %copy-start = (s32[32,512]{1,0:T(8,128)S(1)}, s32[32,512]{1,0:T(8,128)}, u32[]{:S(2)}) copy-start(s32[32,512]{1,0:T(8,128)} %levels.1) | copy-start | bytes 196612

commit v6 on v5

--- a/solution.py
+++ b/solution.py
@@ -29,6 +29,10 @@
 
 def ring(size, by):
     return [(i, (i + by) % size) for i in range(size)]
+
+
+def chain(size, by):
+    return [(i, i + by) for i in range(size) if 0 <= i + by < size]
 
 
 def two_way(size, lanes, even_by):
@@ -340,6 +344,22 @@
 
 def mobility(phi):
     return 1.0 - jnp.clip(phi, -1.0, 1.0)
+
+
+def carry_kernel(shift_ref, out):
+    out[...] = jnp.full(out.shape, shift_ref[0], jnp.int32)
+
+
+def carry(shift):
+    return pl.pallas_call(
+        carry_kernel,
+        out_shape=jax.ShapeDtypeStruct((SUBLANES, LANES), jnp.int32),
+        in_specs=[SMEM],
+        out_specs=VMEM,
+        cost_estimate=cost(SUBLANES * LANES),
+        compiler_params=pltpu.CompilerParams(vmem_limit_bytes=1 << 20),
+        name="carry",
+    )(shift)
 
 
 class Either:
@@ -504,12 +524,12 @@
 
     def value():
         copy.wait()
-        return target[0]
+        return target[0, 0]
 
     return value
 
 
-FETCHED = [pltpu.SMEM((1,), jnp.int32), pltpu.SemaphoreType.DMA]
+FETCHED = [pltpu.SMEM((SUBLANES, LANES), jnp.int32), pltpu.SemaphoreType.DMA]
 
 
 def middle_kernel(planes, shift_ref, phi_a, phi_b, sol_a, sol_b, *rest):
@@ -658,7 +678,7 @@
     return pl.pallas_call(
         functools.partial(middle_kernel, planes),
         out_shape=same(state) + same(state[:3]),
-        in_specs=[HBM] + [VMEM] * 10,
+        in_specs=[VMEM] * 11,
         out_specs=(VMEM,) * 9,
         scratch_shapes=FETCHED,
         input_output_aliases={5 + k: k for k in range(6)},
@@ -672,7 +692,7 @@
     out = pl.pallas_call(
         functools.partial(late_kernel, shape[0]),
         out_shape=(array(*shape), array(*shape)) + same(state),
-        in_specs=[HBM] + [VMEM] * 14,
+        in_specs=[VMEM] * 15,
         out_specs=(VMEM,) * 11,
         scratch_shapes=FETCHED,
         input_output_aliases={6 + k: 2 + k for k in range(9)},
@@ -727,10 +747,11 @@
     cross = pack_rows(planes, cross, side)
     rowid = row_of(cross.shape)
     cross = swap_edges(cross, "cross", (rowid < HALF - 1) | (rowid == HALF))
+    shift_step = carry(shift_step)
     rim_a, rim_b = pack_rims(planes, cross, side)
     rim_a = lax.ppermute(rim_a, both, even_down)
     rim_b = lax.ppermute(rim_b, both, even_up)
-    tops = lax.ppermute(tops, "grow", ring(size, -1))
+    tops = lax.ppermute(tops, "grow", chain(size, -1))
     state = early(phi, sol, side, cross)
     state = middle(planes, shift_step, (phi_a, phi_b, sol_a, sol_b), state)
     outs, state = late(shift_step, side, cross, rim_a, rim_b, seed, state, phi.shape)

time: 25.2 us -> 25 us (level)
  starting transfers between devices: 13.1 us -> 11.4 us
  waiting for transfers between devices: 2.73 us -> 4.35 us
    ppermute x1, starting transfers between devices: 3.52 us -> 1.28 us  [steps(): tops = lax.ppermute(tops, 'grow', chain(size, -1))]
    ppermute x1, waiting for transfers between devices: 0.86 us -> 2.48 us  [steps(): phi_a = lax.ppermute(phi_a, both, even_down)]
    ppermute x1, starting transfers between devices: 0.01 us -> 0.62 us  [steps(): rim_a = lax.ppermute(rim_a, both, even_down)]
where the time goes in v6:
time: 25 us; the launch traced here: 24.9 us
  starting transfers between devices  11.4 us (46%)
  Pallas kernels  7.71 us (31%)
  waiting for transfers between devices  4.35 us (17%)
  between operations  1.4 us (6%)
    pallas_call x1, Pallas kernels, late(): pl.pallas_call(functools.partial(late_kernel, shape[0]), out_shape=(array...  3.17 us
    ppermute x1, starting transfers between devices, steps(): sol_b = lax.ppermute(sol_b, both, even_up)  2.59 us
    ppermute x1, waiting for transfers between devices, steps(): phi_a = lax.ppermute(phi_a, both, even_down)  2.48 us
    ppermute x1, starting transfers between devices, steps(): rim_b = lax.ppermute(rim_b, both, even_up)  2.36 us
    ppermute x2, starting transfers between devices, swap_edges(): return lax.ppermute(message, axis, ring(size, 1))  2.34 us
    ppermute x1, starting transfers between devices, steps(): phi_b = lax.ppermute(phi_b, both, even_up)  2 us
    ppermute x2, waiting for transfers between devices, swap_edges(): return lax.ppermute(message, axis, ring(size, 1))  1.85 us
    pallas_call x1, Pallas kernels, final(): pl.pallas_call(functools.partial(final_kernel, planes), out_shape=(array(...  1.41 us
  transfers between devices with their start and end apart: 9, of which 2 were waited for; matrix products, arithmetic and copies ran while one was open for 0% of the time, Pallas kernels for 21%

profile of v6, /device:TPU:0, one launch (start us, length us, event | category | flops | bytes accessed | tf_op | source)
XLA Modules:
  0.0 24.9 jit_solution(17246115566312568410)
XLA Ops:
  0.6 1.1 %pack_edges.1 = (f32[9,32,128]{2,1,0:T(8,128)S(1)}, f32[7,8,512]{2,1,0:T(8,128)S(1)}, f32[3,32,512]{2,1,0:T(8,128)S(1)}, f32[4,32,512]{2,1,0:T(8,128)S(1)}, f32[4,32,512]{2,1,0:T(8,128)S(1)}) custom-call(f32[4,32,512]{2,1,0:T(8,128)} %phi_in.1, f32[4,32,512]{2,1,0:T(8,128)} %sol_in.1, s32[32,512]{1,0:T(8,128)} %levels.1), custom_call_target="tpu_custom_call" | custom-call | flops 65536 | bytes 262144 | tf_op jit(solution)/shard_map/pack_edges/pallas_call | solution.py:185
  1.7 0.6 %collective-permute-start.2 = (f32[9,32,128]{2,1,0:T(8,128)S(1)}, f32[9,32,128]{2,1,0:T(8,128)S(1)}, u32[]{:S(2)}, u32[]{:S(2)}) collective-permute-start(f32[9,32,128]{2,1,0:T(8,128)S(1)} %get-tuple-element.43), channel_id=1, source_target_pairs={{0,1},{1,0},{2,3},{3,2},{4,5},{5,4},{6,7},{7,6},{8,9},{9,8},{10,11... | collective-permute-start | bytes 442376 | tf_op jit(solution)/shard_map/ppermute | solution.py:729
  2.3 0.0 collective-permute-start.1
  2.3 2.6 %collective-permute-start.8 = (f32[3,32,512]{2,1,0:T(8,128)S(1)}, f32[3,32,512]{2,1,0:T(8,128)S(1)}, u32[]{:S(2)}, u32[]{:S(2)}) collective-permute-start(f32[3,32,512]{2,1,0:T(8,128)S(1)} %get-tuple-element.49), channel_id=1, source_target_pairs={{0,4},{1,0},{4,8},{5,1},{8,12},{9,5},{12,13},{13,9},{2,6},{3,2},{6... | collective-permute-start | bytes 589832 | tf_op jit(solution)/shard_map/ppermute | solution.py:742
  5.0 0.2 collective-permute-start.6
  5.2 0.0 collective-permute-done.2.side
  5.2 0.1 pack_rows.1
  5.2 1.8 %collective-permute-start.3 = (f32[29,8,128]{2,1,0:T(8,128)S(1)}, f32[29,8,128]{2,1,0:T(8,128)S(1)}, u32[]{:S(2)}, u32[]{:S(2)}) collective-permute-start(f32[29,8,128]{2,1,0:T(8,128)S(1)} %pack_rows.1), channel_id=1, source_target_pairs={{0,2},{2,0},{1,3},{3,1},{4,6},{6,4},{5,7},{7,5},{8,10},{10,8},{9,1... | collective-permute-start | bytes 356360 | tf_op jit(solution)/shard_map/ppermute | solution.py:729
  7.0 2.0 %collective-permute-start.7 = (f32[3,32,512]{2,1,0:T(8,128)S(1)}, f32[3,32,512]{2,1,0:T(8,128)S(1)}, u32[]{:S(2)}, u32[]{:S(2)}) collective-permute-start(f32[3,32,512]{2,1,0:T(8,128)S(1)} %get-tuple-element.48), channel_id=1, source_target_pairs={{0,4},{1,0},{4,8},{5,1},{8,12},{9,5},{12,13},{13,9},{2,6},{3,2},{6... | collective-permute-start | bytes 589832 | tf_op jit(solution)/shard_map/ppermute | solution.py:745
  9.0 1.9 %collective-permute-done.3.cross = f32[29,8,128]{2,1,0:T(8,128)S(1)} collective-permute-done((f32[29,8,128]{2,1,0:T(8,128)S(1)}, f32[29,8,128]{2,1,0:T(8,128)S(1)}, u32[]{:S(2)}, u32[]{:S(2)}) %collective-permute-start.3) | collective-permute-done | bytes 118816 | tf_op jit(solution)/shard_map/ppermute | solution.py:729
  10.9 1.3 %collective-permute-start = (f32[2,32,512]{2,1,0:T(8,128)S(1)}, f32[2,32,512]{2,1,0:T(8,128)S(1)}, u32[]{:S(2)}, u32[]{:S(2)}) collective-permute-start(f32[2,32,512]{2,1,0:T(8,128)S(1)} %get-tuple-element.42), channel_id=1, source_target_pairs={{4,0},{8,4},{12,8},{5,1},{9,5},{13,9},{6,2},{10,6},{14,10},{7,3},{... | collective-permute-start | bytes 393224 | tf_op jit(solution)/shard_map/ppermute | solution.py:754
  12.2 0.2 pack_rims.1
  12.3 0.0 collective-permute-done.8.sol_b
  12.3 0.6 %collective-permute-start.4 = (f32[120,128]{1,0:T(8,128)S(1)}, f32[120,128]{1,0:T(8,128)S(1)}, u32[]{:S(2)}, u32[]{:S(2)}) collective-permute-start(f32[120,128]{1,0:T(8,128)S(1)} %get-tuple-element.45), channel_id=1, source_target_pairs={{0,1},{1,5},{4,0},{5,9},{8,4},{9,13},{12,8},{13,12},{2,3},{3,7},{6... | collective-permute-start | bytes 184328 | tf_op jit(solution)/shard_map/ppermute | solution.py:752
  13.0 2.5 %collective-permute-done.6.phi_a = f32[3,32,512]{2,1,0:T(8,128)S(1)} collective-permute-done((f32[3,32,512]{2,1,0:T(8,128)S(1)}, f32[3,32,512]{2,1,0:T(8,128)S(1)}, u32[]{:S(2)}, u32[]{:S(2)}) %collective-permute-start.6) | collective-permute-done | bytes 196640 | tf_op jit(solution)/shard_map/ppermute | solution.py:744
  15.4 2.4 %collective-permute-start.5 = (f32[120,128]{1,0:T(8,128)S(1)}, f32[120,128]{1,0:T(8,128)S(1)}, u32[]{:S(2)}, u32[]{:S(2)}) collective-permute-start(f32[120,128]{1,0:T(8,128)S(1)} %get-tuple-element.46), channel_id=1, source_target_pairs={{0,4},{1,0},{4,8},{5,1},{8,12},{9,5},{12,13},{13,9},{2,6},{3,2},{6... | collective-permute-start | bytes 184328 | tf_op jit(solution)/shard_map/ppermute | solution.py:753
  18.5 0.7 %early.1 = (f32[10,5,48,128]{3,2,1,0:T(8,128)S(1)}, f32[10,5,48,128]{3,2,1,0:T(8,128)S(1)}, f32[10,5,48,128]{3,2,1,0:T(8,128)S(1)}, f32[10,5,48,128]{3,2,1,0:T(8...) custom-call(f32[4,32,512]{2,1,0:T(8,128)S(1)} %get-tuple-element.40.phi, ...), custom_call_target="tpu_custom_call" | custom-call | flops 4194304 | bytes 16777216 | tf_op jit(solution)/shard_map/early/pallas_call | solution.py:662
  19.1 0.0 collective-permute-done.7.phi_b
  19.2 0.0 collective-permute-done.1.sol_a
  19.2 0.0 copy-start
  19.2 1.1 %middle.1 = (f32[10,5,48,128]{3,2,1,0:T(8,128)S(1)}, f32[10,5,48,128]{3,2,1,0:T(8,128)S(1)}, f32[10,5,48,128]{3,2,1,0:T(8,128)S(1)}, f32[10,5,48,128]{3,2,1,0:T(...) custom-call(s32[8,128]{1,0:T(8,128)S(1)} %carry.1.shift_ref, ...), custom_call_target="tpu_custom_call", output_to_operand_aliasing={{0}: (5, {}), {1}: (6, {}), {2}: (7, {}), {3}: (8, {}), {4}... | custom-call | flops 3145728 | bytes 12582912 | tf_op jit(solution)/shard_map/middle/pallas_call | solution.py:678
  20.2 0.0 collective-permute-done.4.rim_a
  20.2 0.0 collective-permute-done.5.rim_b
  20.3 0.0 copy-done
  20.3 3.2 %late.1 = (f32[4,32,512]{2,1,0:T(8,128)S(1)}, f32[4,32,512]{2,1,0:T(8,128)S(1)}, f32[10,5,48,128]{3,2,1,0:T(8,128)S(1)}, f32[10,5,48,128]{3,2,1,0:T(8,128)S(1)},...) custom-call(s32[8,128]{1,0:T(8,128)S(1)} %carry.1.shift_ref, ...), custom_call_target="tpu_custom_call", output_to_operand_aliasing={{2}: (6, {}), {3}: (7, {}), {4}: (8, {}), {5}: (9, {}), {6}... | custom-call | flops 58982400 | bytes 235929600 | tf_op jit(solution)/shard_map/late/pallas_call | solution.py:692
  23.5 0.0 collective-permute-done.tops
  23.5 1.4 %final.1 = (f32[4,32,512]{2,1,0:T(8,128)}, f32[4,32,512]{2,1,0:T(8,128)}, f32[10,5,48,128]{3,2,1,0:T(8,128)S(1)}, f32[10,5,48,128]{3,2,1,0:T(8,128)S(1)}, f32[10...) custom-call(f32[2,32,512]{2,1,0:T(8,128)S(1)} %collective-permute-do, ...), custom_call_target="tpu_custom_call", output_to_operand_aliasing={{2}: (4, {}), {3}: (5, {}), {4}: (6, {}), {5}: (7, {}), {6}... | custom-call | flops 2097152 | bytes 8388608 | tf_op jit(solution)/shard_map/final/pallas_call | solution.py:708
  (2 shorter events, 0.0 us)
Async XLA Ops:
  1.7 3.4 %collective-permute-start.2 = (f32[9,32,128]{2,1,0:T(8,128)S(1)}, f32[9,32,128]{2,1,0:T(8,128)S(1)}, u32[]{:S(2)}, u32[]{:S(2)}) collective-permute-start(f32[9,32,128]{2,1,0:T(8,128)S(1)} %get-tuple-element.43), channel_id=1, source_target_pairs={{0,1},{1,0},{2,3},{3,2},{4,5},{5,4},{6,7},{7,6},{8,9},{9,8},{10,11... | collective-permute-start | bytes 442376 | tf_op jit(solution)/shard_map/ppermute | solution.py:729
  2.3 16.9 %collective-permute-start.1 = (f32[4,32,512]{2,1,0:T(8,128)}, f32[4,32,512]{2,1,0:T(8,128)S(1)}, u32[]{:S(2)}, u32[]{:S(2)}) collective-permute-start(f32[4,32,512]{2,1,0:T(8,128)} %sol_in.1), channel_id=1, source_target_pairs={{0,1},{1,5},{4,0},{5,9},{8,4},{9,13},{12,8},{13,12},{2,3},{3,7},{6... | collective-permute-start | bytes 786440 | tf_op jit(solution)/shard_map/ppermute | solution.py:740
  2.3 10.0 %collective-permute-start.8 = (f32[3,32,512]{2,1,0:T(8,128)S(1)}, f32[3,32,512]{2,1,0:T(8,128)S(1)}, u32[]{:S(2)}, u32[]{:S(2)}) collective-permute-start(f32[3,32,512]{2,1,0:T(8,128)S(1)} %get-tuple-element.49), channel_id=1, source_target_pairs={{0,4},{1,0},{4,8},{5,1},{8,12},{9,5},{12,13},{13,9},{2,6},{3,2},{6... | collective-permute-start | bytes 589832 | tf_op jit(solution)/shard_map/ppermute | solution.py:742
  5.0 10.5 %collective-permute-start.6 = (f32[3,32,512]{2,1,0:T(8,128)S(1)}, f32[3,32,512]{2,1,0:T(8,128)S(1)}, u32[]{:S(2)}, u32[]{:S(2)}) collective-permute-start(f32[3,32,512]{2,1,0:T(8,128)S(1)} %get-tuple-element.47), channel_id=1, source_target_pairs={{0,1},{1,5},{4,0},{5,9},{8,4},{9,13},{12,8},{13,12},{2,3},{3,7},{6... | collective-permute-start | bytes 589832 | tf_op jit(solution)/shard_map/ppermute | solution.py:744
  5.2 5.6 %collective-permute-start.3 = (f32[29,8,128]{2,1,0:T(8,128)S(1)}, f32[29,8,128]{2,1,0:T(8,128)S(1)}, u32[]{:S(2)}, u32[]{:S(2)}) collective-permute-start(f32[29,8,128]{2,1,0:T(8,128)S(1)} %pack_rows.1), channel_id=1, source_target_pairs={{0,2},{2,0},{1,3},{3,1},{4,6},{6,4},{5,7},{7,5},{8,10},{10,8},{9,1... | collective-permute-start | bytes 356360 | tf_op jit(solution)/shard_map/ppermute | solution.py:729
  7.0 12.1 %collective-permute-start.7 = (f32[3,32,512]{2,1,0:T(8,128)S(1)}, f32[3,32,512]{2,1,0:T(8,128)S(1)}, u32[]{:S(2)}, u32[]{:S(2)}) collective-permute-start(f32[3,32,512]{2,1,0:T(8,128)S(1)} %get-tuple-element.48), channel_id=1, source_target_pairs={{0,4},{1,0},{4,8},{5,1},{8,12},{9,5},{12,13},{13,9},{2,6},{3,2},{6... | collective-permute-start | bytes 589832 | tf_op jit(solution)/shard_map/ppermute | solution.py:745
  10.9 12.6 %collective-permute-start = (f32[2,32,512]{2,1,0:T(8,128)S(1)}, f32[2,32,512]{2,1,0:T(8,128)S(1)}, u32[]{:S(2)}, u32[]{:S(2)}) collective-permute-start(f32[2,32,512]{2,1,0:T(8,128)S(1)} %get-tuple-element.42), channel_id=1, source_target_pairs={{4,0},{8,4},{12,8},{5,1},{9,5},{13,9},{6,2},{10,6},{14,10},{7,3},{... | collective-permute-start | bytes 393224 | tf_op jit(solution)/shard_map/ppermute | solution.py:754
  12.3 7.9 %collective-permute-start.4 = (f32[120,128]{1,0:T(8,128)S(1)}, f32[120,128]{1,0:T(8,128)S(1)}, u32[]{:S(2)}, u32[]{:S(2)}) collective-permute-start(f32[120,128]{1,0:T(8,128)S(1)} %get-tuple-element.45), channel_id=1, source_target_pairs={{0,1},{1,5},{4,0},{5,9},{8,4},{9,13},{12,8},{13,12},{2,3},{3,7},{6... | collective-permute-start | bytes 184328 | tf_op jit(solution)/shard_map/ppermute | solution.py:752
  15.4 4.8 %collective-permute-start.5 = (f32[120,128]{1,0:T(8,128)S(1)}, f32[120,128]{1,0:T(8,128)S(1)}, u32[]{:S(2)}, u32[]{:S(2)}) collective-permute-start(f32[120,128]{1,0:T(8,128)S(1)} %get-tuple-element.46), channel_id=1, source_target_pairs={{0,4},{1,0},{4,8},{5,1},{8,12},{9,5},{12,13},{13,9},{2,6},{3,2},{6... | collective-permute-start | bytes 184328 | tf_op jit(solution)/shard_map/ppermute | solution.py:753
  19.2 1.1 %copy-start = (s32[32,512]{1,0:T(8,128)S(1)}, s32[32,512]{1,0:T(8,128)}, u32[]{:S(2)}) copy-start(s32[32,512]{1,0:T(8,128)} %levels.1) | copy-start | bytes 196612
